TPU v7x, 32 devices: a whole 2x2x4 slice. The times are simulated.
32 devices in a mesh: dp: 8 (over z, x), tensor: 4 (over y, core).
Axes of the slice: x: 2, y: 2, z: 4, core: 2. Of those that a mesh axis runs over, the one named last changes fastest.
Arguments:
- tokens: bfloat16 [16, 1024, 2048], P('dp', 'tensor'), may hold values from -6 to 6
- pre_gain: float32 [2048], replicated, may hold values from 0.1 to 1.9
- weight_gate: bfloat16 [2048, 4096], P(None, 'tensor'), may hold values from -0.125 to 0.125
- weight_inner: bfloat16 [2048, 4096], P(None, 'tensor'), may hold values from -0.125 to 0.125
- weight_step: bfloat16 [2048, 64], P(None, 'tensor'), may hold values from -0.0625 to 0.0625
- weight_shared: bfloat16 [2048, 256], replicated, may hold values from -0.125 to 0.125
- conv_kernel: float32 [4, 4096], P(None, 'tensor'), may hold values from -3 to 3
- conv_offset: float32 [4096], P('tensor'), may hold values from -1.8 to 1.8
- shared_kernel: float32 [4, 256], replicated, may hold values from -3 to 3
- shared_offset: float32 [256], replicated, may hold values from -1.8 to 1.8
- step_bias: float32 [64], P('tensor'), may hold values from -7 to -2.3
- log_rate: float32 [64], P('tensor'), may hold values from 0 to 2.77
- skip_gain: float32 [64], P('tensor'), may hold values from 0.5 to 2
- gate_gain: float32 [4096], P('tensor'), may hold values from 0.1 to 1.9
- weight_out: bfloat16 [4096, 2048], P('tensor'), may hold values from -0.09375 to 0.09375
- cotangent: bfloat16 [16, 1024, 2048], P('dp', 'tensor'), may hold values from -6 to 6
- segments: int32 [16, 1024], P('dp'), may hold values from 0 to 7, never falling along the last dimension, each value on 1 to 512 neighbouring positions
- image_span: int32 [16, 2], P('dp'), may hold values from 0 to 4, as said below
Outputs:
- block_out: bfloat16 [16, 1024, 2048], P('dp', 'tensor')
- tokens_grad: bfloat16 [16, 1024, 2048], P('dp', 'tensor')
- pre_gain_grad: float32 [2048], replicated
- weight_gate_grad: float32 [2048, 4096], P(None, 'tensor')
- weight_inner_grad: float32 [2048, 4096], P(None, 'tensor')
- weight_step_grad: float32 [2048, 64], P(None, 'tensor')
- weight_shared_grad: float32 [2048, 256], replicated
- conv_kernel_grad: float32 [4, 4096], P(None, 'tensor')
- conv_offset_grad: float32 [4096], P('tensor')
- shared_kernel_grad: float32 [4, 256], replicated
- shared_offset_grad: float32 [256], replicated
- step_bias_grad: float32 [64], P('tensor')
- log_rate_grad: float32 [64], P('tensor')
- skip_gain_grad: float32 [64], P('tensor')
- gate_gain_grad: float32 [4096], P('tensor')
- weight_out_grad: float32 [4096, 2048], P('tensor')
Inputs may be any that keep to these rules, and one draw needn't show every extreme that they name: `segments`: along a sequence the document ids never fall; a document has 1 to 512 tokens. `image_span`: each row holds (first image piece, number of image pieces); first + number <= 4; a sequence may have no image piece.
All inputs are finite; a program needn't handle non-finite values.
Results may differ from a plain program's by a relative error of at most 0.0087.
Values may be sent and summed in bfloat16 or wider, within the bound.
No kernel may reach another device: no remote copies, remote signals or barrier semaphores. Data moves between devices by JAX's collectives and lax.ppermute only.
A program may use at most 320 MiB of HBM per device.

v0:
```python
from functools import partial

import jax
import jax.numpy as jnp
from jax import lax
from jax.sharding import PartitionSpec as P

STRETCH = 256


EPSILON = 1e-05
HIGHEST = lax.Precision.HIGHEST
CONTRACT_ROWS = (((0,), (0,)), ((), ()))
CONTRACT_COLUMNS = (((1,), (1,)), ((), ()))


def sigmoid_linear(values):
    return values * jax.nn.sigmoid(values)


def causal_conv(signal, kernel, offset):
    length = signal.shape[0]
    tap_count = kernel.shape[0]
    padded = jnp.pad(signal, ((tap_count - 1, 0), (0, 0)))
    summed = offset[None, :] + kernel[0][None, :] * padded[0:length]
    for tap_index in range(1, tap_count):
        summed = summed + kernel[tap_index][None, :] * padded[tap_index : tap_index + length]
    return summed


def piece_flags(span_row, pieces):
    piece_index = jnp.arange(pieces, dtype=jnp.int32)
    inside = (piece_index >= span_row[0]) & (piece_index < span_row[0] + span_row[1])
    return inside.astype(jnp.int32)


def state_scan(inputs_x, step_size, decay_rate, b_matrix, c_matrix, segment, is_image):
    length, head_count, head_width = inputs_x.shape
    pieces = is_image.shape[0]
    block_len = length // pieces
    log_step = (step_size * decay_rate[None, :]).reshape(pieces, block_len, head_count)
    cumulated = jnp.cumsum(jnp.transpose(log_step, (2, 0, 1)), axis=2)
    weighted_x = jnp.transpose(
        (inputs_x * step_size[:, :, None]).reshape(pieces, block_len, head_count, head_width),
        (2, 0, 1, 3),
    )
    b_blocks = b_matrix.reshape(pieces, block_len, -1)
    c_blocks = c_matrix.reshape(pieces, block_len, -1)
    doc_blocks = segment.reshape(pieces, block_len)
    same_doc = doc_blocks[:, :, None] == doc_blocks[:, None, :]
    position = jnp.arange(block_len)
    causal = position[:, None] >= position[None, :]
    allowed = same_doc & (causal[None, :, :] | (is_image[:, None, None] > 0))
    spread = cumulated[:, :, :, None] - cumulated[:, :, None, :]
    decays = jnp.where(allowed[None, :, :, :], jnp.exp(-jnp.abs(spread)), jnp.zeros_like(spread))
    scores = jnp.einsum("ctn,csn->cts", c_blocks, b_blocks, precision=HIGHEST)
    mixing = scores[None, :, :, :] * decays
    within = jnp.einsum("hcts,hcsp->hctp", mixing, weighted_x, precision=HIGHEST)
    last_doc = doc_blocks[:, -1]
    to_end = (doc_blocks == last_doc[:, None]).astype(cumulated.dtype)[None, :, :] * jnp.exp(
        cumulated[:, :, -1:] - cumulated
    )
    fresh_state = jnp.einsum(
        "hcsp,csn->chpn", to_end[:, :, :, None] * weighted_x, b_blocks, precision=HIGHEST
    )
    before_doc = jnp.concatenate([doc_blocks[:1, 0], doc_blocks[:-1, -1]])
    keep_factor = (last_doc == before_doc).astype(cumulated.dtype)[:, None] * jnp.transpose(
        jnp.exp(cumulated[:, :, -1])
    )

    def advance(carry_state, scan_item):
        factor, update = scan_item
        return (factor[:, None, None] * carry_state + update, carry_state)

    start_state = jnp.zeros((head_count, head_width, b_blocks.shape[2]), inputs_x.dtype)
    final_state, entering = lax.scan(advance, start_state, (keep_factor, fresh_state))
    reach_gate = (doc_blocks == before_doc[:, None]).astype(cumulated.dtype)[None, :, :] * jnp.exp(
        cumulated
    )
    carried = (
        jnp.einsum("ctn,chpn->hctp", c_blocks, entering, precision=HIGHEST)
        * reach_gate[:, :, :, None]
    )
    total = jnp.transpose(within + carried, (1, 2, 0, 3))
    return total.reshape(length, head_count, head_width)


def state_mixer(
    segment,
    is_image,
    gate_pre,
    inner_pre,
    step_pre,
    shared_pre,
    conv_kernel,
    conv_offset,
    shared_kernel,
    shared_offset,
    step_bias,
    log_rate,
    skip_gain,
):
    activated = sigmoid_linear(causal_conv(inner_pre, conv_kernel, conv_offset))
    shared = sigmoid_linear(causal_conv(shared_pre, shared_kernel, shared_offset))
    state_width = shared.shape[1] // 2
    head_count = step_bias.shape[0]
    length = inner_pre.shape[0]
    inputs_x = activated.reshape(length, head_count, -1)
    step_size = jax.nn.softplus(step_pre + step_bias[None, :])
    decay_rate = -jnp.exp(log_rate)
    mixed_out = state_scan(
        inputs_x,
        step_size,
        decay_rate,
        shared[:, :state_width],
        shared[:, state_width:],
        segment,
        is_image,
    )
    mixed_out = mixed_out + skip_gain[None, :, None] * inputs_x
    return mixed_out.reshape(length, -1) * sigmoid_linear(gate_pre)


def body(
    tokens,
    pre_gain,
    weight_gate,
    weight_inner,
    weight_step,
    weight_shared,
    conv_kernel,
    conv_offset,
    shared_kernel,
    shared_offset,
    step_bias,
    log_rate,
    skip_gain,
    gate_gain,
    weight_out,
    cotangent,
    segments,
    image_span,
):
    micro_count = tokens.shape[0]
    row_count = tokens.shape[1]
    model_width = tokens.shape[2]
    inner_width = weight_gate.shape[1] * lax.axis_size("tensor")
    pieces = segments.shape[1] // STRETCH
    rank_start = lax.axis_index("tensor") * row_count
    running = [
        jnp.zeros(parameter.shape, jnp.float32)
        for parameter in (
            pre_gain,
            weight_gate,
            weight_inner,
            weight_step,
            weight_shared,
            conv_kernel,
            conv_offset,
            shared_kernel,
            shared_offset,
            step_bias,
            log_rate,
            skip_gain,
            gate_gain,
            weight_out,
        )
    ]
    outputs = []
    input_grads = []
    for micro_index in range(micro_count):
        own_rows = tokens[micro_index].astype(jnp.float32)
        row_scale = lax.rsqrt(jnp.mean(own_rows * own_rows, axis=1, keepdims=True) + EPSILON)
        normed_rows = (own_rows * row_scale * pre_gain[None, :]).astype(jnp.bfloat16)
        normed_in = lax.all_gather(normed_rows, "tensor", axis=0, tiled=True)
        gate_pre = jnp.dot(normed_in, weight_gate, preferred_element_type=jnp.float32)
        inner_pre = jnp.dot(normed_in, weight_inner, preferred_element_type=jnp.float32)
        step_pre = jnp.dot(normed_in, weight_step, preferred_element_type=jnp.float32)
        shared_pre = jnp.dot(normed_in, weight_shared, preferred_element_type=jnp.float32)
        is_image = piece_flags(image_span[micro_index], pieces)
        gated_out, mixer_pullback = jax.vjp(
            partial(state_mixer, segments[micro_index], is_image),
            gate_pre,
            inner_pre,
            step_pre,
            shared_pre,
            conv_kernel,
            conv_offset,
            shared_kernel,
            shared_offset,
            step_bias,
            log_rate,
            skip_gain,
        )
        square_sum = lax.psum(jnp.sum(gated_out * gated_out, axis=1), "tensor")
        gate_scale = lax.rsqrt(square_sum / inner_width + EPSILON)[:, None]
        normed_out = (gated_out * gate_scale * gate_gain[None, :]).astype(jnp.bfloat16)
        mixed_rows = lax.psum_scatter(
            jnp.dot(normed_out, weight_out, preferred_element_type=jnp.float32),
            "tensor",
            scatter_dimension=0,
            tiled=True,
        )
        outputs.append((own_rows + mixed_rows).astype(jnp.bfloat16))
        cot_rows = cotangent[micro_index]
        cot_full = lax.all_gather(cot_rows, "tensor", axis=0, tiled=True)
        normed_grad = lax.dot_general(
            cot_full, weight_out, CONTRACT_COLUMNS, preferred_element_type=jnp.float32
        )
        running[13] = running[13] + lax.dot_general(
            normed_out, cot_full, CONTRACT_ROWS, preferred_element_type=jnp.float32
        )
        running[12] = running[12] + jnp.sum(normed_grad * gated_out * gate_scale, axis=0)
        scaled_grad = normed_grad * gate_gain[None, :]
        coupling = lax.psum(jnp.sum(scaled_grad * gated_out, axis=1), "tensor")
        cubed_scale = gate_scale * gate_scale * gate_scale
        gated_grad = (
            gate_scale * scaled_grad - cubed_scale / inner_width * gated_out * coupling[:, None]
        )
        pieces_grad = mixer_pullback(gated_grad)
        for slot_index in range(4, 11):
            running[slot_index + 1] = running[slot_index + 1] + pieces_grad[slot_index]
        shared_full = lax.psum(pieces_grad[3], "tensor")
        gate_low = pieces_grad[0].astype(jnp.bfloat16)
        inner_low = pieces_grad[1].astype(jnp.bfloat16)
        step_low = pieces_grad[2].astype(jnp.bfloat16)
        shared_low = shared_full.astype(jnp.bfloat16)
        running[1] = running[1] + lax.dot_general(
            normed_in, gate_low, CONTRACT_ROWS, preferred_element_type=jnp.float32
        )
        running[2] = running[2] + lax.dot_general(
            normed_in, inner_low, CONTRACT_ROWS, preferred_element_type=jnp.float32
        )
        running[3] = running[3] + lax.dot_general(
            normed_in, step_low, CONTRACT_ROWS, preferred_element_type=jnp.float32
        )
        running[4] = running[4] + lax.dot_general(
            normed_in, shared_low, CONTRACT_ROWS, preferred_element_type=jnp.float32
        )
        summed = lax.dot_general(
            gate_low, weight_gate, CONTRACT_COLUMNS, preferred_element_type=jnp.float32
        )
        summed = summed + lax.dot_general(
            inner_low, weight_inner, CONTRACT_COLUMNS, preferred_element_type=jnp.float32
        )
        input_part = lax.psum_scatter(
            summed
            + lax.dot_general(
                step_low, weight_step, CONTRACT_COLUMNS, preferred_element_type=jnp.float32
            ),
            "tensor",
            scatter_dimension=0,
            tiled=True,
        )
        shared_rows = lax.dynamic_slice_in_dim(shared_low, rank_start, row_count, 0)
        normed_in_grad = input_part + lax.dot_general(
            shared_rows, weight_shared, CONTRACT_COLUMNS, preferred_element_type=jnp.float32
        )
        weighted_grad = normed_in_grad * pre_gain[None, :]
        projection = jnp.sum(weighted_grad * own_rows, axis=1, keepdims=True)
        cubed_row = row_scale * row_scale * row_scale
        own_grad = row_scale * weighted_grad - cubed_row / model_width * own_rows * projection
        running[0] = running[0] + jnp.sum(normed_in_grad * own_rows * row_scale, axis=0)
        input_grads.append((cot_rows.astype(jnp.float32) + own_grad).astype(jnp.bfloat16))
    reduced = lax.psum(
        (
            running[1],
            running[2],
            running[3],
            running[4],
            running[5],
            running[6],
            running[9],
            running[10],
            running[11],
            running[12],
            running[13],
        ),
        "dp",
    )
    (
        grad_gate,
        grad_inner,
        grad_step,
        grad_shared,
        grad_kernel,
        grad_offset,
        grad_bias,
        grad_rate,
        grad_skip,
        grad_gain,
        grad_out,
    ) = reduced
    shared_sums = lax.psum((running[0], running[7], running[8]), ("dp", "tensor"))
    return (
        jnp.stack(outputs),
        jnp.stack(input_grads),
        shared_sums[0],
        grad_gate,
        grad_inner,
        grad_step,
        grad_shared,
        grad_kernel,
        grad_offset,
        shared_sums[1],
        shared_sums[2],
        grad_bias,
        grad_rate,
        grad_skip,
        grad_gain,
        grad_out,
    )


def solution(mesh):
    placed = (
        P("dp", "tensor", None),
        P(),
        P(None, "tensor"),
        P(None, "tensor"),
        P(None, "tensor"),
        P(),
        P(None, "tensor"),
        P("tensor"),
        P(),
        P(),
        P("tensor"),
        P("tensor"),
        P("tensor"),
        P("tensor"),
        P("tensor", None),
        P("dp", "tensor", None),
        P("dp", None),
        P("dp", None),
    )
    return jax.shard_map(
        body,
        mesh=mesh,
        in_specs=placed,
        out_specs=(
            P("dp", "tensor", None),
            P("dp", "tensor", None),
            P(),
            P(None, "tensor"),
            P(None, "tensor"),
            P(None, "tensor"),
            P(),
            P(None, "tensor"),
            P("tensor"),
            P(),
            P(),
            P("tensor"),
            P("tensor"),
            P("tensor"),
            P("tensor"),
            P("tensor", None),
        ),
        check_vma=False,
    )
```

profile of v0, /device:TPU:0, one launch (start us, length us, event | category | flops | bytes accessed | tf_op | source)
XLA Modules:
  0.0 1913.7 jit_solution(8220009131876546524)
XLA Ops:
  28.7 22.6 %all-gather.9.cloned.1.call-done = bf16[1024,2048]{1,0:T(8,128)(2,1)} async-done(((bf16[256,2048]{1,0:T(8,128)(2,1)}), bf16[1024,2048]{1,0:T(8,128)(2,1)}) %all-gather.9.cloned.1.call-update) | async-done | bytes 4194320 | tf_op jit(solution)/shard_map/all_gather | solution.py:175
  58.2 29.8 %all-gather.7.cloned.1.call-done = bf16[1024,2048]{1,0:T(8,128)(2,1)} async-done(((bf16[256,2048]{1,0:T(8,128)(2,1)}), bf16[1024,2048]{1,0:T(8,128)(2,1)}) %all-gather.7.cloned.1.call-update) | async-done | bytes 4194320 | tf_op jit(solution)/shard_map/all_gather | solution.py:175
  121.1 19.4 %fusion.71 = (f32[1024,1024]{1,0:T(8,128)}, f32[1024,1024]{1,0:T(8,128)}, f32[1024,1024]{1,0:T(8,128)}, f32[1024,1024]{1,0:T(8,128)}) fusion(f32[1024,1024]{1,0:T(8,128)} %fusion.234, f32[1024]{0:T(1024)S(1)} %bitcast.580, f32[1024]{0:T(1024)S(1)} %bitcast.582, f32[1024]{0:T(1024)S(1)} %bitcast.578, f32[1024]{0:T(1024)S(1)} %bitcast.576, ...), kind=kLoop, calls=%fused_computation.158 | loop fusion | flops 25165824 | bytes 25186304 | tf_op jit(solution)/shard_map/jvp()/mul | solution.py:18
  180.1 17.4 copy.550
  225.7 22.0 %fusion.67 = f32[4,256,16,64]{1,3,0,2:T(8,128)} fusion(f32[4,16,64,256]{3,2,1,0:T(8,128)S(1)} %fusion.235, f32[4,256,16]{1,0,2:T(4,128)S(1)} %copy-done.112, f32[16,4,256]{2,1,0:T(4,128)S(1)} %copy.533, f32[4,256,256]{2,1,0:T(8,128)S(1)} %fusion.233, pred[4,256,256]{2,1,0:T(8,128)(4,1)S(1)} %copy-done.99, f32[4,256,16,64]{1,3,2,0:T(8,128)S(1)} %copy-done.5, ...), kind=kOutput, calls=%fused_computation.123 | convolution fusion | flops 3245342720 | bytes 14090240 | tf_op jit(solution)/shard_map/jvp(hcts,hcsp->hctp)/dot_general | solution.py:58
  247.8 21.6 %fusion.66 = f32[4,256,16,64]{1,3,0,2:T(8,128)} fusion(f32[4,16,64,256]{3,2,1,0:T(8,128)S(1)} %fusion.239, f32[4,256,16]{1,0,2:T(4,128)S(1)} %copy-done.111, f32[16,4,256]{2,1,0:T(4,128)S(1)} %copy.546, f32[4,256,256]{2,1,0:T(8,128)S(1)} %fusion.237, pred[4,256,256]{2,1,0:T(8,128)(4,1)S(1)} %copy-done.97, f32[4,256,16,64]{1,3,2,0:T(8,128)S(1)} %copy-done.7, ...), kind=kOutput, calls=%fused_computation.121 | convolution fusion | flops 3245342720 | bytes 14090240 | tf_op jit(solution)/shard_map/jvp(hcts,hcsp->hctp)/dot_general | solution.py:58
  311.7 10.1 fusion.240
  321.8 16.5 multiply_reduce_fusion.17
  344.4 9.9 fusion.54
  354.4 13.7 multiply_reduce_fusion.1
  373.9 20.4 %multiply_reduce_fusion.2 = (f32[1024]{0:T(1024)}, f32[1024,1024]{1,0:T(8,128)}, bf16[1024,1024]{1,0:T(8,128)(2,1)}, bf16[1024,1024]{1,0:T(8,128)(2,1)}, f32[1024]{0:T(1024)}, /*index=5*/f32[1024,1024]{1,0:T(8,128)}) fusion(f32[1024,1024]{1,0:T(8,128)} %get-tuple-element.659, f32[1024,1024]{1,0:T(8,128)} %fusion.240, f32[1024]{0:T(1024)S(1)} %get-tuple-element.580, ...), kind=kLoop, calls=%fused_computation.126 | loop fusion | flops 54523904 | bytes 54566912 | tf_op jit(solution)/shard_map/transpose(jvp())/reduce_sum | solution.py:120
  411.3 32.3 %fusion.170 = (f32[16,4,256]{2,1,0:T(4,128)}, f32[16,4,256]{2,1,0:T(4,128)}, f32[4,256,256]{2,1,0:T(8,128)}, f32[16,4,256,256]{3,2,1,0:T(8,128)}) fusion(f32[4,256,256]{2,1,0:T(8,128)S(1)} %copy-done.82, pred[4,256,256]{2,1,0:T(8,128)(4,1)S(1)} %copy-done.99, f32[16,4,256]{2,1,0:T(4,128)S(1)} %copy.533, f32[4,256,16,64]{1,0,3,2:T(4,128)S(1)} %copy-done.3, ...), kind=kOutput, calls=%fused_computation.301 | convolution fusion | flops 3297476608 | bytes 27787264 | tf_op jit(solution)/shard_map/transpose(jvp(hcts,hcsp->hctp))/dot_general | solution.py:58
  460.6 32.7 %fusion.172 = (f32[16,4,256]{2,1,0:T(4,128)S(1)}, f32[16,4,256]{2,1,0:T(4,128)S(1)}, f32[4,256,256]{2,1,0:T(8,128)}, f32[16,4,256,256]{3,2,1,0:T(8,128)}) fusion(f32[4,256,256]{2,1,0:T(8,128)S(1)} %copy-done.80, pred[4,256,256]{2,1,0:T(8,128)(4,1)S(1)} %copy-done.98, f32[16,4,256]{2,1,0:T(4,128)S(1)} %copy-done.110, f32[4,256,16,64]{1,0,3,2:T(4,128)S(1)} %copy-done.1, ...), kind=kOutput, calls=%fused_computation.303 | convolution fusion | flops 3297476608 | bytes 27787264 | tf_op jit(solution)/shard_map/transpose(jvp(hcts,hcsp->hctp))/dot_general | solution.py:58
  518.4 11.9 while.71
  549.0 12.0 while.70
  570.2 10.8 fusion.243
  581.1 9.9 reduce-window.34
  591.3 18.0 bitcast_add_fusion.5
  630.0 9.9 reduce-window.36
  640.1 17.9 bitcast_add_fusion.4
  678.5 24.3 %multiply_reduce_fusion.11 = (f32[1024]{0:T(1024)}, f32[1024]{0:T(1024)}, f32[1024]{0:T(1024)}, f32[1024]{0:T(1024)}, f32[1024]{0:T(1024)}, /*index=5*/f32[1024,...) fusion(f32[1024,1024]{1,0:T(8,128)} %fusion.234, ...), kind=kLoop, calls=%fused_computation.135 | loop fusion | flops 44029952 | bytes 50376704 | tf_op jit(solution)/shard_map/transpose(jvp())/reduce_sum | solution.py:27
  702.9 10.5 broadcast_multiply_fusion
  762.6 11.8 fusion.208
  775.0 11.5 fusion.209
  787.4 9.8 fusion.151
  833.7 76.4 %all-reduce.54 = (bf16[1024,256]{1,0:T(8,128)(2,1)}, bf16[1024,256]{1,0:T(8,128)(2,1)}) all-reduce(f32[1024,256]{1,0:T(8,128)S(1)} %pad_add_fusion.6, f32[1024,256]{1,0:T(8,128)S(1)} %pad_add_fusion.9), channel_id=1, replica_groups=mesh['dp'=8,'tensor'=4] {'tensor'}, use_global_device_ids=true, to_apply=%region_48.50 | all-reduce | flops 524288 | bytes 3145728 | tf_op jit(solution)/shard_map/psum | solution.py:223
  936.7 9.6 convolution_add_fusion.1
  946.3 9.2 convolution_add_fusion
  964.2 37.8 %all-reduce.45 = (f32[4,1024]{1,0:T(4,128)}, f32[1024]{0:T(1024)}, f32[16]{0:T(128)}, f32[16]{0:T(128)}, f32[16]{0:T(128)}, /*index=5*/f32[1024]{0:T(1024)}) all-reduce(f32[4,1024]{1,0:T(4,128)S(1)} %add_add_fusion.2, f32[1024]{0:T(1024)S(1)} %add.459, f32[16]{0:T(128)S(1)} %add.462, ...), channel_id=1, replica_groups=mesh['dp'=8,'tensor'=4] {'dp'}, use_global_device_ids=true, to_apply=%region_65.67 | all-reduce | flops 6192 | bytes 49536 | tf_op jit(solution)/shard_map/psum | solution.py:265
  1011.6 37.5 %all-reduce.44 = (f32[2048]{0:T(1024)}, f32[4,256]{1,0:T(4,128)}, f32[256]{0:T(256)}) all-reduce(f32[2048]{0:T(1024)S(1)} %add.453, f32[4,256]{1,0:T(4,128)S(1)} %add_add_fusion.3, f32[256]{0:T(256)S(1)} %add.461), channel_id=1, replica_groups=mesh['dp'=8,'tensor'=4] {'dp','tensor'}, use_global_device_ids=true, to_apply=%region_52.54 | all-reduce | flops 3328 | bytes 26624 | tf_op jit(solution)/shard_map/psum | solution.py:294
  1049.1 20.9 %reduce-scatter.7.cloned.1.call-done = f32[256,2048]{1,0:T(8,128)} async-done(((f32[1024,2048]{1,0:T(8,128)}), f32[256,2048]{1,0:T(8,128)}) %reduce-scatter.7.cloned.1.call-update) | async-done | bytes 2097168 | tf_op jit(solution)/shard_map/reduce_scatter | solution.py:198
  1078.0 810.2 %all-reduce.53.cloned.1.call-done = (f32[2048,1024]{1,0:T(8,128)}, f32[2048,1024]{1,0:T(8,128)}, f32[2048,16]{0,1:T(8,128)}, f32[2048,256]{1,0:T(8,128)}, f32[1024,2048]{1,0:T(8,128)}) async-done(((f32[2048,1024]{1,0:T(8,128)}, f32[2048,1024]{1,0:T(8,128)}, f32[2048,16]{0,1:T(8,128)}, f32[2048,256]{1,0:T(8,128)}, f32[1024,2048]{1,0:T(8,128)}), (f32[2048,1024]{1,0:T(8,128)}, f32[2048,1024]{1,0:T(8,128)}, ...) | async-done | bytes 27394064 | tf_op jit(solution)/shard_map/psum | solution.py:265
  (665 shorter events, 505.3 us)
Async XLA Ops:
  7.2 91.8 %copy-start = (bf16[2048,256]{1,0:T(8,128)(2,1)S(1)}, bf16[2048,256]{1,0:T(8,128)(2,1)}, u32[]{:S(2)}) copy-start(bf16[2048,256]{1,0:T(8,128)(2,1)} %param.32) | copy-start | bytes 3145732
  7.2 44.2 %all-gather.9.cloned.1.call-start = ((), (), s32[]{:S(2)}) async-start(), calls=%async_computation.6 | async-start | bytes 5242880 | tf_op jit(solution)/shard_map/all_gather | solution.py:175
  14.1 74.0 %all-gather.7.cloned.1.call-start = ((), (), s32[]{:S(2)}) async-start(), calls=%async_computation.4 | async-start | bytes 5242880 | tf_op jit(solution)/shard_map/all_gather | solution.py:175
  14.8 329.6 %all-gather.13.cloned.1.call-start = ((), (), s32[]{:S(2)}) async-start(), calls=%async_computation.11 | async-start | bytes 5242880 | tf_op jit(solution)/shard_map/all_gather | solution.py:206
  16.4 338.0 %all-gather.11.cloned.1.call-start = ((), (), s32[]{:S(2)}) async-start(), calls=%async_computation.10 | async-start | bytes 5242880 | tf_op jit(solution)/shard_map/all_gather | solution.py:206
  17.0 985.1 %reduce-scatter.11.cloned.1.call-start = ((), (), s32[]{:S(2)}) async-start(), calls=%async_computation.9 | async-start | bytes 10485760 | tf_op jit(solution)/shard_map/reduce_scatter | solution.py:246
  18.8 73.2 %copy-start.150 = (f32[16]{0:T(128)}, f32[16]{0:T(128)S(1)}, u32[]{:S(2)}) copy-start(f32[16]{0:T(128)S(1)} %exponential_negate_fusion) | copy-start | bytes 196
  19.4 84.4 %copy-start.152 = (f32[1,256]{1,0:T(1,128)}, f32[1,256]{1,0:T(1,128)S(1)}, u32[]{:S(2)}) copy-start(f32[1,256]{1,0:T(1,128)S(1)} %get-tuple-element.699) | copy-start | bytes 3076
  19.4 84.4 %copy-start.154 = (f32[1,256]{1,0:T(1,128)}, f32[1,256]{1,0:T(1,128)S(1)}, u32[]{:S(2)}) copy-start(f32[1,256]{1,0:T(1,128)S(1)} %get-tuple-element.700) | copy-start | bytes 3076
  19.5 84.4 %copy-start.156 = (f32[1,256]{1,0:T(1,128)}, f32[1,256]{1,0:T(1,128)S(1)}, u32[]{:S(2)}) copy-start(f32[1,256]{1,0:T(1,128)S(1)} %get-tuple-element.701) | copy-start | bytes 3076
  19.5 84.4 %copy-start.158 = (f32[1,256]{1,0:T(1,128)}, f32[1,256]{1,0:T(1,128)S(1)}, u32[]{:S(2)}) copy-start(f32[1,256]{1,0:T(1,128)S(1)} %get-tuple-element.702) | copy-start | bytes 3076
  19.6 354.2 %copy-start.119 = (f32[1024]{0:T(1024)}, f32[1024]{0:T(1024)S(1)}, u32[]{:S(2)}) copy-start(f32[1024]{0:T(1024)S(1)} %mul.1247) | copy-start | bytes 12292
  20.2 100.9 %copy-start.121 = (f32[1,1024]{1,0:T(1,128)}, f32[1,1024]{1,0:T(1,128)S(1)}, u32[]{:S(2)}) copy-start(f32[1,1024]{1,0:T(1,128)S(1)} %get-tuple-element.664) | copy-start | bytes 12292
  20.2 100.9 %copy-start.123 = (f32[1,1024]{1,0:T(1,128)}, f32[1,1024]{1,0:T(1,128)S(1)}, u32[]{:S(2)}) copy-start(f32[1,1024]{1,0:T(1,128)S(1)} %get-tuple-element.665) | copy-start | bytes 12292
  20.2 100.9 %copy-start.125 = (f32[1,1024]{1,0:T(1,128)}, f32[1,1024]{1,0:T(1,128)S(1)}, u32[]{:S(2)}) copy-start(f32[1,1024]{1,0:T(1,128)S(1)} %get-tuple-element.666) | copy-start | bytes 12292
  25.0 69.9 %copy-start.168 = (f32[4]{0:T(128)}, f32[4]{0:T(128)S(1)}, u32[]{:S(2)}) copy-start(f32[4]{0:T(128)S(1)} %convert_reduce_fusion) | copy-start | bytes 52
  26.5 70.4 %copy-start.166 = (f32[4]{0:T(128)}, f32[4]{0:T(128)S(1)}, u32[]{:S(2)}) copy-start(f32[4]{0:T(128)S(1)} %convert_reduce_fusion.1) | copy-start | bytes 52
  27.3 70.3 %copy-start.117 = (f32[4,256]{1,0:T(4,128)}, f32[4,256]{1,0:T(4,128)S(1)}, u32[]{:S(2)}) copy-start(f32[4,256]{1,0:T(4,128)S(1)} %get-tuple-element.692) | copy-start | bytes 12292
  27.4 70.3 %copy-start.131 = (f32[4,256]{1,0:T(4,128)}, f32[4,256]{1,0:T(4,128)S(1)}, u32[]{:S(2)}) copy-start(f32[4,256]{1,0:T(4,128)S(1)} %get-tuple-element.691) | copy-start | bytes 12292
  27.4 68.1 %copy-start.115 = (f32[4,256]{1,0:T(4,128)}, f32[4,256]{1,0:T(4,128)S(1)}, u32[]{:S(2)}) copy-start(f32[4,256]{1,0:T(4,128)S(1)} %get-tuple-element.696) | copy-start | bytes 12292
  27.4 68.1 %copy-start.129 = (f32[4,256]{1,0:T(4,128)}, f32[4,256]{1,0:T(4,128)S(1)}, u32[]{:S(2)}) copy-start(f32[4,256]{1,0:T(4,128)S(1)} %get-tuple-element.695) | copy-start | bytes 12292
  58.2 189.5 %copy-start.109 = (f32[16,4,256]{2,1,0:T(4,128)}, f32[16,4,256]{2,1,0:T(4,128)S(1)}, u32[]{:S(2)}) copy-start(f32[16,4,256]{2,1,0:T(4,128)S(1)} %copy.546) | copy-start | bytes 196612
  94.9 152.8 %copy-start.70 = (f32[2,4,8,256]{3,2,0,1:T(8,128)}, f32[2,4,8,256]{3,2,0,1:T(8,128)S(1)}, u32[]{:S(2)}) copy-start(f32[2,4,8,256]{3,2,0,1:T(8,128)S(1)} %copy.764) | copy-start | bytes 196612
  96.3 101.3 %copy-start.75 = (f32[16,4,256]{2,0,1:T(8,128)}, f32[16,4,256]{2,0,1:T(8,128)S(1)}, u32[]{:S(2)}) copy-start(f32[16,4,256]{2,0,1:T(8,128)S(1)} %get-tuple-element.651) | copy-start | bytes 196612
  96.9 464.2 %copy-start.73 = (f32[2,4,8,256]{3,2,0,1:T(8,128)}, f32[2,4,8,256]{3,2,0,1:T(8,128)S(1)}, u32[]{:S(2)}) copy-start(f32[2,4,8,256]{3,2,0,1:T(8,128)S(1)} %copy.765) | copy-start | bytes 196612
  107.4 107.4 %copy-start.36 = (f32[1024,128]{1,0:T(8,128)}, f32[1024,128]{1,0:T(8,128)S(1)}, u32[]{:S(2)}) copy-start(f32[1024,128]{1,0:T(8,128)S(1)} %get-tuple-element.641) | copy-start | bytes 1572868
  109.1 108.0 %copy-start.33 = (f32[1024,128]{1,0:T(8,128)}, f32[1024,128]{1,0:T(8,128)S(1)}, u32[]{:S(2)}) copy-start(f32[1024,128]{1,0:T(8,128)S(1)} %get-tuple-element.643) | copy-start | bytes 1572868
  739.0 267.1 %reduce-scatter.9.cloned.1.call-start = ((), (), s32[]{:S(2)}) async-start(), calls=%async_computation.8 | async-start | bytes 10485760 | tf_op jit(solution)/shard_map/reduce_scatter | solution.py:246
  761.9 287.2 %reduce-scatter.5.cloned.1.call-start = ((), (), s32[]{:S(2)}) async-start(), calls=%async_computation.5 | async-start | bytes 10485760 | tf_op jit(solution)/shard_map/reduce_scatter | solution.py:198
  774.4 295.6 %reduce-scatter.7.cloned.1.call-start = ((), (), s32[]{:S(2)}) async-start(), calls=%async_computation.7 | async-start | bytes 10485760 | tf_op jit(solution)/shard_map/reduce_scatter | solution.py:198
  786.6 1101.6 %all-reduce.53.cloned.1.call-start = ((), (), s32[]{:S(2)}) async-start(), calls=%async_computation.12 | async-start | bytes 54788096 | tf_op jit(solution)/shard_map/psum | solution.py:265
  1006.1 63.9 %copy-start.172 = (f32[256]{0:T(256)S(1)}, f32[256]{0:T(256)}, u32[]{:S(2)}) copy-start(f32[256]{0:T(256)} %get-tuple-element.724) | copy-start | bytes 3076
  (172 other events, 1829.7 us)
Sparse Core Ops, SparseCore 0:
  14.2 37.1 all-gather.8
  53.5 34.4 all-gather.6
  89.6 34.5 all-gather.12
  125.6 34.5 all-gather.10
  739.1 72.4 reduce-scatter.10
  814.8 104.1 reduce-scatter.8
  921.5 72.5 reduce-scatter.4
  997.5 72.4 reduce-scatter.6
  1075.8 812.2 all-reduce.52
where the time goes:
time: 1930 us; the launch traced here: 1910 us
  waiting for transfers between devices  885 us (46%)
  matrix products  439 us (23%)
  local copies, waits for them, and re-layouts  213 us (11%)
  other arithmetic  193 us (10%)
  blocking collectives  164 us (8%)
  between operations  19.4 us (1%)
    psum x1, waiting for transfers between devices, body(): lax.psum((running[1], running[2], running[3], running[4], running[5], run...  810 us
    dot_general x6, matrix products, state_scan(): jnp.einsum('hcts,hcsp->hctp', mixing, weighted_x, precision=HIGHEST)  145 us
    psum x1, blocking collectives, body(): shared_full = lax.psum(pieces_grad[3], 'tensor')  76.4 us
    all_gather x2, waiting for transfers between devices, body(): normed_in = lax.all_gather(normed_rows, 'tensor', axis=0, tiled=True)  52.4 us
    dot_general x6, matrix products, state_scan(): jnp.einsum('hcsp,csn->chpn', to_end[:, :, :, None] * weighted_x, b_blocks...  49.4 us
    reshape x6, local copies, waits for them, and re-layouts, state_scan(): return total.reshape(length, head_count, head_width)  43 us
    another operation x14, other arithmetic  41.7 us
    reshape x6, local copies, waits for them, and re-layouts, state_scan(): (inputs_x * step_size[:, :, None]).reshape(pieces, block_len, head_count,...  41 us
  transfers between devices with their start and end apart: 9, of which 4 were waited for; matrix products, arithmetic and copies ran while one was open for 23% of the time, Pallas kernels for 0%

commit v1 on v0

v1 whole, which is shorter than its diff:
```python
from functools import partial

import jax
import jax.numpy as jnp
from jax import lax
from jax.experimental import pallas as pl
from jax.experimental.pallas import tpu as pltpu
from jax.sharding import PartitionSpec as P

STRETCH = 256
HEAD = 64
LANES = 128
GROUPS = 2

EPSILON = 1e-05
LOG2E = 1.4426950408889634
BF16 = jnp.bfloat16
F32 = jnp.float32
NN = (((1,), (0,)), ((), ()))
NT = (((1,), (1,)), ((), ()))
TN = (((0,), (0,)), ((), ()))


def mm(left, right, dims=NN):
    return lax.dot_general(left.astype(BF16), right.astype(BF16), dims, preferred_element_type=F32)


def two_parts(values):
    high = values.astype(BF16)
    return high, (values - high.astype(F32)).astype(BF16)


def iota(shape, axis):
    return lax.broadcasted_iota(jnp.int32, shape, axis)


def expand(values, spread):
    high, low = two_parts(values)
    return mm(jnp.concatenate([high, low], axis=1), spread)


def head_sum(values, spread):
    high, low = two_parts(values)
    half = spread[:LANES]
    return mm(high, half, NT) + mm(low, half, NT)


def column_of(row, eye):
    return jnp.sum(jnp.where(eye, row, 0.0), axis=1, keepdims=True)


def shifted_rows(current, before):
    rows = current.shape[0]
    joined = jnp.concatenate([before, current], axis=0)
    return [joined[5 + tap : 5 + tap + rows] for tap in range(4)]


def conv_of(shifted, kernel, offset):
    total = offset + kernel[0:1] * shifted[0]
    for tap in range(1, 4):
        total = total + kernel[tap : tap + 1] * shifted[tap]
    return total


def conv_back(grad, after, kernel):
    rows = grad.shape[0]
    joined = jnp.concatenate([grad, after], axis=0)
    total = kernel[3:4] * grad
    for tap in range(3):
        total = total + kernel[tap : tap + 1] * joined[3 - tap : 3 - tap + rows]
    return total


def piece_context(seg_sm, span_sm, seg_row, step_pre, bias, rate, seq, piece):
    rows = STRETCH
    i0, i1 = iota((rows, rows), 0), iota((rows, rows), 1)
    eye = i0 == i1
    seg_r = seg_row[...]
    seg_c = column_of(seg_r, eye)
    first = span_sm[seq, 0]
    image = jnp.logical_and(piece >= first, piece < first + span_sm[seq, 1])
    reach_all = jnp.where(image, 2 * rows, 0)
    same = seg_c == seg_r
    order = i0 - i1
    allowed = jnp.logical_and(same, order + reach_all >= 0)
    start = piece * rows
    last_doc = seg_sm[seq, start + rows - 1].astype(F32)
    before_doc = seg_sm[seq, jnp.maximum(start - 1, 0)].astype(F32)
    pre = step_pre + bias
    tail = jnp.exp(-jnp.abs(pre))
    step = jnp.maximum(pre, 0.0) + jnp.log1p(tail)
    log_step = step * rate
    high, low = two_parts(log_step)
    lowest = (log_step - high.astype(F32) - low.astype(F32)).astype(BF16)
    ahead = (order >= 0).astype(F32)
    cum = mm(ahead, high) + mm(ahead, low) + mm(ahead, lowest)
    cum = cum * LOG2E
    end = cum[rows - 1 : rows]
    to_end = jnp.where(seg_c == last_doc, jnp.exp2(end - cum), 0.0)
    reach = jnp.where(seg_c == before_doc, jnp.exp2(cum), 0.0)
    keep = jnp.where(last_doc == before_doc, jnp.exp2(end), 0.0)
    return eye, order, reach_all, same, allowed, pre, step, log_step, cum, to_end, reach, keep


def forward_kernel(
    channels, seg_sm, span_sm, pre, ss, seg_row, spread, kernel, offset, skip, shared_kernel,
    shared_offset, bias, rate, y_out, state_out, square_out, before, shared_before, state,
):
    seq, piece = pl.program_id(0), pl.program_id(1)
    group = channels // GROUPS

    @pl.when(piece == 0)
    def _():
        before[...] = jnp.zeros_like(before)
        shared_before[...] = jnp.zeros_like(shared_before)
        state[...] = jnp.zeros_like(state)

    width = shared_kernel.shape[1]
    half = width // 2
    shared_pre = ss[:, :width]
    _, _, _, _, allowed, _, step, _, cum, to_end, reach, keep = piece_context(
        seg_sm, span_sm, seg_row, ss[:, width:], bias[...], rate[...], seq, piece
    )
    conv = conv_of(shifted_rows(shared_pre, shared_before[...]), shared_kernel[...], shared_offset[...])
    shared_before[...] = shared_pre[STRETCH - 8 :]
    act = conv * jax.nn.sigmoid(conv)
    b, c = act[:, :half].astype(BF16), act[:, half:].astype(BF16)
    scores = jnp.where(allowed, mm(c, b, NT), 0.0)
    cum_rows = cum.T
    b_cols = b.T
    lane = iota((STRETCH, LANES), 1)
    squares = jnp.zeros((8, STRETCH), F32)
    ones = jnp.ones((8, group), BF16)
    for g in range(GROUPS):
        cols = slice(g * group, (g + 1) * group)
        gate = pre[:, 2 * g * group : (2 * g + 1) * group].astype(F32)
        inner = pre[:, (2 * g + 1) * group : (2 * g + 2) * group].astype(F32)
        v = conv_of(shifted_rows(inner, before[:, cols]), kernel[:, cols], offset[:, cols])
        before[:, cols] = inner[STRETCH - 8 :]
        x = v * jax.nn.sigmoid(v)
        spread_g = spread[:, cols]
        u = x * expand(step, spread_g)
        entering = state[:, cols]
        state_out[0, 0, :, cols] = entering.astype(BF16)
        carried = mm(c, entering) * expand(reach, spread_g)
        keep_row = expand(jnp.broadcast_to(keep, (8, LANES)), spread_g)[0:1]
        state[:, cols] = keep_row * entering + mm(b_cols, u * expand(to_end, spread_g))
        u_low = u.astype(BF16)
        mixed = []
        for pair in range(group // LANES):
            pair_u = u_low[:, pair * LANES : (pair + 1) * LANES]
            halves = []
            for one in range(2):
                head = g * (group // HEAD) + 2 * pair + one
                gap = cum[:, head : head + 1] - cum_rows[head : head + 1]
                halves.append(mm(scores * jnp.exp2(-jnp.abs(gap)), pair_u))
            mixed.append(jnp.where(lane < HEAD, halves[0], halves[1]))
        y = jnp.concatenate(mixed, axis=1) + carried + skip[:, cols] * x
        y_out[:, cols] = y
        gated = y * (gate * jax.nn.sigmoid(gate))
        squares = squares + mm(ones, gated * gated, NT)
    square_out[...] = squares


def gate_kernel(channels, pre, y, grad, scale_row, gain, low_out, coupling_out, gain_grad):
    group = channels // GROUPS

    @pl.when(pl.program_id(0) == 0)
    def _():
        gain_grad[...] = jnp.zeros_like(gain_grad)

    rows = STRETCH
    eye = iota((rows, rows), 0) == iota((rows, rows), 1)
    scale = column_of(scale_row[...], eye)
    ones = jnp.ones((8, group), BF16)
    coupling = jnp.zeros((8, rows), F32)
    for g in range(GROUPS):
        cols = slice(g * group, (g + 1) * group)
        gate = pre[:, 2 * g * group : (2 * g + 1) * group].astype(F32)
        gated = y[:, cols].astype(F32) * (gate * jax.nn.sigmoid(gate))
        product = grad[:, cols].astype(F32) * gated
        scaled = gain[:, cols]
        low_out[:, cols] = (gated * scale * scaled).astype(BF16)
        high, low = two_parts(product * scaled)
        coupling = coupling + mm(ones, high, NT) + mm(ones, low, NT)
        gain_grad[0:1, cols] += jnp.sum(product * scale, axis=0, keepdims=True)
    coupling_out[...] = coupling


def backward_kernel(
    g, heads, first_group, last_group, seg_sm, span_sm, gate_in, inner_in, inner_halo, ss, ss_halo,
    grad_in, y_in, state_in, seg_row, scale_row, pull_row, spread, kernel, offset, skip, gain,
    shared_kernel, shared_offset, bias, rate, *rest,
):
    rest = list(rest)
    chain_in = None if first_group else rest.pop(0)
    low_out, chain_out, conv_grads, head_grads = rest[:4]
    rest = rest[4:]
    shared_grads = rest.pop(0) if last_group else None
    after, lam = rest[:2]
    shared_after = rest[2] if last_group else None
    seq = pl.program_id(0)
    backward_piece = pl.program_id(1)
    pieces = pl.num_programs(1)
    piece = pieces - 1 - backward_piece
    group = gate_in.shape[1]

    @pl.when(backward_piece == 0)
    def _():
        after[...] = jnp.zeros_like(after)
        lam[...] = jnp.zeros_like(lam)
        if last_group:
            shared_after[...] = jnp.zeros_like(shared_after)

    @pl.when(jnp.logical_and(backward_piece == 0, seq == 0))
    def _():
        conv_grads[...] = jnp.zeros_like(conv_grads)
        head_grads[...] = jnp.zeros_like(head_grads)
        if last_group:
            shared_grads[...] = jnp.zeros_like(shared_grads)

    rows = STRETCH
    width = shared_kernel.shape[1]
    half = width // 2
    inside = jnp.where(piece > 0, 1.0, 0.0)
    shared_pre = ss[:, :width]
    eye, order, reach_all, same, allowed, pre, step, log_step, cum, to_end, reach, keep = piece_context(
        seg_sm, span_sm, seg_row, ss[:, width:], bias[...], rate[...], seq, piece
    )
    allowed_t = jnp.logical_and(same, reach_all - order >= 0)
    shared_shifted = shifted_rows(shared_pre, ss_halo[:, :width] * inside)
    conv = conv_of(shared_shifted, shared_kernel[...], shared_offset[...])
    shared_sig = jax.nn.sigmoid(conv)
    act = conv * shared_sig
    b, c = act[:, :half].astype(BF16), act[:, half:].astype(BF16)
    scores = jnp.where(allowed, mm(c, b, NT), 0.0)
    scores_t = jnp.where(allowed_t, mm(b, c, NT), 0.0)
    signed = jnp.where(order > 0, scores, jnp.where(order < 0, -scores, 0.0))
    cum_rows = cum.T
    c_cols = c.T
    lane = iota((rows, LANES), 1)
    head_row = iota((LANES, rows), 0)

    scale = column_of(scale_row[...], eye)
    pull = column_of(pull_row[...], eye)
    gate = gate_in[...].astype(F32)
    y = y_in[...].astype(F32)
    gate_sig = jax.nn.sigmoid(gate)
    silu = gate * gate_sig
    d_gated = scale * (gain[...] * grad_in[...].astype(F32)) - pull * (y * silu)
    low_out[:, :group] = (d_gated * y * (gate_sig + silu * (1.0 - gate_sig))).astype(BF16)
    dy = d_gated * silu

    inner = inner_in[...].astype(F32)
    shifted = shifted_rows(inner, inner_halo[...] * inside)
    v = conv_of(shifted, kernel[...], offset[...])
    sig = jax.nn.sigmoid(v)
    x = v * sig
    spread_g = spread[...]
    step_x = expand(step, spread_g)
    reach_x = expand(reach, spread_g)
    to_end_x = expand(to_end, spread_g)
    keep_row = expand(jnp.broadcast_to(keep, (8, LANES)), spread_g)[0:1]
    u = x * step_x
    u_low = u.astype(BF16)
    dy_low = dy.astype(BF16)
    entering = state_in[0, 0]
    lam_now = lam[...]
    lam_low = lam_now.astype(BF16)
    reached = (dy * reach_x).astype(BF16)
    pulled = mm(b, lam_low) * to_end_x
    d_c = mm(reached, entering, NT)
    d_b = mm(u * to_end_x, lam_low, NT)
    from_start = dy * reach_x * mm(c, entering)
    from_end = u * pulled
    edge = jnp.sum(from_end, axis=0, keepdims=True) + keep_row * jnp.sum(
        lam_now * entering.astype(F32), axis=0, keepdims=True
    )
    lam[...] = keep_row * lam_now + mm(c_cols, reached)

    d_scores = jnp.zeros((rows, rows), F32)
    row_sums = jnp.zeros((rows, LANES), F32)
    col_sums = jnp.zeros((LANES, rows), F32)
    du_parts = []
    for pair in range(group // LANES):
        cols = slice(pair * LANES, (pair + 1) * LANES)
        pair_u, pair_dy = u_low[:, cols], dy_low[:, cols]
        halves = []
        for one in range(2):
            head = g * heads + 2 * pair + one
            own = lane < HEAD if one == 0 else lane >= HEAD
            gap = cum[:, head : head + 1] - cum_rows[head : head + 1]
            decay = jnp.exp2(-jnp.abs(gap))
            d_mix = mm(jnp.where(own, pair_dy, jnp.zeros_like(pair_dy)), pair_u, NT) * decay
            d_scores = d_scores + d_mix
            turned = d_mix * signed
            row_sums = row_sums + jnp.where(lane == head, jnp.sum(turned, axis=1, keepdims=True), 0.0)
            col_sums = col_sums + jnp.where(head_row == head, jnp.sum(turned, axis=0, keepdims=True), 0.0)
            halves.append(mm(scores_t * decay, pair_dy))
        du_parts.append(jnp.where(lane < HEAD, halves[0], halves[1]))
    du = jnp.concatenate(du_parts, axis=1) + pulled
    d_scores = jnp.where(allowed, d_scores, 0.0).astype(BF16)
    d_c = d_c + mm(d_scores, b)
    d_b = d_b + mm(d_scores, c, TN)

    d_cum = row_sums - col_sums.T + head_sum(from_start - from_end, spread_g)
    high, low = two_parts(d_cum)
    behind = (order <= 0).astype(F32)
    d_log = mm(behind, high) + mm(behind, low) + head_sum(jnp.broadcast_to(edge, (8, group)), spread_g)[0:1]
    d_step = (d_log * rate[...] + head_sum(x * du, spread_g)) * jax.nn.sigmoid(pre)
    own_heads = jnp.logical_and(lane >= g * heads, lane < (g + 1) * heads)
    d_step = jnp.where(own_heads, d_step, 0.0)
    head_grads[0:1] += jnp.sum(jnp.where(own_heads, d_log * log_step, 0.0), axis=0, keepdims=True)
    head_grads[1:2] += jnp.sum(d_step, axis=0, keepdims=True)

    dx = step_x * du + skip[...] * dy
    dv = dx * (sig + x * (1.0 - sig))
    low_out[:, group:] = conv_back(dv, after[...], kernel[...]).astype(BF16)
    after[...] = dv[:8]
    for tap in range(4):
        conv_grads[tap : tap + 1] += jnp.sum(dv * shifted[tap], axis=0, keepdims=True)
    conv_grads[4:5] += jnp.sum(dv, axis=0, keepdims=True)
    conv_grads[5:6] += jnp.sum(dy * x, axis=0, keepdims=True)

    d_act = jnp.concatenate([d_b, d_c], axis=1)
    if chain_in is not None:
        d_act = d_act + chain_in[:, :width]
        d_step = d_step + chain_in[:, width:]
    if last_group:
        d_conv = d_act * (shared_sig + act * (1.0 - shared_sig))
        chain_out[:, :width] = conv_back(d_conv, shared_after[...], shared_kernel[...]).astype(BF16)
        chain_out[:, width:] = d_step.astype(BF16)
        shared_after[...] = d_conv[:8]
        for tap in range(4):
            shared_grads[tap : tap + 1] += jnp.sum(d_conv * shared_shifted[tap], axis=0, keepdims=True)
        shared_grads[4:5] += jnp.sum(d_conv, axis=0, keepdims=True)
    else:
        chain_out[:, :width] = d_act
        chain_out[:, width:] = d_step


def whole(shape):
    return pl.BlockSpec(shape, lambda *_: (0,) * len(shape))


def cost(flops, moved):
    return pl.CostEstimate(flops=int(flops), bytes_accessed=int(moved), transcendentals=0)


def scan_forward(segments, spans, pre, ss, seg_row, spread, kernel, offset, skip, shared_kernel, shared_offset, bias, rate):
    seqs, length = segments.shape
    pieces = length // STRETCH
    channels = kernel.shape[1]
    width = shared_kernel.shape[1]
    at = lambda s, p, *_: (s * pieces + p, 0)
    row_at = lambda s, p, *_: (0, s * pieces + p)
    total = seqs * length
    return pl.pallas_call(
        partial(forward_kernel, channels),
        name="scan_forward",
        grid_spec=pltpu.PrefetchScalarGridSpec(
            num_scalar_prefetch=2,
            grid=(seqs, pieces),
            in_specs=[
                pl.BlockSpec((STRETCH, 2 * channels), at),
                pl.BlockSpec((STRETCH, ss.shape[1]), at),
                pl.BlockSpec((1, STRETCH), row_at),
                whole(spread.shape), whole(kernel.shape), whole(offset.shape), whole(skip.shape),
                whole(shared_kernel.shape), whole(shared_offset.shape), whole(bias.shape), whole(rate.shape),
            ],
            out_specs=[
                pl.BlockSpec((STRETCH, channels), at),
                pl.BlockSpec((1, 1, width // 2, channels), lambda s, p, *_: (s, p, 0, 0)),
                pl.BlockSpec((8, STRETCH), row_at),
            ],
            scratch_shapes=[
                pltpu.VMEM((8, channels), F32), pltpu.VMEM((8, width), F32), pltpu.VMEM((width // 2, channels), F32),
            ],
        ),
        out_shape=[
            jax.ShapeDtypeStruct((total, channels), F32),
            jax.ShapeDtypeStruct((seqs, pieces, width // 2, channels), BF16),
            jax.ShapeDtypeStruct((8, total), F32),
        ],
        compiler_params=pltpu.CompilerParams(dimension_semantics=("arbitrary", "arbitrary")),
        cost_estimate=cost(12e9, 24e6),
    )(segments, spans, pre, ss, seg_row, spread, kernel, offset, skip, shared_kernel, shared_offset, bias, rate)


def gate_step(pre, y, grad, scale_row, gain):
    total, channels = y.shape
    at = lambda i: (i, 0)
    row_at = lambda i: (0, i)
    return pl.pallas_call(
        partial(gate_kernel, channels),
        name="gate_norm",
        grid=(total // STRETCH,),
        in_specs=[
            pl.BlockSpec((STRETCH, 2 * channels), at),
            pl.BlockSpec((STRETCH, channels), at),
            pl.BlockSpec((STRETCH, channels), at),
            pl.BlockSpec((1, STRETCH), row_at),
            whole(gain.shape),
        ],
        out_specs=[pl.BlockSpec((STRETCH, channels), at), pl.BlockSpec((8, STRETCH), row_at), whole((8, channels))],
        out_shape=[
            jax.ShapeDtypeStruct((total, channels), BF16),
            jax.ShapeDtypeStruct((8, total), F32),
            jax.ShapeDtypeStruct((8, channels), F32),
        ],
        compiler_params=pltpu.CompilerParams(dimension_semantics=("arbitrary",)),
        cost_estimate=cost(4e9, 20e6),
    )(pre, y, grad, scale_row, gain)


def scan_backward(
    g, segments, spans, pre, ss, grad, y, states, seg_row, scale_row, pull_row, spread, kernel, offset, skip, gain,
    shared_kernel, shared_offset, bias, rate, chain,
):
    seqs, length = segments.shape
    pieces = length // STRETCH
    channels = kernel.shape[1]
    group = channels // GROUPS
    width = shared_kernel.shape[1]
    wide = ss.shape[1]
    total = seqs * length
    last = g == GROUPS - 1
    piece_at = lambda s, p: s * pieces + pieces - 1 - p
    at = lambda col: lambda s, p, *_: (piece_at(s, p), col)
    row_at = lambda s, p, *_: (0, piece_at(s, p))
    halo = lambda rows, col: lambda s, p, *_: (jnp.maximum(piece_at(s, p) * (STRETCH // rows) - 1, 0), col)
    cols = lambda rows: pl.BlockSpec((rows, group), lambda *_: (0, g))
    in_specs = [
        pl.BlockSpec((STRETCH, group), at(2 * g)),
        pl.BlockSpec((STRETCH, group), at(2 * g + 1)),
        pl.BlockSpec((8, group), halo(8, 2 * g + 1)),
        pl.BlockSpec((STRETCH, wide), at(0)),
        pl.BlockSpec((8, wide), halo(8, 0)),
        pl.BlockSpec((STRETCH, group), at(g)),
        pl.BlockSpec((STRETCH, group), at(g)),
        pl.BlockSpec((1, 1, width // 2, group), lambda s, p, *_: (s, pieces - 1 - p, 0, g)),
        pl.BlockSpec((1, STRETCH), row_at),
        pl.BlockSpec((1, STRETCH), row_at),
        pl.BlockSpec((1, STRETCH), row_at),
        cols(spread.shape[0]), cols(kernel.shape[0]), cols(1), cols(1), cols(1),
        whole(shared_kernel.shape), whole(shared_offset.shape), whole(bias.shape), whole(rate.shape),
    ]
    operands = [
        pre, pre, pre, ss, ss, grad, y, states, seg_row, scale_row, pull_row, spread, kernel, offset, skip, gain,
        shared_kernel, shared_offset, bias, rate,
    ]
    if chain is not None:
        in_specs.append(pl.BlockSpec((STRETCH, wide), at(0)))
        operands.append(chain)
    out_specs = [pl.BlockSpec((STRETCH, 2 * group), at(0)), pl.BlockSpec((STRETCH, wide), at(0)), whole((8, group)), whole((8, LANES))]
    out_shape = [
        jax.ShapeDtypeStruct((total, 2 * group), BF16),
        jax.ShapeDtypeStruct((total, wide), BF16 if last else F32),
        jax.ShapeDtypeStruct((8, group), F32),
        jax.ShapeDtypeStruct((8, LANES), F32),
    ]
    scratch = [pltpu.VMEM((8, group), F32), pltpu.VMEM((width // 2, group), F32)]
    if last:
        out_specs.append(whole((8, width)))
        out_shape.append(jax.ShapeDtypeStruct((8, width), F32))
        scratch.append(pltpu.VMEM((8, width), F32))
    return pl.pallas_call(
        partial(backward_kernel, g, group // HEAD, chain is None, last),
        name=f"scan_backward_{g}",
        grid_spec=pltpu.PrefetchScalarGridSpec(
            num_scalar_prefetch=2, grid=(seqs, pieces), in_specs=in_specs, out_specs=out_specs, scratch_shapes=scratch
        ),
        out_shape=out_shape,
        compiler_params=pltpu.CompilerParams(dimension_semantics=("arbitrary", "arbitrary")),
        cost_estimate=cost(14e9, 20e6),
    )(segments, spans, *operands)


def ring_order(devices, across):
    depth = devices // across
    if devices % across or across < 2 or depth < 2 or depth % 2 and across % 2:
        return list(range(devices))
    if across == 2:
        return [z * 2 for z in range(depth)] + [z * 2 + 1 for z in reversed(range(depth))]
    walk = [z * across for z in range(depth)]
    for turn, z in enumerate(reversed(range(depth))):
        xs = range(1, across)
        walk += [z * across + x for x in (xs if turn % 2 == 0 else reversed(xs))]
    return walk


def ring_steps(order, parts, puts):
    n = len(order)
    if n > 8:
        slab = lax.psum_scatter(parts, "dp", scatter_dimension=0, tiled=True)
        puts(0, lax.all_gather(slab, "dp", axis=0, tiled=True).astype(F32))
        return
    place = jnp.asarray([order.index(i) for i in range(n)], jnp.int32)[lax.axis_index("dp")]
    onward = [(order[i], order[(i + 1) % n]) for i in range(n)]
    pairs = {1: onward, -1: [(b, a) for a, b in onward]}
    block = parts.shape[0] // (2 * n)

    def row(way, index):
        return (0 if way > 0 else n * block) + jnp.mod(index, n) * block

    def own(way, index):
        return lax.dynamic_slice_in_dim(parts, row(way, index), block, 0)

    held = {way: own(way, place) for way in (1, -1)}
    for step in range(1, n):
        for way in (1, -1):
            arrived = lax.ppermute(held[way], "dp", pairs[way])
            held[way] = (arrived.astype(F32) + own(way, place - way * step).astype(F32)).astype(BF16)
    for step in range(n):
        for way in (1, -1):
            if step:
                held[way] = lax.ppermute(held[way], "dp", pairs[way])
            puts(row(way, place + way - way * step), held[way].astype(F32))


def tensor_pairs(size):
    core = [(i, i ^ 1) for i in range(size)]
    along = [(i, (i + 2) % size) for i in range(size)]
    return core, along


def gather_rows(rows, size):
    core, along = tensor_pairs(size)
    index = lax.axis_index("tensor")
    block = rows.shape[0]
    out = jnp.zeros((size * block,) + rows.shape[1:], rows.dtype)
    held = rows
    for step in range(size // 2):
        if step:
            held = lax.ppermute(held, "tensor", along)
        origin = jnp.mod(index - 2 * step, size)
        out = lax.dynamic_update_slice_in_dim(out, held, origin * block, 0)
        other = lax.ppermute(held, "tensor", core)
        out = lax.dynamic_update_slice_in_dim(out, other, (origin ^ 1) * block, 0)
    return out


def total_over(values, axis, size):
    step = 1
    while step < size:
        values = values + lax.ppermute(values, axis, [(i, i ^ step) for i in range(size)])
        step *= 2
    return values


def body(
    ranks, dps, tokens, pre_gain, weight_gate, weight_inner, weight_step, weight_shared, conv_kernel, conv_offset,
    shared_kernel, shared_offset, step_bias, log_rate, skip_gain, gate_gain, weight_out, cotangent, segments, image_span,
):
    seqs, rows, model = tokens.shape
    length = rows * ranks
    total = seqs * length
    channels = weight_gate.shape[1]
    group = channels // GROUPS
    heads = step_bias.shape[0]
    inner_width = channels * ranks
    width = weight_shared.shape[1]
    index = lax.axis_index("tensor")

    own = tokens.astype(F32)
    row_scale = lax.rsqrt(jnp.mean(own * own, axis=2, keepdims=True) + EPSILON)
    normed_rows = (own * row_scale * pre_gain[None, None, :]).astype(BF16)
    normed_in = jnp.concatenate([gather_rows(normed_rows[s], ranks) for s in range(seqs)], axis=0)
    cot_full = jnp.concatenate([gather_rows(cotangent[s], ranks) for s in range(seqs)], axis=0)

    columns = []
    for g in range(GROUPS):
        cols = slice(g * group, (g + 1) * group)
        columns += [weight_gate[:, cols], weight_inner[:, cols]]
    weight_pre = jnp.concatenate(columns, axis=1)
    weight_ss = jnp.concatenate(
        [weight_shared, weight_step, jnp.zeros((model, LANES - heads), BF16)], axis=1
    )
    pad_heads = lambda values: jnp.pad(values, (0, LANES - heads))[None, :]
    bias = pad_heads(step_bias)
    rate = pad_heads(-jnp.exp(log_rate))
    skip = jnp.repeat(skip_gain, HEAD)[None, :]
    heads_of = (jnp.arange(LANES)[:, None] == (jnp.arange(channels) // HEAD)[None, :]).astype(BF16)
    spread = jnp.concatenate([heads_of, heads_of], axis=0)
    seg_row = segments.astype(F32).reshape(1, total)
    offset_row, shared_offset_row = conv_offset[None, :], shared_offset[None, :]
    gain_row = gate_gain[None, :]

    pre = lax.dot_general(normed_in, weight_pre, NN, preferred_element_type=F32)
    ss = lax.dot_general(normed_in, weight_ss, NN, preferred_element_type=F32)
    y, states, squares = scan_forward(
        segments, image_span, pre, ss, seg_row, spread, conv_kernel, offset_row, skip, shared_kernel, shared_offset_row,
        bias, rate,
    )
    grad = lax.dot_general(cot_full, weight_out, NT, preferred_element_type=F32)
    square_sum = total_over(squares[0:1], "tensor", ranks)
    scale_row = lax.rsqrt(square_sum / inner_width + EPSILON)
    normed_out, coupling, gain_grad = gate_step(pre, y, grad, scale_row, gain_row)
    coupling_sum = total_over(coupling[0:1], "tensor", ranks)
    pull_row = scale_row * scale_row * scale_row / inner_width * coupling_sum

    order = ring_order(dps, ranks // 2)
    grads = {}

    def reduce_into(parts, targets):
        def put(row, values):
            for name, start, count, column in targets:
                grads[name] = lax.dynamic_update_slice(grads[name], values[:, start : start + count], (row, column))

        ring_steps(order, parts, put)

    grads["out"] = jnp.zeros((channels, model), F32)
    grads["gate"] = jnp.zeros((model, channels), F32)
    grads["inner"] = jnp.zeros((model, channels), F32)
    grads["ss"] = jnp.zeros((model, LANES), F32)
    out_part = lax.dot_general(normed_out, cot_full, TN, preferred_element_type=BF16)
    reduce_into(out_part, [("out", 0, model, 0)])
    mixed = lax.dot_general(normed_out, weight_out, NN, preferred_element_type=BF16)

    chain = None
    low_parts, conv_parts, head_grads = [], [], jnp.zeros((8, LANES), F32)
    for g in range(GROUPS):
        result = scan_backward(
            g, segments, image_span, pre, ss, grad, y, states, seg_row, scale_row, pull_row, spread, conv_kernel,
            offset_row, skip, gain_row, shared_kernel, shared_offset_row, bias, rate, chain,
        )
        low, chain = result[0], result[1]
        low_parts.append(low)
        conv_parts.append(result[2])
        head_grads = head_grads + result[3]
        part = lax.dot_general(normed_in, low, TN, preferred_element_type=BF16)
        reduce_into(part, [("gate", 0, group, g * group), ("inner", group, group, g * group)])
    shared_grads = result[4]

    slab = width // ranks
    shared_part = jnp.moveaxis(chain[:, :width].reshape(total, ranks, slab), 1, 0)
    shared_low = lax.psum_scatter(shared_part, "tensor", scatter_dimension=0, tiled=True)[0]
    side = jnp.concatenate(
        [shared_low, chain[:, width : width + heads], jnp.zeros((total, LANES - slab - heads), BF16)], axis=1
    )
    weight_side = jnp.concatenate(
        [
            lax.dynamic_slice_in_dim(weight_shared, index * slab, slab, 1),
            weight_step,
            jnp.zeros((model, LANES - slab - heads), BF16),
        ],
        axis=1,
    )
    side_part = lax.dot_general(normed_in, side, TN, preferred_element_type=BF16)
    reduce_into(side_part, [("ss", 0, LANES, 0)])
    grad_shared = lax.all_gather(grads["ss"][:, :slab].astype(BF16), "tensor", axis=1, tiled=True).astype(F32)
    grad_step = grads["ss"][:, slab : slab + heads]

    blocks, token_blocks = [], []
    pre_gain_grad = jnp.zeros((model,), F32)
    for s in range(seqs):
        part = slice(s * length, (s + 1) * length)
        mixed_rows = lax.psum_scatter(mixed[part], "tensor", scatter_dimension=0, tiled=True)
        blocks.append((own[s] + mixed_rows.astype(F32)).astype(BF16))
    for s in range(seqs):
        part = slice(s * length, (s + 1) * length)
        summed = lax.dot_general(side[part], weight_side, NT, preferred_element_type=F32)
        for g in range(GROUPS):
            weights = weight_pre[:, 2 * g * group : 2 * (g + 1) * group]
            summed = summed + lax.dot_general(low_parts[g][part], weights, NT, preferred_element_type=F32)
        normed_grad = lax.psum_scatter(summed.astype(BF16), "tensor", scatter_dimension=0, tiled=True).astype(F32)
        weighted = normed_grad * pre_gain[None, :]
        scale = row_scale[s]
        projection = jnp.sum(weighted * own[s], axis=1, keepdims=True)
        own_grad = scale * weighted - scale * scale * scale / model * own[s] * projection
        pre_gain_grad = pre_gain_grad + jnp.sum(normed_grad * own[s] * scale, axis=0)
        token_blocks.append((cotangent[s].astype(F32) + own_grad).astype(BF16))

    conv_grads = jnp.concatenate(conv_parts, axis=1)
    packed = jnp.concatenate([conv_grads[:6], gain_grad[0:1], jnp.pad(head_grads[:2], ((0, 0), (0, channels - LANES)))], axis=0)
    packed = total_over(packed, "dp", dps)
    shared_packed = total_over(total_over(shared_grads, "dp", dps), "tensor", ranks)
    gain_total = total_over(total_over(pre_gain_grad[None, :], "dp", dps), "tensor", ranks)[0]
    return (
        jnp.stack(blocks),
        jnp.stack(token_blocks),
        gain_total,
        grads["gate"],
        grads["inner"],
        grad_step,
        grad_shared,
        packed[0:4],
        packed[4],
        shared_packed[0:4],
        shared_packed[4],
        packed[8, :heads],
        packed[7, :heads],
        jnp.sum(packed[5].reshape(heads, HEAD), axis=1),
        packed[6],
        grads["out"],
    )


def solution(mesh):
    placed = (
        P("dp", "tensor", None),
        P(),
        P(None, "tensor"),
        P(None, "tensor"),
        P(None, "tensor"),
        P(),
        P(None, "tensor"),
        P("tensor"),
        P(),
        P(),
        P("tensor"),
        P("tensor"),
        P("tensor"),
        P("tensor"),
        P("tensor", None),
        P("dp", "tensor", None),
        P("dp", None),
        P("dp", None),
    )
    return jax.shard_map(
        partial(body, mesh.shape["tensor"], mesh.shape["dp"]),
        mesh=mesh,
        in_specs=placed,
        out_specs=(
            P("dp", "tensor", None),
            P("dp", "tensor", None),
            P(),
            P(None, "tensor"),
            P(None, "tensor"),
            P(None, "tensor"),
            P(),
            P(None, "tensor"),
            P("tensor"),
            P(),
            P(),
            P("tensor"),
            P("tensor"),
            P("tensor"),
            P("tensor"),
            P("tensor", None),
        ),
        check_vma=False,
    )
```

time: 1930 us -> 823 us (0.43)
  waiting for transfers between devices: 885 us -> 219 us
  matrix products: 439 us -> 150 us
  blocking collectives: 164 us -> 0 us
  other arithmetic: 193 us -> 40.7 us
  starting transfers between devices: 0.94 us -> 143 us
  Pallas kernels: 0 us -> 133 us
  local copies, waits for them, and re-layouts: 213 us -> 101 us
    psum x1 -> x0, waiting for transfers between devices: 810 us -> none  [body(): lax.psum((running[1], running[2], running[3], running[4], running[5], run...]
    dot_general x54 -> x14, matrix products: 439 us -> 150 us  [the longest x4 31.6 us: body(): lax.dot_general(low_parts[g][part], weights, NT, preferred_element_type=F32)]
    ppermute x0 -> x141, waiting for transfers between devices: none -> 213 us  [the longest x56 75 us: ring_steps(): held[way] = lax.ppermute(held[way], 'dp', pairs[way])]
    psum x5 -> x0, blocking collectives: 164 us -> none  [the longest x1 76.4 us: body(): shared_full = lax.psum(pieces_grad[3], 'tensor')]
    ppermute x0 -> x141, starting transfers between devices: none -> 142 us  [the longest x56 63.1 us: ring_steps(): arrived = lax.ppermute(held[way], 'dp', pairs[way])]
    pallas_call x0 -> x4, Pallas kernels: none -> 133 us  [the longest x2 85.2 us: scan_backward(): pl.pallas_call(partial(backward_kernel, g, group // HEAD, chain is None,...]
    reshape x21 -> x0, local copies, waits for them, and re-layouts: 124 us -> none  [the longest x6 43 us: state_scan(): return total.reshape(length, head_count, head_width)]
    reduce_sum x22 -> x3, other arithmetic: 73.3 us -> 7.03 us  [the longest x1 4.19 us: body(): jnp.sum(normed_grad * own[s] * scale, axis=0)]
  transfers between devices with their start and end apart: 9 -> 147, of which waited for: 4 -> 76; matrix products, arithmetic and copies ran while one was open for 23% -> 32% of each run, Pallas kernels for 0% -> 4%
where the time goes in v1:
time: 823 us; the launch traced here: 814 us
  waiting for transfers between devices  219 us (27%)
  matrix products  150 us (18%)
  starting transfers between devices  143 us (17%)
  Pallas kernels  133 us (16%)
  local copies, waits for them, and re-layouts  101 us (12%)
  other arithmetic  40.7 us (5%)
  between operations  27.4 us (3%)
    pallas_call x2, Pallas kernels, scan_backward(): pl.pallas_call(partial(backward_kernel, g, group // HEAD, chain is None,...  85.2 us
    ppermute x56, waiting for transfers between devices, ring_steps(): held[way] = lax.ppermute(held[way], 'dp', pairs[way])  75 us
    ppermute x56, waiting for transfers between devices, ring_steps(): arrived = lax.ppermute(held[way], 'dp', pairs[way])  64.2 us
    ppermute x56, starting transfers between devices, ring_steps(): arrived = lax.ppermute(held[way], 'dp', pairs[way])  63.1 us
    ppermute x4, waiting for transfers between devices, gather_rows(): held = lax.ppermute(held, 'tensor', along)  60.2 us
    ppermute x56, starting transfers between devices, ring_steps(): held[way] = lax.ppermute(held[way], 'dp', pairs[way])  57.2 us
    pallas_call x1, Pallas kernels, scan_forward(): pl.pallas_call(partial(forward_kernel, channels), name='scan_forward', gr...  33.1 us
    dot_general x4, matrix products, body(): lax.dot_general(low_parts[g][part], weights, NT, preferred_element_type=F32)  31.6 us
  transfers between devices with their start and end apart: 147, of which 76 were waited for; matrix products, arithmetic and copies ran while one was open for 32% of the time, Pallas kernels for 4%

profile of v1, /device:TPU:0, one launch (start us, length us, event | category | flops | bytes accessed | tf_op | source)
XLA Modules:
  0.0 814.0 jit_solution(15291710151155312220)
XLA Ops:
  36.0 5.5 collective-permute-done.1
  51.5 12.7 %collective-permute-done.4 = bf16[256,2048]{1,0:T(8,128)(2,1)} collective-permute-done((bf16[256,2048]{1,0:T(8,128)(2,1)}, bf16[256,2048]{1,0:T(8,128)(2,1)}, u32[]{:S(2)}, u32[]{:S(2)}) %collective-permute-start.4) | collective-permute-done | bytes 1048608 | tf_op jit(solution)/shard_map/ppermute | solution.py:535
  67.0 19.6 %collective-permute-done.10 = bf16[256,2048]{1,0:T(8,128)(2,1)} collective-permute-done((bf16[256,2048]{1,0:T(8,128)(2,1)}, bf16[256,2048]{1,0:T(8,128)(2,1)}, u32[]{:S(2)}, u32[]{:S(2)}) %collective-permute-start.10) | collective-permute-done | bytes 1048608 | tf_op jit(solution)/shard_map/ppermute | solution.py:535
  86.6 22.3 %collective-permute-done.7 = bf16[256,2048]{1,0:T(8,128)(2,1)} collective-permute-done((bf16[256,2048]{1,0:T(8,128)(2,1)}, bf16[256,2048]{1,0:T(8,128)(2,1)}, u32[]{:S(2)}, u32[]{:S(2)}) %collective-permute-start.7) | collective-permute-done | bytes 1048608 | tf_op jit(solution)/shard_map/ppermute | solution.py:535
  118.2 10.0 %fusion.34.ss.ss_halo = f32[2048,384]{1,0:T(8,128)} fusion(bf16[2048,16]{1,0:T(8,128)(2,1)S(1)} %copy.79, bf16[2048,256]{1,0:T(8,128)(2,1)S(1)} %copy-done.27, bf16[384]{0:T(512)(128)(2,1)S(1)} %pad.39.clone, bf16[1024,2048]{1,0:T(8,128)(2,1)S(1)} %constant_dynamic-update-slice_fusion.8, bf16[1024,2048]{1,0:T(8,128)(2,1)} %constant_dynamic-update-slice_fusion.12), kind=kOutput, calls=%fused_computation.52 | convolution fusion | flops 3242721280 | bytes 12649216 | tf_op jit(solution)/shard_map/dot_general | solution.py:590
  128.2 26.4 %fusion.pre.gate_in.inner_in.inner_halo = f32[2048,2048]{1,0:T(8,128)} fusion(bf16[2048,512]{1,0:T(8,128)(2,1)} %get-tuple-element.257, bf16[2048,512]{1,0:T(8,128)(2,1)S(1)} %copy-done.21, bf16[2048,512]{1,0:T(8,128)(2,1)} %get-tuple-element.258, bf16[2048,512]{1,0:T(8,128)(2,1)} %get-tuple-element.167, bf16[1024,2048]{1,0:T(8,128)(2,1)} %copy-done.8, ...), kind=kOutput, calls=%fused_computation.1 | convolution fusion | flops 17230200832 | bytes 33554432 | tf_op jit(solution)/shard_map/dot_general | solution.py:589
  154.6 33.1 %scan_forward.1 = (f32[2048,1024]{1,0:T(8,128)}, bf16[2,4,128,1024]{3,2,1,0:T(8,128)(2,1)}, f32[8,2048]{1,0:T(8,128)}) custom-call(s32[2,1024]{1,0:T(2,128)} %seg_sm.5, s32[2,2]{1,0:T(2,128)} %span_sm.5, f32[2048,2048]{1,0:T(8,128)} %fusion.pre.gate_in.inner_in.inner_halo, f32[2048,384]{1,0:T(8,128)} %fusion.34.ss.ss_halo, f32[1,2048]{1,0:T(1,128)} %bitcast.92, ...), custom_call_target="tpu_custom_call" | custom-call | flops 12000000000 | bytes 24000000 | tf_op jit(solution)/shard_map/scan_forward/pallas_call | solution.py:358
  196.3 15.2 %fusion.9.grad.grad_in = f32[2048,1024]{1,0:T(8,128)} fusion(bf16[1024,2048]{1,0:T(8,128)(2,1)} %param.36, bf16[1024,2048]{1,0:T(8,128)(2,1)} %constant_dynamic-update-slice_fusion, bf16[1024,2048]{1,0:T(8,128)(2,1)} %constant_dynamic-update-slice_fusion.4), kind=kOutput, calls=%fused_computation.13 | convolution fusion | flops 8606711808 | bytes 20971520 | tf_op jit(solution)/shard_map/dot_general | solution.py:595
  212.1 15.2 %gate_norm.1 = (bf16[2048,1024]{1,0:T(8,128)(2,1)}, f32[8,2048]{1,0:T(8,128)}, f32[8,1024]{1,0:T(8,128)}) custom-call(f32[2048,2048]{1,0:T(8,128)} %fusion.pre.gate_in.inner_in.inner_halo, f32[2048,1024]{1,0:T(8,128)} %get-tuple-element.31.y.y_in, f32[2048,1024]{1,0:T(8,128)} %fusion.9.grad.grad_in, f32[1,2048]{1,0:T(1,128)} %add_rsqrt_fusion.scale_row, ...), custom_call_target="tpu_custom_call" | custom-call | flops 4000000000 | bytes 20000000 | tf_op jit(solution)/shard_map/gate_norm/pallas_call | solution.py:394
  234.5 41.0 %scan_backward_0.1 = (bf16[2048,1024]{1,0:T(8,128)(2,1)}, f32[2048,384]{1,0:T(8,128)}, f32[8,512]{1,0:T(8,128)}, f32[8,128]{1,0:T(8,128)}) custom-call(s32[2,1024]{1,0:T(2,128)} %seg_sm.5, s32[2,2]{1,0:T(2,128)} %span_sm.5, f32[2048,2048]{1,0:T(8,128)} %fusion.pre.gate_in.inner_in.inner_halo, f32[2048,2048]{1,0:T(8,128)} %fusion.pre.gate_in.inner_in.inner_halo, ...), custom_call_target="tpu_custom_call" | custom-call | flops 14000000000 | bytes 20000000 | tf_op jit(solution)/shard_map/scan_backward_0/pallas_call | solution.py:467
  275.6 44.2 %scan_backward_1.1 = (bf16[2048,1024]{1,0:T(8,128)(2,1)}, bf16[2048,384]{1,0:T(8,128)(2,1)}, f32[8,512]{1,0:T(8,128)}, f32[8,128]{1,0:T(8,128)}, f32[8,256]{1,0:T(8,128)}) custom-call(s32[2,1024]{1,0:T(2,128)} %seg_sm.5, s32[2,2]{1,0:T(2,128)} %span_sm.5, f32[2048,2048]{1,0:T(8,128)} %fusion.pre.gate_in.inner_in.inner_halo, ...), custom_call_target="tpu_custom_call" | custom-call | flops 14000000000 | bytes 20000000 | tf_op jit(solution)/shard_map/scan_backward_1/pallas_call | solution.py:467
  324.3 10.9 %fusion.10 = f32[1024,2048]{1,0:T(8,128)} fusion(bf16[2048,512]{1,0:T(8,128)(2,1)} %get-tuple-element.257, bf16[2048,512]{1,0:T(8,128)(2,1)} %get-tuple-element.168, bf16[2048,1024]{1,0:T(8,128)(2,1)} %get-tuple-element.39), kind=kOutput, calls=%fused_computation.18 | convolution fusion | flops 4303355904 | bytes 14680064 | tf_op jit(solution)/shard_map/dot_general | solution.py:665
  335.3 6.8 fusion.12
  342.1 5.8 reduce-scatter.10.cloned.1.call-done
  348.9 9.2 %add_convert_fusion = bf16[1024,2048]{1,0:T(8,128)(2,1)} fusion(f32[1024,2048]{1,0:T(8,128)} %fusion.10, f32[1024,2048]{1,0:T(8,128)} %fusion.12, bf16[2048,128]{0,1:T(8,128)(2,1)S(1)} %maximum_maximum_fusion, bf16[2048,16]{1,0:T(8,128)(2,1)S(1)} %copy.79, bf16[2048,64]{1,0:T(8,128)(2,1)S(1)} %constant_dynamic-slice_fusion.22, bf16[128]{0:T(256)(128)(2,1)S(1)} %pad.30.clone), kind=kOutput, calls=%fused_computation.10 | convolution fusion | flops 544735232 | bytes 22282752 | tf_op jit(solution)/shard_map/dot_general | solution.py:662
  358.6 7.2 fusion.13
  365.8 6.7 fusion.11
  372.5 3.5 add_convert_fusion.1
  378.7 4.8 fusion.65
  451.0 11.9 %fusion.77 = bf16[2048,2048]{1,0:T(8,128)(2,1)S(1)} fusion(bf16[2048,1024]{1,0:T(8,128)(2,1)} %get-tuple-element.33, bf16[1024,2048]{1,0:T(8,128)(2,1)} %param.36), kind=kOutput, calls=%fused_computation.317 | convolution fusion | flops 8589934592 | bytes 16777216 | tf_op jit(solution)/shard_map/dot_general | solution.py:618
  462.9 3.9 fusion.72
  469.5 12.7 %fusion.8 = bf16[1024,2048]{1,0:T(8,128)(2,1)S(1)} fusion(bf16[2048,1024]{1,0:T(8,128)(2,1)} %get-tuple-element.33, bf16[1024,2048]{1,0:T(8,128)(2,1)} %constant_dynamic-update-slice_fusion, bf16[1024,2048]{1,0:T(8,128)(2,1)} %constant_dynamic-update-slice_fusion.4), kind=kOutput, calls=%fused_computation.12 | convolution fusion | flops 8606711808 | bytes 16777216 | tf_op jit(solution)/shard_map/dot_general | solution.py:616
  488.7 14.0 %fusion.66 = bf16[2048,1024]{1,0:T(8,128)(2,1)S(1)} fusion(bf16[2048,1024]{1,0:T(8,128)(2,1)} %get-tuple-element.39, bf16[1024,2048]{1,0:T(8,128)(2,1)} %copy-done.8, bf16[1024,2048]{1,0:T(8,128)(2,1)} %constant_dynamic-update-slice_fusion.12), kind=kOutput, calls=%fused_computation.306 | convolution fusion | flops 8606711808 | bytes 16777216 | tf_op jit(solution)/shard_map/dot_general | solution.py:631
  506.7 10.8 %fusion.67 = bf16[2048,1024]{1,0:T(8,128)(2,1)S(1)} fusion(bf16[2048,1024]{1,0:T(8,128)(2,1)S(1)} %copy-done.43, bf16[1024,2048]{1,0:T(8,128)(2,1)S(1)} %copy-done.9, bf16[1024,2048]{1,0:T(8,128)(2,1)} %constant_dynamic-update-slice_fusion.12), kind=kOutput, calls=%fused_computation.307 | convolution fusion | flops 8606711808 | bytes 16777216 | tf_op jit(solution)/shard_map/dot_general | solution.py:631
  633.7 4.6 collective-permute-done.27
  641.2 4.5 broadcast.216.clone.1
  646.4 4.5 broadcast.216.clone
  713.6 3.4 collective-permute-done.70
  758.0 4.0 collective-permute-done.48
  762.0 4.5 collective-permute-done.76
  781.5 4.2 fusion.27
  797.0 4.0 fusion.41
  (594 shorter events, 399.6 us)
Async XLA Ops:
  7.2 340.7 %reduce-scatter.10.cloned.1.call-start = ((), (), s32[]{:S(2)}) async-start(), calls=%async_computation.7 | async-start | bytes 1310720 | tf_op jit(solution)/shard_map/reduce_scatter | solution.py:637
  14.4 19.9 %collective-permute-start = (bf16[256,2048]{1,0:T(8,128)(2,1)}, bf16[256,2048]{1,0:T(8,128)(2,1)}, u32[]{:S(2)}, u32[]{:S(2)}) collective-permute-start(bf16[256,2048]{1,0:T(8,128)(2,1)} %get-tuple-element.173), channel_id=1, source_target_pairs={{0,1},{1,0},{2,3},{3,2},{4,5},{5,4},{6,7},{7,6},{8,9},{9,8},{10,11... | collective-permute-start | bytes 3145736 | tf_op jit(solution)/shard_map/ppermute | solution.py:538
  14.9 26.7 %collective-permute-start.1 = (bf16[256,2048]{1,0:T(8,128)(2,1)}, bf16[256,2048]{1,0:T(8,128)(2,1)S(1)}, u32[]{:S(2)}, u32[]{:S(2)}) collective-permute-start(bf16[256,2048]{1,0:T(8,128)(2,1)} %get-tuple-element.173), channel_id=1, source_target_pairs={{0,2},{1,3},{2,0},{3,1},{4,6},{5,7},{6,4},{7,5},{8,10},{9,11},{10,... | collective-permute-start | bytes 3145736 | tf_op jit(solution)/shard_map/ppermute | solution.py:535
  17.4 30.8 %collective-permute-start.3 = (bf16[256,2048]{1,0:T(8,128)(2,1)}, bf16[256,2048]{1,0:T(8,128)(2,1)}, u32[]{:S(2)}, u32[]{:S(2)}) collective-permute-start(bf16[256,2048]{1,0:T(8,128)(2,1)} %get-tuple-element.174), channel_id=1, source_target_pairs={{0,1},{1,0},{2,3},{3,2},{4,5},{5,4},{6,7},{7,6},{8,9},{9,8},{10,11... | collective-permute-start | bytes 3145736 | tf_op jit(solution)/shard_map/ppermute | solution.py:538
  17.6 46.6 %collective-permute-start.4 = (bf16[256,2048]{1,0:T(8,128)(2,1)}, bf16[256,2048]{1,0:T(8,128)(2,1)}, u32[]{:S(2)}, u32[]{:S(2)}) collective-permute-start(bf16[256,2048]{1,0:T(8,128)(2,1)} %get-tuple-element.174), channel_id=1, source_target_pairs={{0,2},{1,3},{2,0},{3,1},{4,6},{5,7},{6,4},{7,5},{8,10},{9,11},{10,... | collective-permute-start | bytes 3145736 | tf_op jit(solution)/shard_map/ppermute | solution.py:535
  19.4 47.1 %collective-permute-start.9 = (bf16[256,2048]{1,0:T(8,128)(2,1)}, bf16[256,2048]{1,0:T(8,128)(2,1)}, u32[]{:S(2)}, u32[]{:S(2)}) collective-permute-start(bf16[256,2048]{1,0:T(8,128)(2,1)} %get-tuple-element.172), channel_id=1, source_target_pairs={{0,1},{1,0},{2,3},{3,2},{4,5},{5,4},{6,7},{7,6},{8,9},{9,8},{10,11... | collective-permute-start | bytes 3145736 | tf_op jit(solution)/shard_map/ppermute | solution.py:538
  34.3 52.4 %collective-permute-start.10 = (bf16[256,2048]{1,0:T(8,128)(2,1)}, bf16[256,2048]{1,0:T(8,128)(2,1)}, u32[]{:S(2)}, u32[]{:S(2)}) collective-permute-start(bf16[256,2048]{1,0:T(8,128)(2,1)} %get-tuple-element.172), channel_id=1, source_target_pairs={{0,2},{1,3},{2,0},{3,1},{4,6},{5,7},{6,4},{7,5},{8,10},{9,11},{10,... | collective-permute-start | bytes 3145736 | tf_op jit(solution)/shard_map/ppermute | solution.py:535
  41.6 67.3 %collective-permute-start.7 = (bf16[256,2048]{1,0:T(8,128)(2,1)}, bf16[256,2048]{1,0:T(8,128)(2,1)}, u32[]{:S(2)}, u32[]{:S(2)}) collective-permute-start(bf16[256,2048]{1,0:T(8,128)(2,1)} %get-tuple-element.171), channel_id=1, source_target_pairs={{0,2},{1,3},{2,0},{3,1},{4,6},{5,7},{6,4},{7,5},{8,10},{9,11},{10,... | collective-permute-start | bytes 3145736 | tf_op jit(solution)/shard_map/ppermute | solution.py:535
  48.1 65.4 %collective-permute-start.6 = (bf16[256,2048]{1,0:T(8,128)(2,1)}, bf16[256,2048]{1,0:T(8,128)(2,1)S(1)}, u32[]{:S(2)}, u32[]{:S(2)}) collective-permute-start(bf16[256,2048]{1,0:T(8,128)(2,1)} %get-tuple-element.171), channel_id=1, source_target_pairs={{0,1},{1,0},{2,3},{3,2},{4,5},{5,4},{6,7},{7,6},{8,9},{9,8},{10,11... | collective-permute-start | bytes 3145736 | tf_op jit(solution)/shard_map/ppermute | solution.py:538
  64.2 52.8 %collective-permute-start.2 = (bf16[256,2048]{1,0:T(8,128)(2,1)S(1)}, bf16[256,2048]{1,0:T(8,128)(2,1)S(1)}, u32[]{:S(2)}, u32[]{:S(2)}) collective-permute-start(bf16[256,2048]{1,0:T(8,128)(2,1)S(1)} %collective-permute-done.1), channel_id=1, source_target_pairs={{0,1},{1,0},{2,3},{3,2},{4,5},{5,4},{6,7},{7,6},{8,9},{9,8},{10,11... | collective-permute-start | bytes 3145736 | tf_op jit(solution)/shard_map/ppermute | solution.py:538
  66.5 51.5 %collective-permute-start.5 = (bf16[256,2048]{1,0:T(8,128)(2,1)}, bf16[256,2048]{1,0:T(8,128)(2,1)S(1)}, u32[]{:S(2)}, u32[]{:S(2)}) collective-permute-start(bf16[256,2048]{1,0:T(8,128)(2,1)} %collective-permute-done.4), channel_id=1, source_target_pairs={{0,1},{1,0},{2,3},{3,2},{4,5},{5,4},{6,7},{7,6},{8,9},{9,8},{10,11... | collective-permute-start | bytes 3145736 | tf_op jit(solution)/shard_map/ppermute | solution.py:538
  86.6 102.3 %collective-permute-start.11 = (bf16[256,2048]{1,0:T(8,128)(2,1)}, bf16[256,2048]{1,0:T(8,128)(2,1)}, u32[]{:S(2)}, u32[]{:S(2)}) collective-permute-start(bf16[256,2048]{1,0:T(8,128)(2,1)} %collective-permute-done.10), channel_id=1, source_target_pairs={{0,1},{1,0},{2,3},{3,2},{4,5},{5,4},{6,7},{7,6},{8,9},{9,8},{10,11... | collective-permute-start | bytes 3145736 | tf_op jit(solution)/shard_map/ppermute | solution.py:538
  108.9 82.4 %collective-permute-start.8 = (bf16[256,2048]{1,0:T(8,128)(2,1)}, bf16[256,2048]{1,0:T(8,128)(2,1)}, u32[]{:S(2)}, u32[]{:S(2)}) collective-permute-start(bf16[256,2048]{1,0:T(8,128)(2,1)} %collective-permute-done.7), channel_id=1, source_target_pairs={{0,1},{1,0},{2,3},{3,2},{4,5},{5,4},{6,7},{7,6},{8,9},{9,8},{10,11... | collective-permute-start | bytes 3145736 | tf_op jit(solution)/shard_map/ppermute | solution.py:538
  194.4 17.1 %collective-permute-start.13 = (f32[1,2048]{1,0:T(1,128)S(1)}, f32[1,2048]{1,0:T(1,128)S(1)}, u32[]{:S(2)}, u32[]{:S(2)}) collective-permute-start(f32[1,2048]{1,0:T(1,128)S(1)} %slice_add_fusion.1), channel_id=1, source_target_pairs={{0,2},{1,3},{2,0},{3,1},{4,6},{5,7},{6,4},{7,5},{8,10},{9,11},{10,... | collective-permute-start | bytes 24584 | tf_op jit(solution)/shard_map/ppermute | solution.py:546
  322.5 459.0 %reduce-scatter.14.cloned.1.call-start = ((), (), s32[]{:S(2)}) async-start(), calls=%async_computation.9 | async-start | bytes 5242880 | tf_op jit(solution)/shard_map/reduce_scatter | solution.py:666
  358.1 423.4 %reduce-scatter.12.cloned.1.call-start = ((), (), s32[]{:S(2)}) async-start(), calls=%async_computation.8 | async-start | bytes 5242880 | tf_op jit(solution)/shard_map/reduce_scatter | solution.py:666
  376.0 417.0 %all-gather.2.cloned.1.call-start = ((), (), s32[]{:S(2)}) async-start(), calls=%async_computation.10 | async-start | bytes 1310720 | tf_op jit(solution)/shard_map/all_gather | solution.py:651
  450.7 346.2 %reduce-scatter.6.cloned.1.call-start = ((), (), s32[]{:S(2)}) async-start(), calls=%async_computation.5 | async-start | bytes 5242880 | tf_op jit(solution)/shard_map/reduce_scatter | solution.py:658
  466.8 330.1 %reduce-scatter.8.cloned.1.call-start = ((), (), s32[]{:S(2)}) async-start(), calls=%async_computation.6 | async-start | bytes 5242880 | tf_op jit(solution)/shard_map/reduce_scatter | solution.py:658
  484.3 48.5 %collective-permute-start.113 = (bf16[64,2048]{1,0:T(8,128)(2,1)S(1)}, bf16[64,2048]{1,0:T(8,128)(2,1)S(1)}, u32[]{:S(2)}, u32[]{:S(2)}) collective-permute-start(bf16[64,2048]{1,0:T(8,128)(2,1)S(1)} %get-tuple-element.132), channel_id=1, source_target_pairs={{0,8},{8,16},{16,24},{24,28},{28,20},{20,12},{12,4},{4,0},{1,9},{9... | collective-permute-start | bytes 786440 | tf_op jit(solution)/shard_map/ppermute | solution.py:512
  485.1 58.4 %collective-permute-start.120 = (bf16[64,2048]{1,0:T(8,128)(2,1)S(1)}, bf16[64,2048]{1,0:T(8,128)(2,1)S(1)}, u32[]{:S(2)}, u32[]{:S(2)}) collective-permute-start(bf16[64,2048]{1,0:T(8,128)(2,1)S(1)} %get-tuple-element.131), channel_id=1, source_target_pairs={{8,0},{16,8},{24,16},{28,24},{20,28},{12,20},{4,12},{0,4},{9,1},{1... | collective-permute-start | bytes 786440 | tf_op jit(solution)/shard_map/ppermute | solution.py:512
  619.4 32.2 %collective-permute-start.55 = (bf16[128,1024]{1,0:T(8,128)(2,1)S(1)}, bf16[128,1024]{1,0:T(8,128)(2,1)S(1)}, u32[]{:S(2)}, u32[]{:S(2)}) collective-permute-start(bf16[128,1024]{1,0:T(8,128)(2,1)S(1)} %get-tuple-element.136), channel_id=1, source_target_pairs={{0,8},{8,16},{16,24},{24,28},{28,20},{20,12},{12,4},{4,0},{1,9},{9... | collective-permute-start | bytes 786440 | tf_op jit(solution)/shard_map/ppermute | solution.py:512
  622.8 28.8 %collective-permute-start.62 = (bf16[128,1024]{1,0:T(8,128)(2,1)S(1)}, bf16[128,1024]{1,0:T(8,128)(2,1)S(1)}, u32[]{:S(2)}, u32[]{:S(2)}) collective-permute-start(bf16[128,1024]{1,0:T(8,128)(2,1)S(1)} %get-tuple-element.135), channel_id=1, source_target_pairs={{8,0},{16,8},{24,16},{28,24},{20,28},{12,20},{4,12},{0,4},{9,1},{1... | collective-permute-start | bytes 786440 | tf_op jit(solution)/shard_map/ppermute | solution.py:512
  631.6 23.1 %collective-permute-start.126 = (bf16[64,2048]{1,0:T(8,128)(2,1)S(1)}, bf16[64,2048]{1,0:T(8,128)(2,1)S(1)}, u32[]{:S(2)}, u32[]{:S(2)}) collective-permute-start(bf16[64,2048]{1,0:T(8,128)(2,1)S(1)} %get-tuple-element.120), channel_id=1, source_target_pairs={{8,0},{16,8},{24,16},{28,24},{20,28},{12,20},{4,12},{0,4},{9,1},{1... | collective-permute-start | bytes 786440 | tf_op jit(solution)/shard_map/ppermute | solution.py:512
  639.1 17.2 %collective-permute-start.35 = (bf16[128,1024]{1,0:T(8,128)(2,1)S(1)}, bf16[128,1024]{1,0:T(8,128)(2,1)S(1)}, u32[]{:S(2)}, u32[]{:S(2)}) collective-permute-start(bf16[128,1024]{1,0:T(8,128)(2,1)S(1)} %get-tuple-element.150), channel_id=1, source_target_pairs={{0,8},{8,16},{16,24},{24,28},{28,20},{20,12},{12,4},{4,0},{1,9},{9... | collective-permute-start | bytes 786440 | tf_op jit(solution)/shard_map/ppermute | solution.py:517
  654.8 17.2 %collective-permute-start.128 = (bf16[64,2048]{1,0:T(8,128)(2,1)S(1)}, bf16[64,2048]{1,0:T(8,128)(2,1)S(1)}, u32[]{:S(2)}, u32[]{:S(2)}) collective-permute-start(bf16[64,2048]{1,0:T(8,128)(2,1)S(1)} %get-tuple-element.101), channel_id=1, source_target_pairs={{8,0},{16,8},{24,16},{28,24},{20,28},{12,20},{4,12},{0,4},{9,1},{1... | collective-permute-start | bytes 786440 | tf_op jit(solution)/shard_map/ppermute | solution.py:517
  672.1 16.8 %collective-permute-start.130 = (bf16[64,2048]{1,0:T(8,128)(2,1)S(1)}, bf16[64,2048]{1,0:T(8,128)(2,1)S(1)}, u32[]{:S(2)}, u32[]{:S(2)}) collective-permute-start(bf16[64,2048]{1,0:T(8,128)(2,1)S(1)} %collective-permute-done.128), channel_id=1, source_target_pairs={{8,0},{16,8},{24,16},{28,24},{20,28},{12,20},{4,12},{0,4},{9,1},{1... | collective-permute-start | bytes 786440 | tf_op jit(solution)/shard_map/ppermute | solution.py:517
  689.0 16.8 %collective-permute-start.132 = (bf16[64,2048]{1,0:T(8,128)(2,1)S(1)}, bf16[64,2048]{1,0:T(8,128)(2,1)S(1)}, u32[]{:S(2)}, u32[]{:S(2)}) collective-permute-start(bf16[64,2048]{1,0:T(8,128)(2,1)S(1)} %collective-permute-done.130), channel_id=1, source_target_pairs={{8,0},{16,8},{24,16},{28,24},{20,28},{12,20},{4,12},{0,4},{9,1},{1... | collective-permute-start | bytes 786440 | tf_op jit(solution)/shard_map/ppermute | solution.py:517
  705.8 16.8 %collective-permute-start.134 = (bf16[64,2048]{1,0:T(8,128)(2,1)S(1)}, bf16[64,2048]{1,0:T(8,128)(2,1)S(1)}, u32[]{:S(2)}, u32[]{:S(2)}) collective-permute-start(bf16[64,2048]{1,0:T(8,128)(2,1)S(1)} %collective-permute-done.132), channel_id=1, source_target_pairs={{8,0},{16,8},{24,16},{28,24},{20,28},{12,20},{4,12},{0,4},{9,1},{1... | collective-permute-start | bytes 786440 | tf_op jit(solution)/shard_map/ppermute | solution.py:517
  722.7 16.8 %collective-permute-start.136 = (bf16[64,2048]{1,0:T(8,128)(2,1)S(1)}, bf16[64,2048]{1,0:T(8,128)(2,1)S(1)}, u32[]{:S(2)}, u32[]{:S(2)}) collective-permute-start(bf16[64,2048]{1,0:T(8,128)(2,1)S(1)} %collective-permute-done.134), channel_id=1, source_target_pairs={{8,0},{16,8},{24,16},{28,24},{20,28},{12,20},{4,12},{0,4},{9,1},{1... | collective-permute-start | bytes 786440 | tf_op jit(solution)/shard_map/ppermute | solution.py:517
  739.5 16.8 %collective-permute-start.138 = (bf16[64,2048]{1,0:T(8,128)(2,1)S(1)}, bf16[64,2048]{1,0:T(8,128)(2,1)S(1)}, u32[]{:S(2)}, u32[]{:S(2)}) collective-permute-start(bf16[64,2048]{1,0:T(8,128)(2,1)S(1)} %collective-permute-done.136), channel_id=1, source_target_pairs={{8,0},{16,8},{24,16},{28,24},{20,28},{12,20},{4,12},{0,4},{9,1},{1... | collective-permute-start | bytes 786440 | tf_op jit(solution)/shard_map/ppermute | solution.py:517
  756.4 34.8 %collective-permute-start.140 = (bf16[64,2048]{1,0:T(8,128)(2,1)S(1)}, bf16[64,2048]{1,0:T(8,128)(2,1)}, u32[]{:S(2)}, u32[]{:S(2)}) collective-permute-start(bf16[64,2048]{1,0:T(8,128)(2,1)S(1)} %collective-permute-done.138), channel_id=1, source_target_pairs={{8,0},{16,8},{24,16},{28,24},{20,28},{12,20},{4,12},{0,4},{9,1},{1... | collective-permute-start | bytes 786440 | tf_op jit(solution)/shard_map/ppermute | solution.py:517
  (161 other events, 1868.2 us)
Sparse Core Ops, SparseCore 0:
  322.6 25.1 reduce-scatter.9
  358.2 44.5 reduce-scatter.13
  405.4 44.4 reduce-scatter.11
  452.0 16.7 all-gather.1
  471.3 44.4 reduce-scatter.5
  518.2 44.4 reduce-scatter.7

commit v2 on v1

v2 whole, which is shorter than its diff:
```python
from functools import partial

import jax
import jax.numpy as jnp
from jax import lax
from jax.experimental import pallas as pl
from jax.experimental.pallas import tpu as pltpu
from jax.sharding import PartitionSpec as P

STRETCH = 256
HEAD = 64
LANES = 128

EPSILON = 1e-05
LOG2E = 1.4426950408889634
BF16 = jnp.bfloat16
F32 = jnp.float32
NN = (((1,), (0,)), ((), ()))
NT = (((1,), (1,)), ((), ()))
TN = (((0,), (0,)), ((), ()))


def mm(left, right, dims=NN):
    return lax.dot_general(left.astype(BF16), right.astype(BF16), dims, preferred_element_type=F32)


def two_parts(values):
    high = values.astype(BF16)
    return high, (values - high.astype(F32)).astype(BF16)


def iota(shape, axis):
    return lax.broadcasted_iota(jnp.int32, shape, axis)


def expand(values, spread):
    high, low = two_parts(values)
    return mm(jnp.concatenate([high, low], axis=1), spread)


def head_sum(values, spread):
    high, low = two_parts(values)
    half = spread[:LANES]
    return mm(high, half, NT) + mm(low, half, NT)


def column_of(row, eye):
    return jnp.sum(jnp.where(eye, row, 0.0), axis=1, keepdims=True)


def token_of(rows):
    return (rows & 7) * (STRETCH // 8) + (rows >> 3)


def lagged(current, before):
    last = current[STRETCH - 24 :]
    top = iota(last.shape, 0) & 7
    first = jnp.where(top == 0, pltpu.roll(before, 17, 0), pltpu.roll(last, 1, 0))
    joined = jnp.concatenate([first, current], axis=0)
    return [joined[8 * tap : 8 * tap + STRETCH] for tap in range(4)]


def leading(current, after):
    first = current[:24]
    top = iota(first.shape, 0) & 7
    last = jnp.where(top == 7, pltpu.roll(after, 7, 0), pltpu.roll(first, 23, 0))
    joined = jnp.concatenate([current, last], axis=0)
    return [joined[24 - 8 * tap : 24 - 8 * tap + STRETCH] for tap in range(4)]


def taps(values, kernel):
    total = kernel[0:1] * values[0]
    for tap in range(1, 4):
        total = total + kernel[tap : tap + 1] * values[tap]
    return total


def column_sum(values):
    return jnp.sum(values, axis=0, keepdims=True)


def piece_context(seg_sm, span_sm, seg_row, step_pre, bias, rate, seq, piece):
    rows = STRETCH
    i0, i1 = token_of(iota((rows, rows), 0)), token_of(iota((rows, rows), 1))
    order = i0 - i1
    eye = order == 0
    seg_r = seg_row[...]
    seg_c = column_of(seg_r, eye)
    first = span_sm[seq, 0]
    image = jnp.logical_and(piece >= first, piece < first + span_sm[seq, 1])
    reach_all = jnp.where(image, 2 * rows, 0)
    same = seg_c == seg_r
    start = piece * rows
    last_doc = seg_sm[seq, start + rows - 1].astype(F32)
    before_doc = seg_sm[seq, jnp.maximum(start - 1, 0)].astype(F32)
    pre = step_pre + bias
    tail = jnp.exp(-jnp.abs(pre))
    step = jnp.maximum(pre, 0.0) + jnp.log1p(tail)
    log_step = step * rate
    high, low = two_parts(log_step)
    lowest = (log_step - high.astype(F32) - low.astype(F32)).astype(BF16)
    ahead = (order >= 0).astype(F32)
    cum = mm(ahead, high) + mm(ahead, low) + mm(ahead, lowest)
    cum = cum * LOG2E
    end = cum[rows - 1 : rows]
    to_end = jnp.where(seg_c == last_doc, jnp.exp2(end - cum), 0.0)
    reach = jnp.where(seg_c == before_doc, jnp.exp2(cum), 0.0)
    keep = jnp.where(last_doc == before_doc, jnp.exp2(end), 0.0)
    sign = jnp.where(order > 0, 1.0, jnp.where(order < 0, -1.0, 0.0))
    return eye, order, reach_all, same, sign, pre, step, log_step, cum, to_end, reach, keep


def forward_kernel(
    channels, slots, seg_sm, span_sm, pre, seg_row, spread, kernel, offset, skip, shared_kernel, shared_offset, bias, rate,
    y_out, gated_out, state_out, square_out, before, shared_before, state,
):
    seq, piece = pl.program_id(0), pl.program_id(1)
    width = shared_kernel.shape[1]
    half = width // 2

    @pl.when(piece == 0)
    def _():
        before[...] = jnp.zeros_like(before)
        shared_before[...] = jnp.zeros_like(shared_before)
        state[...] = jnp.zeros_like(state)

    shared_pre = pre[:, 2 * channels : 2 * channels + width]
    step_columns = pre[:, 2 * channels + width : 2 * channels + width + LANES]
    _, order, reach_all, same, sign, _, step, _, cum, to_end, reach, keep = piece_context(
        seg_sm, span_sm, seg_row, step_columns, bias[...], rate[...], seq, piece
    )
    allowed = jnp.logical_and(same, order + reach_all >= 0)
    conv = taps(lagged(shared_pre, shared_before[...]), shared_kernel) + shared_offset[...]
    shared_before[...] = shared_pre[STRETCH - 24 :]
    act = conv * jax.nn.sigmoid(conv)
    b, c = act[:, :half].astype(BF16), act[:, half:].astype(BF16)
    scores = jnp.where(allowed, mm(c, b, NT), 0.0)
    cum_rows = cum.T
    b_cols = b.T
    lane = iota((STRETCH, LANES), 1)
    spread_all = spread[...]

    gate = pre[:, :channels]
    inner = pre[:, channels : 2 * channels]
    v = taps(lagged(inner, before[...]), kernel) + offset[...]
    before[...] = inner[STRETCH - 24 :]
    x = v * jax.nn.sigmoid(v)
    u = x * expand(step, spread_all)
    entering = state[...]
    state_out[0, 0] = entering.astype(BF16)
    carried = mm(c, entering) * expand(reach, spread_all)
    keep_row = expand(jnp.broadcast_to(keep, (8, LANES)), spread_all)[0:1]
    state[...] = keep_row * entering + mm(b_cols, u * expand(to_end, spread_all))
    u_low = u.astype(BF16)
    mixed = []
    for pair in range(channels // LANES):
        pair_u = u_low[:, pair * LANES : (pair + 1) * LANES]
        halves = []
        for head in (2 * pair, 2 * pair + 1):
            gap = cum[:, head : head + 1] - cum_rows[head : head + 1]
            halves.append(mm(scores * jnp.exp2(gap * sign), pair_u))
        mixed.append(jnp.where(lane < HEAD, halves[0], halves[1]))
    y = jnp.concatenate(mixed, axis=1) + carried + skip[...] * x
    y_out[...] = y
    gated = y * (gate * jax.nn.sigmoid(gate))
    gated_out[...] = gated.astype(BF16)
    square_out[...] = mm(jnp.ones((8, channels), BF16), gated * gated, NT)


def coupling_kernel(slots, gated, grad, gain, coupling_out):
    product = grad[...] * (gated[...].astype(F32) * gain[...])
    coupling_out[...] = mm(jnp.ones((8, gain.shape[1]), BF16), product, NT)


def norm_kernel(slots, gated, scale_row, gain, low_out):
    eye = iota((STRETCH, STRETCH), 0) == iota((STRETCH, STRETCH), 1)
    scale = column_of(scale_row[...], eye)
    low_out[...] = (gated[...].astype(F32) * gain[...] * scale).astype(BF16)


def backward_kernel(
    channels, start, slots, seg_sm, span_sm, pre, halo, grad_in, y_in, state_in, seg_row, scale_row, pull_row, spread, kernel,
    offset, skip, gain, shared_kernel, shared_offset, bias, rate,
    *rest,
):
    earlier = rest[3:6] if start else None
    low_out, shared_out, step_out, channel_grads, head_grads, shared_grads, after, lam, shared_after = rest[-9:]
    seq = pl.program_id(0) + start
    backward_piece = pl.program_id(1)
    piece = pl.num_programs(1) - 1 - backward_piece
    width = shared_kernel.shape[1]
    half = width // 2
    rows = STRETCH

    @pl.when(backward_piece == 0)
    def _():
        after[...] = jnp.zeros_like(after)
        lam[...] = jnp.zeros_like(lam)
        shared_after[...] = jnp.zeros_like(shared_after)

    @pl.when(jnp.logical_and(backward_piece == 0, seq == start))
    def _():
        for i, total in enumerate((channel_grads, head_grads, shared_grads)):
            total[...] = earlier[i][...] if start else jnp.zeros_like(total)

    inside = jnp.where(piece > 0, 1.0, 0.0)
    shared_pre = pre[:, 2 * channels : 2 * channels + width]
    step_columns = pre[:, 2 * channels + width : 2 * channels + width + LANES]
    eye, order, reach_all, same, sign, step_pre, step, log_step, cum, to_end, reach, keep = piece_context(
        seg_sm, span_sm, seg_row, step_columns, bias[...], rate[...], seq, piece
    )
    allowed = jnp.logical_and(same, order + reach_all >= 0)
    allowed_t = jnp.logical_and(same, reach_all - order >= 0)
    conv = taps(lagged(shared_pre, halo[8:32, 2 * channels : 2 * channels + width] * inside), shared_kernel) + shared_offset[...]
    shared_sig = jax.nn.sigmoid(conv)
    act = conv * shared_sig
    b, c = act[:, :half].astype(BF16), act[:, half:].astype(BF16)
    scores = jnp.where(allowed, mm(c, b, NT), 0.0)
    scores_t = jnp.where(allowed_t, mm(b, c, NT), 0.0)
    signed = scores * sign
    cum_rows = cum.T
    c_cols = c.T
    lane = iota((rows, LANES), 1)
    head_row = iota((LANES, rows), 0)

    scale = column_of(scale_row[...], eye)
    pull = column_of(pull_row[...], eye)
    gate = pre[:, :channels]
    y = y_in[...]
    gate_sig = jax.nn.sigmoid(gate)
    silu = gate * gate_sig
    gated = y * silu
    scaled_grad = scale * grad_in[...]
    d_gated = gain[...] * scaled_grad - pull * gated
    low_out[:, :channels] = (d_gated * y * (gate_sig + silu * (1.0 - gate_sig))).astype(BF16)
    channel_grads[6:7] += column_sum(scaled_grad * gated)
    dy = d_gated * silu

    inner = pre[:, channels : 2 * channels]
    v = taps(lagged(inner, halo[8:32, channels : 2 * channels] * inside), kernel) + offset[...]
    sig = jax.nn.sigmoid(v)
    x = v * sig
    spread_all = spread[...]
    step_x = expand(step, spread_all)
    to_end_x = expand(to_end, spread_all)
    keep_row = expand(jnp.broadcast_to(keep, (8, LANES)), spread_all)[0:1]
    u = x * step_x
    u_low = u.astype(BF16)
    dy_low = dy.astype(BF16)
    entering = state_in[0, 0]
    lam_now = lam[...]
    lam_low = lam_now.astype(BF16)
    reached_full = dy * expand(reach, spread_all)
    reached = reached_full.astype(BF16)
    pulled = mm(b, lam_low) * to_end_x
    d_c = mm(reached, entering, NT)
    d_b = mm(u * to_end_x, lam_low, NT)
    from_start = reached_full * mm(c, entering)
    from_end = u * pulled
    edge = column_sum(from_end) + keep_row * column_sum(lam_now * entering.astype(F32))
    lam[...] = keep_row * lam_now + mm(c_cols, reached)

    d_scores = jnp.zeros((rows, rows), F32)
    row_sums = jnp.zeros((rows, LANES), F32)
    col_sums = jnp.zeros((LANES, rows), F32)
    du_parts = []
    for pair in range(channels // LANES):
        cols = slice(pair * LANES, (pair + 1) * LANES)
        pair_u, pair_dy = u_low[:, cols], dy_low[:, cols]
        halves = []
        for one in range(2):
            head = 2 * pair + one
            own = lane < HEAD if one == 0 else lane >= HEAD
            gap = cum[:, head : head + 1] - cum_rows[head : head + 1]
            decay = jnp.exp2(gap * sign)
            d_mix = mm(jnp.where(own, pair_dy, jnp.zeros_like(pair_dy)), pair_u, NT) * decay
            d_scores = d_scores + d_mix
            turned = d_mix * signed
            row_sums = row_sums + jnp.where(lane == head, jnp.sum(turned, axis=1, keepdims=True), 0.0)
            col_sums = col_sums + jnp.where(head_row == head, column_sum(turned), 0.0)
            halves.append(mm(scores_t * decay, pair_dy))
        du_parts.append(jnp.where(lane < HEAD, halves[0], halves[1]))
    du = jnp.concatenate(du_parts, axis=1) + pulled
    d_scores = jnp.where(allowed, d_scores, 0.0).astype(BF16)
    d_c = d_c + mm(d_scores, b)
    d_b = d_b + mm(d_scores, c, TN)

    d_cum = row_sums - col_sums.T + head_sum(from_start - from_end, spread_all)
    high, low = two_parts(d_cum)
    behind = (order <= 0).astype(F32)
    d_log = mm(behind, high) + mm(behind, low) + head_sum(jnp.broadcast_to(edge, (8, channels)), spread_all)[0:1]
    d_step = (d_log * rate[...] + head_sum(x * du, spread_all)) * jax.nn.sigmoid(step_pre)
    d_step = jnp.where(lane < channels // HEAD, d_step, 0.0)
    step_out[...] = d_step.astype(BF16)
    head_grads[0:1] += column_sum(d_log * log_step)
    head_grads[1:2] += column_sum(d_step)

    dx = step_x * du + skip[...] * dy
    dv = dx * (sig + x * (1.0 - sig))
    ahead = leading(dv, after[...])
    after[...] = dv[:24]
    low_out[:, channels:] = taps(ahead, kernel).astype(BF16)
    for tap in range(4):
        channel_grads[tap : tap + 1] += column_sum(ahead[tap] * inner)
    channel_grads[4:5] += column_sum(dv)
    channel_grads[5:6] += column_sum(dy * x)

    d_conv = jnp.concatenate([d_b, d_c], axis=1) * (shared_sig + act * (1.0 - shared_sig))
    ahead = leading(d_conv, shared_after[...])
    shared_after[...] = d_conv[:24]
    shared_out[...] = taps(ahead, shared_kernel).astype(BF16)
    for tap in range(4):
        shared_grads[tap : tap + 1] += column_sum(ahead[tap] * shared_pre)
    shared_grads[4:5] += column_sum(d_conv)


def whole(shape):
    return pl.BlockSpec(shape, lambda *_: (0,) * len(shape))


def limits(mebibytes):
    return pltpu.CompilerParams(vmem_limit_bytes=mebibytes << 20)


def cost(flops, moved):
    return pl.CostEstimate(flops=int(flops), bytes_accessed=int(moved), transcendentals=0)


def fill_kernel(dims, spans, first, own, other, *rest):
    weights = rest[: len(spans)]
    product, joined, held, sems = rest[-4:]
    rows = own.shape[0]
    tile = product.shape[1]
    part = min(tile, 256)
    index, step = pl.program_id(0), pl.program_id(1)
    copies = [
        pltpu.make_async_copy(block, joined.at[pl.ds((2 * i + first) * rows, rows)], sems.at[i])
        for i, block in enumerate((own, other))
    ]
    for i, block in enumerate((own, other)):

        @pl.when(jnp.logical_and(index == 0, step == i))
        def _():
            copies[i].start()
            held[i] = block[...]

    for (start, count), weight in zip(spans, weights):

        @pl.when(jnp.logical_and(index >= start, index < start + count))
        def _():
            @pl.loop(0, tile // part)
            def _(piece):
                cols = pl.ds(pl.multiple_of(piece * part, part), part)
                own_weight = weight[:, cols] if dims == NN else weight[cols, :]
                product[:, cols] = lax.dot_general(held[step], own_weight, dims, preferred_element_type=F32)

    @pl.when(jnp.logical_and(index == pl.num_programs(0) - 1, step == 1))
    def _():
        for copy in copies:
            copy.wait()


def fill_rows(own, other, weights, dims, filled):
    rows, depth = own.shape
    side = 1 if dims == NN else 0
    widths = [values.shape[side] for values in weights]
    tile = min(512, *widths)
    spans, first = [], 0
    for width in widths:
        spans.append((first, width // tile))
        first += width // tile
    second = filled is not None
    anywhere = pl.BlockSpec(memory_space=pl.ANY)

    def weight_spec(span):
        column = lambda j: jnp.clip(j - span[0], 0, span[1] - 1)
        if dims == NN:
            return pl.BlockSpec((depth, tile), lambda j, i: (0, column(j)))
        return pl.BlockSpec((tile, depth), lambda j, i: (column(j), 0))

    count = len(weights)
    block = lambda i: 2 * i + (1 if second else 0)
    return pl.pallas_call(
        partial(fill_kernel, dims, spans, 1 if second else 0),
        name="fill_rows",
        grid=(first, 2),
        in_specs=[whole(own.shape), whole(other.shape)]
        + [weight_spec(span) for span in spans]
        + ([anywhere] * 2 if second else []),
        out_specs=[
            pl.BlockSpec((rows, tile), lambda j, i: (block(i), j)),
            anywhere,
        ],
        out_shape=[jax.ShapeDtypeStruct((4 * rows, sum(widths)), F32), jax.ShapeDtypeStruct((4 * rows, depth), BF16)],
        scratch_shapes=[pltpu.VMEM((2, rows, depth), BF16), pltpu.SemaphoreType.DMA((2,))],
        input_output_aliases={2 + count: 0, 3 + count: 1} if second else {},
        compiler_params=limits(36),
        cost_estimate=cost(4 * rows * depth * sum(widths), 4 * rows * (depth + sum(widths))),
    )(own, other, *weights, *(filled if second else ()))


def blank(shape):
    return pl.pallas_call(
        lambda out: None, name="blank", out_specs=pl.BlockSpec(memory_space=pl.ANY), out_shape=jax.ShapeDtypeStruct(shape, F32)
    )()


def scan_forward(slots, segments, spans, pre, seg_row, spread, kernel, offset, skip, shared_kernel, shared_offset, bias, rate):
    seqs, length = segments.shape
    pieces = length // STRETCH
    channels = kernel.shape[1]
    width = shared_kernel.shape[1]
    at = lambda s, p, where, *_: (where[p] * seqs + s, 0)
    row_at = lambda s, p, *_: (0, s * pieces + p)
    total = seqs * length
    return pl.pallas_call(
        partial(forward_kernel, channels),
        name="scan_forward",
        grid_spec=pltpu.PrefetchScalarGridSpec(
            num_scalar_prefetch=3,
            grid=(seqs, pieces),
            in_specs=[
                pl.BlockSpec((STRETCH, pre.shape[1]), at),
                pl.BlockSpec((1, STRETCH), row_at),
                whole(spread.shape), whole(kernel.shape), whole(offset.shape), whole(skip.shape),
                whole(shared_kernel.shape), whole(shared_offset.shape), whole(bias.shape), whole(rate.shape),
            ],
            out_specs=[
                pl.BlockSpec((STRETCH, channels), at),
                pl.BlockSpec((STRETCH, channels), at),
                pl.BlockSpec((1, 1, width // 2, channels), lambda s, p, *_: (s, p, 0, 0)),
                pl.BlockSpec((8, STRETCH), row_at),
            ],
            scratch_shapes=[
                pltpu.VMEM((24, channels), F32), pltpu.VMEM((24, width), F32), pltpu.VMEM((width // 2, channels), F32),
            ],
        ),
        out_shape=[
            jax.ShapeDtypeStruct((total, channels), F32),
            jax.ShapeDtypeStruct((total, channels), BF16),
            jax.ShapeDtypeStruct((seqs, pieces, width // 2, channels), BF16),
            jax.ShapeDtypeStruct((8, total), F32),
        ],
        compiler_params=pltpu.CompilerParams(dimension_semantics=("arbitrary", "arbitrary")),
        cost_estimate=cost(20e9, 40e6),
    )(slots, segments, spans, pre, seg_row, spread, kernel, offset, skip, shared_kernel, shared_offset, bias, rate)


def coupling_step(slots, seqs, gated, grad, gain):
    total, channels = gated.shape
    pieces = total // STRETCH // seqs
    at = lambda s, p, where: (where[p] * seqs + s, 0)
    return pl.pallas_call(
        coupling_kernel,
        name="coupling",
        grid_spec=pltpu.PrefetchScalarGridSpec(
            num_scalar_prefetch=1,
            grid=(seqs, pieces),
            in_specs=[pl.BlockSpec((STRETCH, channels), at), pl.BlockSpec((STRETCH, channels), at), whole(gain.shape)],
            out_specs=pl.BlockSpec((8, STRETCH), lambda s, p, *_: (0, s * pieces + p)),
        ),
        out_shape=jax.ShapeDtypeStruct((8, total), F32),
        compiler_params=limits(8),
        cost_estimate=cost(2e9, 12e6),
    )(slots, gated, grad, gain)


def norm_step(slots, seqs, gated, scale_row, gain):
    total, channels = gated.shape
    pieces = total // STRETCH // seqs
    at = lambda s, p, where: (where[p] * seqs + s, 0)
    return pl.pallas_call(
        norm_kernel,
        name="norm_rows",
        grid_spec=pltpu.PrefetchScalarGridSpec(
            num_scalar_prefetch=1,
            grid=(seqs, pieces),
            in_specs=[
                pl.BlockSpec((STRETCH, channels), at),
                pl.BlockSpec((1, STRETCH), lambda s, p, *_: (0, s * pieces + p)),
                whole(gain.shape),
            ],
            out_specs=pl.BlockSpec((STRETCH, channels), at),
        ),
        out_shape=jax.ShapeDtypeStruct((total, channels), BF16),
        compiler_params=limits(8),
        cost_estimate=cost(1e9, 8e6),
    )(slots, gated, scale_row, gain)


def scan_backward(
    start, count, done, slots, segments, spans, pre, grad, y, states, seg_row, scale_row, pull_row, spread, kernel, offset, skip, gain,
    shared_kernel, shared_offset, bias, rate,
):
    seqs, length = segments.shape
    pieces = length // STRETCH
    channels = kernel.shape[1]
    width = shared_kernel.shape[1]
    total = seqs * length
    piece_at = lambda p: pieces - 1 - p
    at = lambda s, p, where, *_: (where[piece_at(p)] * seqs + s + start, 0)
    row_at = lambda s, p, *_: (0, (s + start) * pieces + piece_at(p))
    halo_at = lambda s, p, where, *_: (
        (where[jnp.maximum(piece_at(p) - 1, 0)] * seqs + s + start) * (STRETCH // 32) + STRETCH // 32 - 1, 0
    )
    plain_at = lambda s, p, *_: ((s + start) * pieces + piece_at(p), 0)
    return pl.pallas_call(
        partial(backward_kernel, channels, start),
        name="scan_backward",
        grid_spec=pltpu.PrefetchScalarGridSpec(
            num_scalar_prefetch=3,
            grid=(count, pieces),
            in_specs=[
                pl.BlockSpec((STRETCH, pre.shape[1]), at),
                pl.BlockSpec((32, pre.shape[1]), halo_at),
                pl.BlockSpec((STRETCH, channels), at),
                pl.BlockSpec((STRETCH, channels), at),
                pl.BlockSpec((1, 1, width // 2, channels), lambda s, p, *_: (s + start, piece_at(p), 0, 0)),
                pl.BlockSpec((1, STRETCH), row_at),
                pl.BlockSpec((1, STRETCH), row_at),
                pl.BlockSpec((1, STRETCH), row_at),
                whole(spread.shape), whole(kernel.shape), whole(offset.shape), whole(skip.shape), whole(gain.shape),
                whole(shared_kernel.shape), whole(shared_offset.shape), whole(bias.shape), whole(rate.shape),
            ]
            + ([pl.BlockSpec(memory_space=pl.ANY)] * 3 + [whole(values.shape) for values in done[3:]] if start else []),
            out_specs=[
                pl.BlockSpec((STRETCH, 2 * channels), at),
                pl.BlockSpec((STRETCH, width), plain_at),
                pl.BlockSpec((STRETCH, LANES), at),
                whole((8, channels)),
                whole((8, LANES)),
                whole((8, width)),
            ],
            scratch_shapes=[
                pltpu.VMEM((24, channels), F32), pltpu.VMEM((width // 2, channels), F32), pltpu.VMEM((24, width), F32),
            ],
        ),
        out_shape=[
            jax.ShapeDtypeStruct((total, 2 * channels), BF16),
            jax.ShapeDtypeStruct((total, width), BF16),
            jax.ShapeDtypeStruct((total, LANES), BF16),
            jax.ShapeDtypeStruct((8, channels), F32),
            jax.ShapeDtypeStruct((8, LANES), F32),
            jax.ShapeDtypeStruct((8, width), F32),
        ],
        input_output_aliases={20: 0, 21: 1, 22: 2} if start else {},
        compiler_params=pltpu.CompilerParams(dimension_semantics=("arbitrary", "arbitrary")),
        cost_estimate=cost(22e9 * count, 30e6 * count),
    )(
        slots, segments, spans, pre, pre, grad, y, states, seg_row, scale_row, pull_row, spread, kernel, offset, skip, gain,
        shared_kernel, shared_offset, bias, rate, *(done if start else ()),
    )


def ring_order(devices, across):
    depth = devices // across
    if devices % across or across < 2 or depth < 2 or depth % 2 and across % 2:
        return list(range(devices))
    if across == 2:
        return [z * 2 for z in range(depth)] + [z * 2 + 1 for z in reversed(range(depth))]
    walk = [z * across for z in range(depth)]
    for turn, z in enumerate(reversed(range(depth))):
        xs = range(1, across)
        walk += [z * across + x for x in (xs if turn % 2 == 0 else reversed(xs))]
    return walk


class Numbers:
    def __init__(self, axis, size, columns):
        self.names = {name: i for i, name in enumerate(columns)}
        table = jnp.asarray([[values(i) for values in columns.values()] for i in range(size)], jnp.int32)
        row = lax.dynamic_slice(table, (lax.axis_index(axis), 0), (1, len(columns)), allow_negative_indices=False)
        self.row = lax.optimization_barrier(row)

    def __getitem__(self, name):
        return self.row[0, self.names[name]]


def rows_at(values, start, count, axis=0):
    starts = [start if i == axis else 0 for i in range(values.ndim)]
    sizes = [count if i == axis else size for i, size in enumerate(values.shape)]
    return lax.dynamic_slice(values, starts, sizes, allow_negative_indices=False)


def put_at(values, update, row, column=0):
    return lax.dynamic_update_slice(values, update, (row, column), allow_negative_indices=False)


WAYS = (1, -1)


class Ring:
    def __init__(self, devices, across, height, halved):
        self.size = n = devices
        self.order = order = ring_order(devices, across)
        self.block = block = height // (2 * n)
        self.eighth = eighth = halved // 8
        onward = [(order[i], order[(i + 1) % n]) for i in range(n)]
        self.pairs = {1: onward, -1: [(b, a) for a, b in onward]}
        columns = {}
        for step in range(n):
            for kind, lead in (("add", 0), ("store", 1)):
                for way in WAYS:
                    columns[kind, step, way] = lambda i, w=way, s=step, d=lead: (0 if w > 0 else n) + (
                        order.index(i) + w * (d - s)
                    ) % n
            for way in WAYS:

                def eighth_of(i, w=way, s=step):
                    origin = order[(order.index(i) - w * s) % n]
                    return 2 * ((origin & 1) * 4 + (origin >> 1 & 1) * 2 + (origin >> 2 & 1)) + (0 if w > 0 else 1)

                columns["side", step, way] = eighth_of
        for way in WAYS:
            columns["first", way] = lambda i, w=way: (0 if w > 0 else n * block) + order.index(i) * block
        for bit in range(3):
            columns["keep", bit] = lambda i, k=bit: (i >> k & 1) * (halved >> k + 1)
            columns["give", bit] = lambda i, k=bit: (1 - (i >> k & 1)) * (halved >> k + 1)
        self.at = Numbers("dp", n, columns)

    def exchange(self, values, bit):
        return lax.ppermute(values, "dp", [(i, i ^ (1 << bit)) for i in range(self.size)])

    def add(self, parts, arrived, step):
        shape = (self.block, parts.shape[1])
        first = self.at.names["add", step, 1]

        def kernel(row, one, two, came_one, came_two, out_one, out_two):
            out_one[...] = (came_one[...].astype(F32) + one[...].astype(F32)).astype(BF16)
            out_two[...] = (came_two[...].astype(F32) + two[...].astype(F32)).astype(BF16)

        return pl.pallas_call(
            kernel,
            name="ring_add",
            grid_spec=pltpu.PrefetchScalarGridSpec(
                num_scalar_prefetch=1,
                grid=(1,),
                in_specs=[
                    pl.BlockSpec(shape, lambda i, row: (row[0, first], 0)),
                    pl.BlockSpec(shape, lambda i, row: (row[0, first + 1], 0)),
                    whole(shape),
                    whole(shape),
                ],
                out_specs=[whole(shape), whole(shape)],
            ),
            out_shape=[jax.ShapeDtypeStruct(shape, BF16)] * 2,
            compiler_params=limits(8),
            cost_estimate=cost(1e6, 4e6),
        )(self.at.row, parts, parts, *arrived)

    def store(self, sums, held, step):
        block, height = self.block, self.eighth // 2
        channels, model = sums[0].shape[1], sums[2].shape[1]
        first, side = self.at.names["store", step, 1], self.at.names["side", step, 1]

        def kernel(row, one, two, *rest):
            gate, inner, out = rest[3:]
            for way, source in enumerate((one, two)):

                @pl.when(pl.program_id(0) == way)
                def _():
                    gate[...] = source[:block, :channels].astype(F32)
                    inner[...] = source[:block, channels:].astype(F32)
                    out[...] = source[block:, :].astype(F32)

        low_spec = pl.BlockSpec((block, channels), lambda i, row: (row[0, first + i], 0))
        return pl.pallas_call(
            kernel,
            name="ring_store",
            grid_spec=pltpu.PrefetchScalarGridSpec(
                num_scalar_prefetch=1,
                grid=(2,),
                in_specs=[whole(held[0].shape), whole(held[1].shape)] + [pl.BlockSpec(memory_space=pl.ANY)] * 3,
                out_specs=[low_spec, low_spec, pl.BlockSpec((height, model), lambda i, row: (row[0, side + i], 0))],
            ),
            out_shape=[jax.ShapeDtypeStruct(values.shape, F32) for values in sums],
            input_output_aliases={3: 0, 4: 1, 5: 2},
            compiler_params=limits(12),
            cost_estimate=cost(1e6, 6e6),
        )(self.at.row, *held, *sums)

    def all_reduce(self, parts, sums, fillers, finished):
        n, fillers = self.size, list(fillers)

        def send(held):
            arrived = [lax.ppermute(values, "dp", self.pairs[way]) for way, values in zip(WAYS, held)]
            made = fillers.pop(0)(lambda values: after(values, *held)) if fillers else []
            return lax.optimization_barrier((*arrived, *made))[:2]

        held = [rows_at(parts, self.at["first", way], self.block) for way in WAYS]
        for step in range(1, n):
            held = self.add(parts, send(held), step)
        extra = finished()
        half = extra.shape[0] // 2
        held = [jnp.concatenate([held[0], extra[:half]], axis=0), jnp.concatenate([held[1], extra[half:]], axis=0)]
        for step in range(n):
            if step:
                held = send(held)
            sums = self.store(sums, held, step)
        for filler in fillers:
            filler(lambda values: values)
        return sums


class Ranks:
    def __init__(self, size, slab):
        self.size, self.along = size, size // 2
        along = self.along

        def owner(i, slot):
            other, place = divmod(slot, along)
            return ((i - 2 * place) % size) ^ other

        def slot(i, owner):
            other = (owner ^ i) & 1
            return other * along + (i - (owner ^ other)) % size // 2

        columns = {}
        for k in range(size):
            columns["owner", k] = lambda i, k=k: owner(i, k)
        for k in range(size):
            columns["slot", k] = lambda i, k=k: slot(i, k)
        columns["slab"] = lambda i: i * slab
        self.at = Numbers("tensor", size, columns)

    def core(self, values):
        return lax.ppermute(values, "tensor", [(i, i ^ 1) for i in range(self.size)])

    def shift(self, values, places):
        return lax.ppermute(values, "tensor", [(i, (i + 2 * places) % self.size) for i in range(self.size)])

    def gather(self, own):
        held = [own]
        for _ in range(1, self.along):
            held.append(self.shift(held[-1], 1))
        return jnp.concatenate(held + [self.core(values) for values in held], axis=0)


def total_over(values, axis, size):
    step = 1
    while step < size:
        values = values + lax.ppermute(values, axis, [(i, i ^ step) for i in range(size)])
        step *= 2
    return values


def after(values, *earlier):
    return lax.optimization_barrier((values, *earlier))[0]


def body(
    ranks, dps, tokens, pre_gain, weight_gate, weight_inner, weight_step, weight_shared, conv_kernel, conv_offset,
    shared_kernel, shared_offset, step_bias, log_rate, skip_gain, gate_gain, weight_out, cotangent, segments, image_span,
):
    seqs, rows, model = tokens.shape
    length = rows * ranks
    pieces = length // STRETCH
    total = seqs * length
    channels = weight_gate.shape[1]
    heads = step_bias.shape[0]
    inner_width = channels * ranks
    width = weight_shared.shape[1]
    slab = width // ranks
    group = Ranks(ranks, slab)
    local = rows == STRETCH

    mixer = (token_of(jnp.arange(STRETCH))[:, None] == jnp.arange(STRETCH)[None, :]).astype(BF16)

    def reorder(values, dims=NN):
        blocks = values.reshape(-1, STRETCH, values.shape[-1])
        moved = [lax.dot_general(mixer, blocks[i], dims, preferred_element_type=BF16) for i in range(blocks.shape[0])]
        return jnp.concatenate(moved, axis=0).reshape(values.shape)

    def gather(values):
        if local:
            return group.gather(values.reshape(seqs * rows, model))
        every = lax.all_gather(values, "tensor", axis=1, tiled=True).reshape(seqs, pieces, STRETCH, model)
        return reorder(jnp.moveaxis(every, 1, 0)).reshape(total, model)

    def scatter(values):
        every = jnp.moveaxis(reorder(values, TN).reshape(pieces, seqs, STRETCH, model), 0, 1).reshape(seqs, length, model)
        return lax.psum_scatter(every, "tensor", scatter_dimension=1, tiled=True).astype(F32)

    def slabs(values):
        blocks = values.reshape(seqs, pieces, STRETCH, values.shape[-1])
        if not local:
            return jnp.moveaxis(blocks, 1, 0).reshape(values.shape)
        return jnp.concatenate(
            [rows_at(blocks, group.at["owner", slot], 1, 1)[:, 0] for slot in range(ranks)], axis=0
        ).reshape(values.shape)

    slots = jnp.arange(pieces, dtype=jnp.int32)
    if local:
        first = group.at.names["slot", 0]
        slots = group.at.row[0, first : first + pieces]
    own_low = reorder(tokens) if local else tokens
    cot_low = reorder(cotangent) if local else cotangent
    own = own_low.astype(F32)
    row_scale = lax.rsqrt(jnp.mean(own * own, axis=2, keepdims=True) + EPSILON)
    normed_low = (own * row_scale * pre_gain[None, None, :]).astype(BF16)
    tail = min(512, channels) - width - heads
    weight_ss = jnp.concatenate([weight_shared, weight_step, jnp.zeros((model, tail), BF16)], axis=1)
    pad_heads = lambda values: jnp.pad(values, (0, LANES - heads))[None, :]
    bias = pad_heads(step_bias)
    rate = pad_heads(-jnp.exp(log_rate))
    skip = jnp.repeat(skip_gain, HEAD)[None, :]
    heads_of = (jnp.arange(LANES)[:, None] == (jnp.arange(channels) // HEAD)[None, :]).astype(BF16)
    spread = jnp.concatenate([heads_of, heads_of], axis=0)
    seg_row = jnp.swapaxes(segments.astype(F32).reshape(seqs, pieces, 8, STRETCH // 8), 2, 3).reshape(1, total)
    offset_row, shared_offset_row = conv_offset[None, :], shared_offset[None, :]
    gain_row = gate_gain[None, :]

    blocked = local and ranks == 4
    if blocked:
        own_rows, cot_rows = normed_low.reshape(seqs * rows, model), cot_low.reshape(seqs * rows, model)
        far_rows = group.shift(own_rows, 1)
        far_cot = group.shift(after(cot_rows, own_rows), 1)
        weights = (weight_gate, weight_inner, weight_ss)
        first = fill_rows(own_rows, group.core(own_rows), weights, NN, None)
        first_cot = fill_rows(cot_rows, group.core(cot_rows), (weight_out,), NT, None)
        far_rows = after(far_rows, first[0], first_cot[0])
        pre, normed_in = fill_rows(far_rows, group.core(far_rows), weights, NN, first)
    else:
        normed_in, cot_full = gather(normed_low), gather(cot_low)
        weights = jnp.concatenate([weight_gate, weight_inner, weight_ss], axis=1)
        pre = lax.dot_general(normed_in, weights, NN, preferred_element_type=F32)
        grad = lax.dot_general(cot_full, weight_out, NT, preferred_element_type=F32)
    y, gated, states, squares = scan_forward(
        slots, segments, image_span, pre, seg_row, spread, conv_kernel, offset_row, skip, shared_kernel, shared_offset_row,
        bias, rate,
    )
    if blocked:
        far_cot = after(far_cot, squares)
        grad, cot_full = fill_rows(far_cot, group.core(far_cot), (weight_out,), NT, first_cot)
    coupling = coupling_step(slots, seqs, gated, grad, gain_row)
    sums = total_over(jnp.concatenate([squares[0:1], coupling[0:1]], axis=0), "tensor", ranks)
    scale_row = lax.rsqrt(sums[0:1] / inner_width + EPSILON)
    pull_row = scale_row * scale_row * scale_row / inner_width * sums[1:2]
    normed_out = norm_step(slots, seqs, gated, scale_row, gain_row)

    def backward(start, count, done, pull):
        return scan_backward(
            start, count, done, slots, segments, image_span, pre, grad, y, states, seg_row, scale_row, pull, spread,
            conv_kernel, offset_row, skip, gain_row, shared_kernel, shared_offset_row, bias, rate,
        )

    out_product = lambda left: lax.dot_general(left, cot_full, TN, preferred_element_type=BF16)
    made = {}
    ringed = dps == 8 and seqs > 1 and model == 2 * channels
    if ringed:
        ring = Ring(dps, ranks // 2, model, channels)
        join = lambda mine, arrived: (mine.astype(F32) + arrived.astype(F32)).astype(BF16)
        part_of = lambda values, kind, bit, axis=0: rows_at(values, ring.at[kind, bit], channels >> bit + 1, axis)
        given = out_product(part_of(normed_out, "give", 0, 1))
        arrived = ring.exchange(given, 0)
        kept = out_product(after(part_of(normed_out, "keep", 0, 1), given))
        low, shared_part, step_low, channel_grads, head_grads, shared_grads = backward(0, seqs, None, after(pull_row, kept))
        kept = join(after(kept, low), arrived)
        given = part_of(kept, "give", 1)
        arrived = ring.exchange(given, 1)
        low_part = lax.dot_general(normed_in, after(low, given), TN, preferred_element_type=BF16)
        made["quarter"] = part_of(kept, "keep", 1), arrived
    else:
        out_sum = lax.psum(out_product(normed_out), "dp")
        low, shared_part, step_low, channel_grads, head_grads, shared_grads = backward(0, seqs, None, pull_row)
        low_part = lax.dot_general(normed_in, low, TN, preferred_element_type=BF16)

    cut = total // 2 if local else 0
    half = ranks // 2
    weight_low = jnp.concatenate([weight_gate, weight_inner], axis=1)
    weight_side = jnp.concatenate(
        [
            rows_at(weight_shared, group.at["slab"], slab, 1),
            weight_step,
            jnp.zeros((model, LANES - slab - heads), BF16),
        ],
        axis=1,
    )
    by_rank = lambda values: values.reshape(-1, seqs, rows, model)

    def quarter_join(hold):
        mine, other = made["quarter"]
        kept = join(hold(mine), other)
        given = part_of(kept, "give", 2)
        made["eighth"] = part_of(kept, "keep", 2), ring.exchange(given, 2)
        return [given]

    def finished(hold=lambda values: values):
        if "finished" not in made:
            made["finished"] = join(hold(made["eighth"][0]), made["eighth"][1])
        return made["finished"]

    def finish(hold):
        return [finished(hold)] if ringed else []

    def columns_out(hold):
        columns = jnp.moveaxis(hold(shared_part).reshape(total, ranks, slab), 1, 0)
        columns = jnp.concatenate([rows_at(columns, group.at["owner", slot], 1) for slot in range(ranks)], axis=0)
        made["columns"] = columns[:half], group.core(columns[half:])
        return [columns] + (quarter_join(hold) if ringed else [])

    def columns_in(hold):
        shared_low = slabs(take_rows("columns", hold).astype(BF16))
        made["side"] = jnp.concatenate([shared_low, step_low[:, :heads], jnp.zeros((total, LANES - slab - heads), BF16)], axis=1)
        return [made["side"]]

    def pass_on(name):
        def run(hold):
            mine, other = made[name]
            sent = [(hold(mine)[i].astype(F32) + other[i].astype(F32)).astype(BF16) for i in range(1, half)]
            made[name] = mine[0], [other[0]] + [group.shift(values, -1 - i) for i, values in enumerate(sent)]
            return sent

        return run if local or name == "columns" else lambda hold: []

    def take_rows(name, hold):
        mine, others = made[name]
        mine = hold(mine).astype(F32)
        for values in others:
            mine = mine + values.astype(F32)
        return mine

    def input_rows_of(slot):
        part = slice(slot * seqs * rows, (slot + 1) * seqs * rows) if local else slice(0, total)

        def run(hold):
            side, low_rows = lax.optimization_barrier((hold(made["side"]), low))
            summed = lax.dot_general(side[part], weight_side, NT, preferred_element_type=F32)
            summed = (summed + lax.dot_general(low_rows[part], weight_low, NT, preferred_element_type=F32)).astype(BF16)
            if local:
                made["input", slot] = by_rank(summed)[0]
                if slot >= half:
                    made["input", slot] = group.core(made["input", slot])
            else:
                made["input"] = scatter(summed), []
            return [summed]

        return run

    def input_pair(hold):
        if local:
            made["input"] = [made["input", slot] for slot in range(half)], [made["input", slot] for slot in range(half, ranks)]
        return []

    def mix_of(slots, far):
        part = slice(slots.start * seqs * rows, slots.stop * seqs * rows) if local else slice(0, total)

        def run(hold):
            product = lax.dot_general(hold(normed_out[part]), weight_out, NN, preferred_element_type=BF16)
            if not local:
                made["mixed"] = scatter(product), []
            elif far:
                made["mixed far"] = group.core(by_rank(product))
            else:
                made["mixed"] = by_rank(product), made["mixed far"]
            return [product]

        return run

    def side_product(hold):
        made["side_part"] = lax.dot_general(normed_in, hold(made["side"]), TN, preferred_element_type=BF16)
        return [made["side_part"]]

    def input_rows(hold):
        normed_grad = take_rows("input", hold)
        weighted = normed_grad * pre_gain[None, None, :]
        projection = jnp.sum(weighted * own, axis=2, keepdims=True)
        own_grad = row_scale * weighted - row_scale * row_scale * row_scale / model * own * projection
        made["pre_gain"] = jnp.sum(normed_grad * own * row_scale, axis=(0, 1))
        made["tokens_grad"] = (cot_low.astype(F32) + own_grad).astype(BF16)
        return [made["tokens_grad"], made["pre_gain"]]

    def input_order(hold):
        if local:
            made["tokens_grad"] = reorder(hold(made["tokens_grad"]), TN)
        return [made["tokens_grad"]]

    def block_rows(hold):
        made["block_out"] = (own + take_rows("mixed", hold)).astype(BF16)
        return [made["block_out"]]

    def block_order(hold):
        if local:
            made["block_out"] = reorder(hold(made["block_out"]), TN)
        return [made["block_out"]]

    def small_start(hold):
        made["small"] = jnp.concatenate(
            [jnp.pad(hold(shared_grads), ((0, 0), (0, channels - width))), made["pre_gain"].reshape(-1, channels)], axis=0
        )
        return []

    def pack(hold):
        made["small"] = jnp.concatenate(
            [channel_grads, jnp.pad(head_grads, ((0, 0), (0, channels - LANES))), made["small"]], axis=0
        )
        return []

    def spread_sum(name, axis, size, bits, kind=F32):
        partners = [0]
        for bit in bits:
            partners += [partner ^ (1 << bit) for partner in partners]

        def send(hold):
            values = hold(made[name])
            made[name] = values, [lax.ppermute(values, axis, [(i, i ^ k) for i in range(size)]) for k in partners[1:]]
            return [values]

        def receive(hold):
            values, others = made[name]
            terms = [hold(values).astype(F32)] + [other.astype(F32) for other in others]
            while len(terms) > 1:
                terms = [terms[i] + terms[i + 1] for i in range(0, len(terms), 2)]
            made[name] = terms[0].astype(kind)
            return [made[name]]

        return send, receive

    def together(*parts):
        def run(hold):
            return [value for part in parts for value in part(hold)]

        return run

    bits_of = lambda size: list(range((size - 1).bit_length()))
    tensor_send, tensor_take = spread_sum("small", "tensor", ranks, bits_of(ranks))
    small_dp = [spread_sum("small", "dp", dps, bits) for bits in (bits_of(dps)[:1], bits_of(dps)[1:])]
    if ringed:
        side_dp = [spread_sum("side_part", "dp", dps, [bit], BF16) for bit in range(3)]
    else:

        def side_whole(hold):
            made["side_part"] = lax.psum(made["side_part"], "dp")
            return []

        side_dp = [(side_whole, lambda hold: [])] + [(lambda hold: [], lambda hold: [])] * 2
    nothing = lambda hold: []
    far = [input_rows_of(slot) for slot in (range(half, ranks) if local else range(1))]
    near = [input_rows_of(slot) for slot in (range(half) if local else range(0))]
    def gather_near(hold):
        slabs_of = hold(made["side_part"])[:, :slab]
        made["gathered"] = [slabs_of]
        for _ in range(1, half):
            made["gathered"].append(group.shift(made["gathered"][-1], 1))
        return []

    def gather_far(hold):
        made["gathered"] = made["gathered"] + [group.core(hold(values)) for values in made["gathered"]]
        return []

    fillers = [
        columns_out,
        together(pass_on("columns"), mix_of(range(half, ranks), True) if local else nothing),
        together(columns_in, side_product),
        together(side_dp[0][0], *far[:1]),
        *far[1:],
        together(side_dp[0][1], side_dp[1][0], *near[:1], finish),
        *near[1:],
        together(input_pair, pass_on("input"), side_dp[1][1], side_dp[2][0], mix_of(range(half), False)),
        pass_on("mixed"),
        together(input_rows, side_dp[2][1]),
        together(small_start, tensor_send, input_order, gather_near),
        together(tensor_take, pack, small_dp[0][0], block_rows),
        together(small_dp[0][1], small_dp[1][0], block_order, gather_far),
    ]
    if ringed:
        sums = [blank((model, channels)), blank((model, channels)), blank((channels, model))]
        grads = dict(zip(("gate", "inner", "out"), ring.all_reduce(low_part, sums, fillers, finished)))
    else:
        low_sum = lax.psum(low_part, "dp").astype(F32)
        grads = {"gate": low_sum[:, :channels], "inner": low_sum[:, channels:], "out": out_sum.astype(F32)}
        for filler in fillers:
            filler(lambda values: values)
    plain = lambda values: values
    small_dp[1][1](plain)
    packed, side_sum = made["small"], made["side_part"]
    block_out, tokens_grad, grad_out = made["block_out"], made["tokens_grad"], grads["out"]
    gathered = jnp.stack(made["gathered"])
    grad_shared = jnp.concatenate(
        [rows_at(gathered, group.at["slot", owner], 1)[0] for owner in range(ranks)], axis=1
    ).astype(F32)
    grad_step = side_sum[:, slab : slab + heads].astype(F32)

    shared_sums = packed[16:24, :width]
    return (
        block_out,
        tokens_grad,
        packed[24:].reshape(model),
        grads["gate"],
        grads["inner"],
        grad_step,
        grad_shared,
        packed[0:4],
        packed[4],
        shared_sums[0:4],
        shared_sums[4],
        packed[9, :heads],
        packed[8, :heads],
        jnp.sum(packed[5].reshape(heads, HEAD), axis=1),
        packed[6],
        grad_out,
    )


def solution(mesh):
    placed = (
        P("dp", "tensor", None),
        P(),
        P(None, "tensor"),
        P(None, "tensor"),
        P(None, "tensor"),
        P(),
        P(None, "tensor"),
        P("tensor"),
        P(),
        P(),
        P("tensor"),
        P("tensor"),
        P("tensor"),
        P("tensor"),
        P("tensor", None),
        P("dp", "tensor", None),
        P("dp", None),
        P("dp", None),
    )
    return jax.shard_map(
        partial(body, mesh.shape["tensor"], mesh.shape["dp"]),
        mesh=mesh,
        in_specs=placed,
        out_specs=(
            P("dp", "tensor", None),
            P("dp", "tensor", None),
            P(),
            P(None, "tensor"),
            P(None, "tensor"),
            P(None, "tensor"),
            P(),
            P(None, "tensor"),
            P("tensor"),
            P(),
            P(),
            P("tensor"),
            P("tensor"),
            P("tensor"),
            P("tensor"),
            P("tensor", None),
        ),
        check_vma=False,
    )
```

time: 823 us -> 613 us (0.74)
  waiting for transfers between devices: 219 us -> 128 us
  starting transfers between devices: 143 us -> 76.3 us
  matrix products: 150 us -> 100 us
  Pallas kernels: 133 us -> 176 us
  between operations: 27.4 us -> 2.22 us
  local copies, waits for them, and re-layouts: 101 us -> 80.5 us
    ppermute x124 -> x57, waiting for transfers between devices: 199 us -> 125 us  [the longest x28 89 us: send(): lax.ppermute(values, 'dp', self.pairs[way])]
    dynamic_update_slice x49 -> x0, local copies, waits for them, and re-layouts: 52.8 us -> none  [the longest x33 28.2 us: put(): lax.dynamic_update_slice(grads[name], values[:, start:start + count], (ro...]
    ppermute x124 -> x57, starting transfers between devices: 128 us -> 75.8 us  [the longest x28 52.9 us: send(): lax.ppermute(values, 'dp', self.pairs[way])]
    dot_general x14 -> x22, matrix products: 150 us -> 100 us  [the longest x4 30.6 us: run(): lax.dot_general(low_rows[part], weight_low, NT, preferred_element_type=F32)]
    pallas_call x3 -> x25, Pallas kernels: 100 us -> 150 us  [the longest x1 63.6 us: scan_backward(): pl.pallas_call(partial(backward_kernel, channels, start), name='scan_back...]
    unnamed x95 -> x131, local copies, waits for them, and re-layouts: 10.6 us -> 32.6 us
    dynamic_slice x6 -> x8, local copies, waits for them, and re-layouts: 0.93 us -> 17.6 us  [the longest x6 16.2 us: rows_at(): lax.dynamic_slice(values, starts, sizes, allow_negative_indices=False)]
    ppermute x17 -> x2, starting transfers between devices: 13.8 us -> 0.53 us  [total_over(): lax.ppermute(values, axis, [(i, i ^ step) for i in range(size)])]
  transfers between devices with their start and end apart: 147 -> 59, of which waited for: 76 -> 24; matrix products, arithmetic and copies ran while one was open for 32% -> 29% of each run, Pallas kernels for 4% -> 26%
where the time goes in v2:
time: 613 us; the launch traced here: 609 us
  Pallas kernels  176 us (29%)
  waiting for transfers between devices  128 us (21%)
  matrix products  100 us (16%)
  local copies, waits for them, and re-layouts  80.5 us (13%)
  starting transfers between devices  76.3 us (12%)
  other arithmetic  45.2 us (7%)
    ppermute x28, waiting for transfers between devices, send(): lax.ppermute(values, 'dp', self.pairs[way])  89 us
    pallas_call x1, Pallas kernels, scan_backward(): pl.pallas_call(partial(backward_kernel, channels, start), name='scan_back...  63.6 us
    pallas_call x4, Pallas kernels, fill_rows(): pl.pallas_call(partial(fill_kernel, dims, spans, 1 if second else 0), nam...  57 us
    ppermute x28, starting transfers between devices, send(): lax.ppermute(values, 'dp', self.pairs[way])  52.9 us
    unnamed x131, local copies, waits for them, and re-layouts  32.6 us
    dot_general x4, matrix products, run(): lax.dot_general(low_rows[part], weight_low, NT, preferred_element_type=F32)  30.6 us
    ppermute x10, waiting for transfers between devices, send(): lax.ppermute(values, axis, [(i, i ^ k) for i in range(size)])  28 us
    pallas_call x1, Pallas kernels, scan_forward(): pl.pallas_call(partial(forward_kernel, channels), name='scan_forward', gr...  26.8 us
  transfers between devices with their start and end apart: 59, of which 24 were waited for; matrix products, arithmetic and copies ran while one was open for 29% of the time, Pallas kernels for 26%

profile of v2, /device:TPU:0, one launch (start us, length us, event | category | flops | bytes accessed | tf_op | source)
XLA Modules:
  0.0 608.8 jit_solution(2141614809996087769)
XLA Ops:
  18.4 9.8 %fill_rows.5 = (f32[2048,1024]{1,0:T(8,128)S(1)}, bf16[2048,2048]{1,0:T(8,128)(2,1)}) custom-call(bf16[512,2048]{1,0:T(8,128)(2,1)} %pad_maximum_fusion.own, bf16[512,2048]{1,0:T(8,128)(2,1)} %collective-permute-done.2.other, bf16[1024,2048]{1,0:T(8,128)(2,1)S(1)} %copy-done.13), custom_call_target="tpu_custom_call" | custom-call | flops 4294967296 | bytes 6291456 | tf_op jit(solution)/shard_map/fill_rows/pallas_call | solution.py:383
  31.6 19.4 %fill_rows.4 = (f32[2048,2560]{1,0:T(8,128)}, bf16[2048,2048]{1,0:T(8,128)(2,1)}) custom-call(bf16[512,2048]{1,0:T(8,128)(2,1)} %multiply_convert_fusion.own, bf16[512,2048]{1,0:T(8,128)(2,1)} %collective-permute-done.1.other, bf16[2048,1024]{1,0:T(8,128)(2,1)S(1)} %copy-done.8, bf16[2048,1024]{1,0:T(8,128)(2,1)S(1)} %copy-done.10, ...), custom_call_target="tpu_custom_call" | custom-call | flops 10737418240 | bytes 9437184 | tf_op jit(solution)/shard_map/fill_rows/pallas_call | solution.py:383
  51.0 8.3 %collective-permute-done.own = bf16[512,2048]{1,0:T(8,128)(2,1)} collective-permute-done((bf16[512,2048]{1,0:T(8,128)(2,1)}, bf16[512,2048]{1,0:T(8,128)(2,1)}, u32[]{:S(2)}, u32[]{:S(2)}) %collective-permute-start) | collective-permute-done | bytes 2097184 | tf_op jit(solution)/shard_map/ppermute | solution.py:730
  69.8 19.5 %fill_rows.6 = (f32[2048,2560]{1,0:T(8,128)}, bf16[2048,2048]{1,0:T(8,128)(2,1)}) custom-call(bf16[512,2048]{1,0:T(8,128)(2,1)} %collective-permute-done.own, bf16[512,2048]{1,0:T(8,128)(2,1)} %collective-permute-done.3.other, bf16[2048,1024]{1,0:T(8,128)(2,1)S(1)} %copy-done.9, ...), custom_call_target="tpu_custom_call", output_to_operand_aliasing={{0}: (5, {}), {1}: (6, {})} | custom-call | flops 10737418240 | bytes 9437184 | tf_op jit(solution)/shard_map/fill_rows/pallas_call | solution.py:383
  89.3 26.8 %scan_forward.1 = (f32[2048,1024]{1,0:T(8,128)}, bf16[2048,1024]{1,0:T(8,128)(2,1)}, bf16[2,4,128,1024]{3,2,1,0:T(8,128)(2,1)}, f32[8,2048]{1,0:T(8,128)}) custom-call(s32[4]{0:T(128)} %slice_bitcast_fusion.5.slots, s32[2,1024]{1,0:T(2,128)} %seg_sm.3, s32[2,2]{1,0:T(2,128)} %span_sm.3, f32[2048,2560]{1,0:T(8,128)} %get-tuple-element.152.pre.halo, ...), custom_call_target="tpu_custom_call" | custom-call | flops 20000000000 | bytes 40000000 | tf_op jit(solution)/shard_map/scan_forward/pallas_call | solution.py:416
  131.8 8.4 %fill_rows.7 = (f32[2048,1024]{1,0:T(8,128)S(1)}, bf16[2048,2048]{1,0:T(8,128)(2,1)}) custom-call(bf16[512,2048]{1,0:T(8,128)(2,1)} %collective-permute-done.4.own, bf16[512,2048]{1,0:T(8,128)(2,1)S(1)} %collective-permute-done.5.other, bf16[1024,2048]{1,0:T(8,128)(2,1)S(1)} %copy-done.14, ...), custom_call_target="tpu_custom_call", output_to_operand_aliasing={{0}: (3, {}), {1}: (4, {})} | custom-call | flops 4294967296 | bytes 6291456 | tf_op jit(solution)/shard_map/fill_rows/pallas_call | solution.py:383
  155.1 11.4 %fusion.19 = bf16[512,2048]{1,0:T(8,128)(2,1)} fusion(bf16[2048,2048]{1,0:T(8,128)(2,1)} %get-tuple-element.162, bf16[2048,1024]{1,0:T(8,128)(2,1)S(1)} %norm_rows.1, s32[]{:T(128)} %bitcast.13), kind=kOutput, calls=%fused_computation.39 | convolution fusion | flops 4294967296 | bytes 12582916 | tf_op jit(solution)/shard_map/dot_general | solution.py:847
  168.0 5.7 fusion.80
  173.8 63.6 %scan_backward.1 = (bf16[2048,2048]{1,0:T(8,128)(2,1)}, bf16[2048,256]{1,0:T(8,128)(2,1)}, bf16[2048,128]{1,0:T(8,128)(2,1)}, f32[8,1024]{1,0:T(8,128)}, f32[8,128]{1,0:T(8,128)}, /*index=5*/f32[8,256]{1,0:T(8,128)}) custom-call(s32[4]{0:T(128)} %slice_bitcast_fusion.5.slots, s32[2,1024]{1,0:T(2,128)} %seg_sm.3, s32[2,2]{1,0:T(2,128)} %span_sm.3, ...), custom_call_target="tpu_custom_call" | custom-call | flops 44000002048 | bytes 60000000 | tf_op jit(solution)/shard_map/scan_backward/pallas_call | solution.py:507
  238.6 5.0 fusion.75
  250.4 19.8 %fusion.81.one.two = bf16[2048,2048]{1,0:T(8,128)(2,1)S(1)} fusion(bf16[2048,2048]{1,0:T(8,128)(2,1)S(1)} %bitcast.168, bf16[2048,2048]{1,0:T(8,128)(2,1)S(1)} %copy-done.52), kind=kOutput, calls=%fused_computation.176 | convolution fusion | flops 17179869184 | bytes 25165824 | tf_op jit(solution)/shard_map/dot_general | solution.py:861
  280.1 4.5 dynamic-slice_bitcast_fusion.7
  294.8 6.1 fusion.82
  300.9 13.9 %collective-permute-done.12.came_one = bf16[128,2048]{1,0:T(8,128)(2,1)S(1)} collective-permute-done((bf16[128,2048]{1,0:T(8,128)(2,1)S(1)}, bf16[128,2048]{1,0:T(8,128)(2,1)S(1)}, u32[]{:S(2)}, u32[]{:S(2)}) %collective-permute-start.12) | collective-permute-done | bytes 524320 | tf_op jit(solution)/shard_map/ppermute | solution.py:686
  317.8 10.4 %collective-permute-start.15 = (bf16[128,2048]{1,0:T(8,128)(2,1)S(1)}, bf16[128,2048]{1,0:T(8,128)(2,1)S(1)}, u32[]{:S(2)}, u32[]{:S(2)}) collective-permute-start(bf16[128,2048]{1,0:T(8,128)(2,1)S(1)} %get-tuple-element.179), channel_id=1, source_target_pairs={{0,8},{8,16},{16,24},{24,28},{28,20},{20,12},{12,4},{4,0},{1,9},{9... | collective-permute-start | bytes 1572872 | tf_op jit(solution)/shard_map/ppermute | solution.py:686
  332.1 5.8 fusion.83
  348.2 7.6 %fusion.17 = f32[512,2048]{1,0:T(8,128)S(1)} fusion(bf16[2048,2048]{1,0:T(8,128)(2,1)} %copy-done.34, bf16[2048,2048]{1,0:T(8,128)(2,1)} %get-tuple-element.215), kind=kOutput, calls=%fused_computation.36 | convolution fusion | flops 4294967296 | bytes 14680064 | tf_op jit(solution)/shard_map/dot_general | solution.py:929
  363.9 7.6 %fusion.15 = f32[512,2048]{1,0:T(8,128)S(1)} fusion(bf16[2048,2048]{1,0:T(8,128)(2,1)} %copy-done.34, bf16[2048,2048]{1,0:T(8,128)(2,1)} %get-tuple-element.215), kind=kOutput, calls=%fused_computation.34 | convolution fusion | flops 4294967296 | bytes 14680064 | tf_op jit(solution)/shard_map/dot_general | solution.py:929
  373.6 7.1 %collective-permute-done.20.came_one = bf16[128,2048]{1,0:T(8,128)(2,1)S(1)} collective-permute-done((bf16[128,2048]{1,0:T(8,128)(2,1)S(1)}, bf16[128,2048]{1,0:T(8,128)(2,1)S(1)}, u32[]{:S(2)}, u32[]{:S(2)}) %collective-permute-start.20) | collective-permute-done | bytes 524320 | tf_op jit(solution)/shard_map/ppermute | solution.py:686
  382.0 7.7 %fusion.13 = f32[512,2048]{1,0:T(8,128)S(1)} fusion(bf16[2048,2048]{1,0:T(8,128)(2,1)} %copy-done.34, bf16[2048,2048]{1,0:T(8,128)(2,1)} %get-tuple-element.215), kind=kOutput, calls=%fused_computation.32 | convolution fusion | flops 4294967296 | bytes 14680064 | tf_op jit(solution)/shard_map/dot_general | solution.py:929
  395.4 8.2 %collective-permute-done.22.came_one = bf16[128,2048]{1,0:T(8,128)(2,1)S(1)} collective-permute-done((bf16[128,2048]{1,0:T(8,128)(2,1)S(1)}, bf16[128,2048]{1,0:T(8,128)(2,1)S(1)}, u32[]{:S(2)}, u32[]{:S(2)}) %collective-permute-start.22) | collective-permute-done | bytes 524320 | tf_op jit(solution)/shard_map/ppermute | solution.py:686
  406.7 7.6 %fusion.11 = f32[512,2048]{1,0:T(8,128)S(1)} fusion(bf16[2048,2048]{1,0:T(8,128)(2,1)} %copy-done.34, bf16[2048,2048]{1,0:T(8,128)(2,1)} %get-tuple-element.215), kind=kOutput, calls=%fused_computation.30 | convolution fusion | flops 4294967296 | bytes 14680064 | tf_op jit(solution)/shard_map/dot_general | solution.py:929
  422.4 4.7 fusion.84
  433.3 14.5 %collective-permute-done.29.two = bf16[192,2048]{1,0:T(8,128)(2,1)S(1)} collective-permute-done((bf16[192,2048]{1,0:T(8,128)(2,1)S(1)}, bf16[192,2048]{1,0:T(8,128)(2,1)S(1)}, u32[]{:S(2)}, u32[]{:S(2)}) %collective-permute-start.29) | collective-permute-done | bytes 786464 | tf_op jit(solution)/shard_map/ppermute | solution.py:686
  461.8 5.7 collective-permute-done.32.one
  467.9 14.4 %collective-permute-start.35 = (bf16[192,2048]{1,0:T(8,128)(2,1)S(1)}, bf16[192,2048]{1,0:T(8,128)(2,1)S(1)}, u32[]{:S(2)}, u32[]{:S(2)}) collective-permute-start(bf16[192,2048]{1,0:T(8,128)(2,1)S(1)} %collective-permute-done.32.one), channel_id=1, source_target_pairs={{0,8},{8,16},{16,24},{24,28},{28,20},{20,12},{12,4},{4,0},{1,9},{9... | collective-permute-start | bytes 2359304 | tf_op jit(solution)/shard_map/ppermute | solution.py:686
  482.3 9.8 %collective-permute-done.39 = bf16[2048,128]{1,0:T(8,128)(2,1)S(1)} collective-permute-done((bf16[2048,128]{1,0:T(8,128)(2,1)S(1)}, bf16[2048,128]{1,0:T(8,128)(2,1)S(1)}, u32[]{:S(2)}, u32[]{:S(2)}) %collective-permute-start.39) | collective-permute-done | bytes 524320 | tf_op jit(solution)/shard_map/ppermute | solution.py:1006
  501.2 8.5 %fusion.4 = bf16[2,256,2048]{2,1,0:T(8,128)(2,1)} fusion(bf16[2,256,2048]{2,1,0:T(8,128)(2,1)} %bitcast.71, f32[2,256,2048]{2,1,0:T(8,128)S(1)} %bitcast.170, f32[2,256]{1,0:T(2,128)S(1)} %fusion.70, f32[2048]{0:T(1024)S(1)} %copy-done.45, f32[2,256]{1,0:T(2,128)S(1)} %copy-done.43, bf16[2,256,2048]{2,1,0:T(8,128)(2,1)} %collective-permute-done.38, ...), kind=kOutput, calls=%fused_computation.6 | output fusion | flops 20974080 | bytes 14692352 | tf_op jit(solution)/shard_map/mul | solution.py:968
  520.5 5.4 collective-permute-done.40.one
  539.7 10.3 %collective-permute-done.43.one = bf16[192,2048]{1,0:T(8,128)(2,1)S(1)} collective-permute-done((bf16[192,2048]{1,0:T(8,128)(2,1)S(1)}, bf16[192,2048]{1,0:T(8,128)(2,1)S(1)}, u32[]{:S(2)}, u32[]{:S(2)}) %collective-permute-start.43) | collective-permute-done | bytes 786464 | tf_op jit(solution)/shard_map/ppermute | solution.py:686
  563.8 10.4 %collective-permute-done.49 = f32[26,1024]{1,0:T(8,128)S(1)} collective-permute-done((f32[26,1024]{1,0:T(8,128)S(1)}, f32[26,1024]{1,0:T(8,128)S(1)}, u32[]{:S(2)}, u32[]{:S(2)}) %collective-permute-start.49) | collective-permute-done | bytes 106528 | tf_op jit(solution)/shard_map/ppermute | solution.py:1006
  596.2 8.2 %collective-permute-done.54.one = bf16[192,2048]{1,0:T(8,128)(2,1)S(1)} collective-permute-done((bf16[192,2048]{1,0:T(8,128)(2,1)S(1)}, bf16[192,2048]{1,0:T(8,128)(2,1)S(1)}, u32[]{:S(2)}, u32[]{:S(2)}) %collective-permute-start.54) | collective-permute-done | bytes 786464 | tf_op jit(solution)/shard_map/ppermute | solution.py:686
  (359 shorter events, 230.6 us)
Async XLA Ops:
  10.1 21.4 %collective-permute-start.1 = (bf16[512,2048]{1,0:T(8,128)(2,1)}, bf16[512,2048]{1,0:T(8,128)(2,1)}, u32[]{:S(2)}, u32[]{:S(2)}) collective-permute-start(bf16[512,2048]{1,0:T(8,128)(2,1)} %multiply_convert_fusion.own), channel_id=1, source_target_pairs={{0,1},{1,0},{2,3},{3,2},{4,5},{5,4},{6,7},{7,6},{8,9},{9,8},{10,11... | collective-permute-start | bytes 6291464 | tf_op jit(solution)/shard_map/ppermute | solution.py:727
  10.2 49.1 %collective-permute-start = (bf16[512,2048]{1,0:T(8,128)(2,1)}, bf16[512,2048]{1,0:T(8,128)(2,1)}, u32[]{:S(2)}, u32[]{:S(2)}) collective-permute-start(bf16[512,2048]{1,0:T(8,128)(2,1)} %multiply_convert_fusion.own), channel_id=1, source_target_pairs={{0,2},{1,3},{2,0},{3,1},{4,6},{5,7},{6,4},{7,5},{8,10},{9,11},{10,... | collective-permute-start | bytes 6291464 | tf_op jit(solution)/shard_map/ppermute | solution.py:730
  59.3 56.8 %collective-permute-start.4 = (bf16[512,2048]{1,0:T(8,128)(2,1)}, bf16[512,2048]{1,0:T(8,128)(2,1)}, u32[]{:S(2)}, u32[]{:S(2)}) collective-permute-start(bf16[512,2048]{1,0:T(8,128)(2,1)} %pad_maximum_fusion.own), channel_id=1, source_target_pairs={{0,2},{1,3},{2,0},{3,1},{4,6},{5,7},{6,4},{7,5},{8,10},{9,11},{10,... | collective-permute-start | bytes 6291464 | tf_op jit(solution)/shard_map/ppermute | solution.py:730
  166.6 77.0 %collective-permute-start.8 = (bf16[512,2048]{1,0:T(8,128)(2,1)}, bf16[512,2048]{1,0:T(8,128)(2,1)S(1)}, u32[]{:S(2)}, u32[]{:S(2)}) collective-permute-start(bf16[512,2048]{1,0:T(8,128)(2,1)} %fusion.19), channel_id=1, source_target_pairs={{0,4},{4,0},{8,12},{12,8},{16,20},{20,16},{24,28},{28,24},{1,5},{5... | collective-permute-start | bytes 6291464 | tf_op jit(solution)/shard_map/ppermute | solution.py:622
  248.8 36.0 %collective-permute-start.11 = (bf16[256,2048]{1,0:T(8,128)(2,1)}, bf16[256,2048]{1,0:T(8,128)(2,1)}, u32[]{:S(2)}, u32[]{:S(2)}) collective-permute-start(bf16[256,2048]{1,0:T(8,128)(2,1)} %get-tuple-element.355), channel_id=1, source_target_pairs={{0,8},{4,12},{8,0},{12,4},{16,24},{20,28},{24,16},{28,20},{1,9},{5... | collective-permute-start | bytes 3145736 | tf_op jit(solution)/shard_map/ppermute | solution.py:622
  288.8 101.1 %collective-permute-start.25 = (bf16[128,2048]{1,0:T(8,128)(2,1)}, bf16[128,2048]{1,0:T(8,128)(2,1)}, u32[]{:S(2)}, u32[]{:S(2)}) collective-permute-start(bf16[128,2048]{1,0:T(8,128)(2,1)} %get-tuple-element.362), channel_id=1, source_target_pairs={{0,16},{4,20},{8,24},{12,28},{16,0},{20,4},{24,8},{28,12},{1,17},{... | collective-permute-start | bytes 1572872 | tf_op jit(solution)/shard_map/ppermute | solution.py:622
  292.2 22.5 %collective-permute-start.12 = (bf16[128,2048]{1,0:T(8,128)(2,1)S(1)}, bf16[128,2048]{1,0:T(8,128)(2,1)S(1)}, u32[]{:S(2)}, u32[]{:S(2)}) collective-permute-start(bf16[128,2048]{1,0:T(8,128)(2,1)S(1)} %get-tuple-element.171), channel_id=1, source_target_pairs={{0,8},{8,16},{16,24},{24,28},{28,20},{20,12},{12,4},{4,0},{1,9},{9... | collective-permute-start | bytes 1572872 | tf_op jit(solution)/shard_map/ppermute | solution.py:686
  292.7 24.3 %collective-permute-start.13 = (bf16[128,2048]{1,0:T(8,128)(2,1)S(1)}, bf16[128,2048]{1,0:T(8,128)(2,1)S(1)}, u32[]{:S(2)}, u32[]{:S(2)}) collective-permute-start(bf16[128,2048]{1,0:T(8,128)(2,1)S(1)} %get-tuple-element.172), channel_id=1, source_target_pairs={{8,0},{16,8},{24,16},{28,24},{20,28},{12,20},{4,12},{0,4},{9,1},{1... | collective-permute-start | bytes 1572872 | tf_op jit(solution)/shard_map/ppermute | solution.py:686
  294.4 34.0 %collective-permute-start.17 = (bf16[2048,64]{0,1:T(8,128)(2,1)S(1)}, bf16[2048,64]{0,1:T(8,128)(2,1)S(1)}, u32[]{:S(2)}, u32[]{:S(2)}) collective-permute-start(bf16[2048,64]{0,1:T(8,128)(2,1)S(1)} %fusion.47), channel_id=1, source_target_pairs={{0,2},{1,3},{2,0},{3,1},{4,6},{5,7},{6,4},{7,5},{8,10},{9,11},{10,... | collective-permute-start | bytes 786440 | tf_op jit(solution)/shard_map/ppermute | solution.py:730
  300.9 155.2 %collective-permute-start.34 = (bf16[2,2,256,2048]{3,2,1,0:T(8,128)(2,1)}, bf16[2,2,256,2048]{3,2,1,0:T(8,128)(2,1)}, u32[]{:S(2)}, u32[]{:S(2)}) collective-permute-start(bf16[2,2,256,2048]{3,2,1,0:T(8,128)(2,1)} %bitcast.42), channel_id=1, source_target_pairs={{0,1},{1,0},{2,3},{3,2},{4,5},{5,4},{6,7},{7,6},{8,9},{9,8},{10,11... | collective-permute-start | bytes 12582920 | tf_op jit(solution)/shard_map/ppermute | solution.py:727
  317.8 21.4 %collective-permute-start.15 = (bf16[128,2048]{1,0:T(8,128)(2,1)S(1)}, bf16[128,2048]{1,0:T(8,128)(2,1)S(1)}, u32[]{:S(2)}, u32[]{:S(2)}) collective-permute-start(bf16[128,2048]{1,0:T(8,128)(2,1)S(1)} %get-tuple-element.179), channel_id=1, source_target_pairs={{0,8},{8,16},{16,24},{24,28},{28,20},{20,12},{12,4},{4,0},{1,9},{9... | collective-permute-start | bytes 1572872 | tf_op jit(solution)/shard_map/ppermute | solution.py:686
  347.9 41.8 %collective-permute-start.24 = (bf16[2048,128]{1,0:T(8,128)(2,1)S(1)}, bf16[2048,128]{1,0:T(8,128)(2,1)S(1)}, u32[]{:S(2)}, u32[]{:S(2)}) collective-permute-start(bf16[2048,128]{1,0:T(8,128)(2,1)S(1)} %fusion.83), channel_id=1, source_target_pairs={{0,4},{4,0},{8,12},{12,8},{16,20},{20,16},{24,28},{28,24},{1,5},{5... | collective-permute-start | bytes 1572872 | tf_op jit(solution)/shard_map/ppermute | solution.py:1006
  380.7 119.0 %collective-permute-start.37 = (bf16[2,256,2048]{2,1,0:T(8,128)(2,1)}, bf16[2,256,2048]{2,1,0:T(8,128)(2,1)}, u32[]{:S(2)}, u32[]{:S(2)}) collective-permute-start(bf16[2,256,2048]{2,1,0:T(8,128)(2,1)} %bitcast.45), channel_id=1, source_target_pairs={{0,1},{1,0},{2,3},{3,2},{4,5},{5,4},{6,7},{7,6},{8,9},{9,8},{10,11... | collective-permute-start | bytes 6291464 | tf_op jit(solution)/shard_map/ppermute | solution.py:727
  380.7 46.4 %collective-permute-start.30 = (bf16[2,256,2048]{2,1,0:T(8,128)(2,1)}, bf16[2,256,2048]{2,1,0:T(8,128)(2,1)S(1)}, u32[]{:S(2)}, u32[]{:S(2)}) collective-permute-start(bf16[2,256,2048]{2,1,0:T(8,128)(2,1)} %bitcast.40), channel_id=1, source_target_pairs={{0,1},{1,0},{2,3},{3,2},{4,5},{5,4},{6,7},{7,6},{8,9},{9,8},{10,11... | collective-permute-start | bytes 6291464 | tf_op jit(solution)/shard_map/ppermute | solution.py:727
  420.9 26.9 %collective-permute-start.29 = (bf16[192,2048]{1,0:T(8,128)(2,1)S(1)}, bf16[192,2048]{1,0:T(8,128)(2,1)S(1)}, u32[]{:S(2)}, u32[]{:S(2)}) collective-permute-start(bf16[192,2048]{1,0:T(8,128)(2,1)S(1)} %pad_maximum_fusion.5.two), channel_id=1, source_target_pairs={{8,0},{16,8},{24,16},{28,24},{20,28},{12,20},{4,12},{0,4},{9,1},{1... | collective-permute-start | bytes 2359304 | tf_op jit(solution)/shard_map/ppermute | solution.py:686
  427.1 20.7 %collective-permute-start.28 = (bf16[192,2048]{1,0:T(8,128)(2,1)S(1)}, bf16[192,2048]{1,0:T(8,128)(2,1)S(1)}, u32[]{:S(2)}, u32[]{:S(2)}) collective-permute-start(bf16[192,2048]{1,0:T(8,128)(2,1)S(1)} %pad_maximum_fusion.4.one), channel_id=1, source_target_pairs={{0,8},{8,16},{16,24},{24,28},{28,20},{20,12},{12,4},{4,0},{1,9},{9... | collective-permute-start | bytes 2359304 | tf_op jit(solution)/shard_map/ppermute | solution.py:686
  432.9 66.8 %collective-permute-start.38 = (bf16[2,256,2048]{2,1,0:T(8,128)(2,1)}, bf16[2,256,2048]{2,1,0:T(8,128)(2,1)}, u32[]{:S(2)}, u32[]{:S(2)}) collective-permute-start(bf16[2,256,2048]{2,1,0:T(8,128)(2,1)} %add_convert_fusion.1), channel_id=1, source_target_pairs={{0,2},{1,3},{2,0},{3,1},{4,6},{5,7},{6,4},{7,5},{8,10},{9,11},{10,... | collective-permute-start | bytes 6291464 | tf_op jit(solution)/shard_map/ppermute | solution.py:730
  447.8 19.7 %collective-permute-start.32 = (bf16[192,2048]{1,0:T(8,128)(2,1)S(1)}, bf16[192,2048]{1,0:T(8,128)(2,1)S(1)}, u32[]{:S(2)}, u32[]{:S(2)}) collective-permute-start(bf16[192,2048]{1,0:T(8,128)(2,1)S(1)} %collective-permute-done.28.one), channel_id=1, source_target_pairs={{0,8},{8,16},{16,24},{24,28},{28,20},{20,12},{12,4},{4,0},{1,9},{9... | collective-permute-start | bytes 2359304 | tf_op jit(solution)/shard_map/ppermute | solution.py:686
  456.0 36.0 %collective-permute-start.39 = (bf16[2048,128]{1,0:T(8,128)(2,1)S(1)}, bf16[2048,128]{1,0:T(8,128)(2,1)S(1)}, u32[]{:S(2)}, u32[]{:S(2)}) collective-permute-start(bf16[2048,128]{1,0:T(8,128)(2,1)S(1)} %add_convert_fusion.9), channel_id=1, source_target_pairs={{0,16},{4,20},{8,24},{12,28},{16,0},{20,4},{24,8},{28,12},{1,17},{... | collective-permute-start | bytes 1572872 | tf_op jit(solution)/shard_map/ppermute | solution.py:1006
  467.5 67.7 %collective-permute-start.42 = (bf16[2,256,2048]{2,1,0:T(8,128)(2,1)}, bf16[2,256,2048]{2,1,0:T(8,128)(2,1)}, u32[]{:S(2)}, u32[]{:S(2)}) collective-permute-start(bf16[2,256,2048]{2,1,0:T(8,128)(2,1)} %fusion.9), channel_id=1, source_target_pairs={{0,2},{1,3},{2,0},{3,1},{4,6},{5,7},{6,4},{7,5},{8,10},{9,11},{10,... | collective-permute-start | bytes 6291464 | tf_op jit(solution)/shard_map/ppermute | solution.py:730
  467.9 45.4 %collective-permute-start.35 = (bf16[192,2048]{1,0:T(8,128)(2,1)S(1)}, bf16[192,2048]{1,0:T(8,128)(2,1)S(1)}, u32[]{:S(2)}, u32[]{:S(2)}) collective-permute-start(bf16[192,2048]{1,0:T(8,128)(2,1)S(1)} %collective-permute-done.32.one), channel_id=1, source_target_pairs={{0,8},{8,16},{16,24},{24,28},{28,20},{20,12},{12,4},{4,0},{1,9},{9... | collective-permute-start | bytes 2359304 | tf_op jit(solution)/shard_map/ppermute | solution.py:686
  492.1 21.3 %collective-permute-start.36 = (bf16[192,2048]{1,0:T(8,128)(2,1)S(1)}, bf16[192,2048]{1,0:T(8,128)(2,1)S(1)}, u32[]{:S(2)}, u32[]{:S(2)}) collective-permute-start(bf16[192,2048]{1,0:T(8,128)(2,1)S(1)} %collective-permute-done.33.two), channel_id=1, source_target_pairs={{8,0},{16,8},{24,16},{28,24},{20,28},{12,20},{4,12},{0,4},{9,1},{1... | collective-permute-start | bytes 2359304 | tf_op jit(solution)/shard_map/ppermute | solution.py:686
  529.8 29.7 %collective-permute-start.56 = (bf16[2048,64]{1,0:T(8,128)(2,1)}, bf16[2048,64]{1,0:T(8,128)(2,1)}, u32[]{:S(2)}, u32[]{:S(2)}) collective-permute-start(bf16[2048,64]{1,0:T(8,128)(2,1)} %get-tuple-element.277), channel_id=1, source_target_pairs={{0,2},{1,3},{2,0},{3,1},{4,6},{5,7},{6,4},{7,5},{8,10},{9,11},{10,... | collective-permute-start | bytes 786440 | tf_op jit(solution)/shard_map/ppermute | solution.py:730
  530.1 19.9 %collective-permute-start.43 = (bf16[192,2048]{1,0:T(8,128)(2,1)S(1)}, bf16[192,2048]{1,0:T(8,128)(2,1)S(1)}, u32[]{:S(2)}, u32[]{:S(2)}) collective-permute-start(bf16[192,2048]{1,0:T(8,128)(2,1)S(1)} %collective-permute-done.40.one), channel_id=1, source_target_pairs={{0,8},{8,16},{16,24},{24,28},{28,20},{20,12},{12,4},{4,0},{1,9},{9... | collective-permute-start | bytes 2359304 | tf_op jit(solution)/shard_map/ppermute | solution.py:686
  531.7 20.4 %collective-permute-start.44 = (bf16[192,2048]{1,0:T(8,128)(2,1)S(1)}, bf16[192,2048]{1,0:T(8,128)(2,1)S(1)}, u32[]{:S(2)}, u32[]{:S(2)}) collective-permute-start(bf16[192,2048]{1,0:T(8,128)(2,1)S(1)} %collective-permute-done.41.two), channel_id=1, source_target_pairs={{8,0},{16,8},{24,16},{28,24},{20,28},{12,20},{4,12},{0,4},{9,1},{1... | collective-permute-start | bytes 2359304 | tf_op jit(solution)/shard_map/ppermute | solution.py:686
  532.5 21.0 %collective-permute-start.48 = (f32[26,1024]{1,0:T(8,128)S(1)}, f32[26,1024]{1,0:T(8,128)S(1)}, u32[]{:S(2)}, u32[]{:S(2)}) collective-permute-start(f32[26,1024]{1,0:T(8,128)S(1)} %fusion.48), channel_id=1, source_target_pairs={{0,4},{4,0},{8,12},{12,8},{16,20},{20,16},{24,28},{28,24},{1,5},{5... | collective-permute-start | bytes 319496 | tf_op jit(solution)/shard_map/ppermute | solution.py:1006
  553.2 30.4 %collective-permute-start.52 = (bf16[192,2048]{1,0:T(8,128)(2,1)S(1)}, bf16[192,2048]{1,0:T(8,128)(2,1)S(1)}, u32[]{:S(2)}, u32[]{:S(2)}) collective-permute-start(bf16[192,2048]{1,0:T(8,128)(2,1)S(1)} %collective-permute-done.43.one), channel_id=1, source_target_pairs={{0,8},{8,16},{16,24},{24,28},{28,20},{20,12},{12,4},{4,0},{1,9},{9... | collective-permute-start | bytes 2359304 | tf_op jit(solution)/shard_map/ppermute | solution.py:686
  553.5 20.6 %collective-permute-start.49 = (f32[26,1024]{1,0:T(8,128)S(1)}, f32[26,1024]{1,0:T(8,128)S(1)}, u32[]{:S(2)}, u32[]{:S(2)}) collective-permute-start(f32[26,1024]{1,0:T(8,128)S(1)} %add.179), channel_id=1, source_target_pairs={{0,8},{4,12},{8,0},{12,4},{16,24},{20,28},{24,16},{28,20},{1,9},{5... | collective-permute-start | bytes 319496 | tf_op jit(solution)/shard_map/ppermute | solution.py:1006
  554.2 22.8 %collective-permute-start.50 = (f32[26,1024]{1,0:T(8,128)S(1)}, f32[26,1024]{1,0:T(8,128)S(1)}, u32[]{:S(2)}, u32[]{:S(2)}) collective-permute-start(f32[26,1024]{1,0:T(8,128)S(1)} %add.179), channel_id=1, source_target_pairs={{0,16},{4,20},{8,24},{12,28},{16,0},{20,4},{24,8},{28,12},{1,17},{... | collective-permute-start | bytes 319496 | tf_op jit(solution)/shard_map/ppermute | solution.py:1006
  557.0 22.4 %collective-permute-start.51 = (f32[26,1024]{1,0:T(8,128)S(1)}, f32[26,1024]{1,0:T(8,128)S(1)}, u32[]{:S(2)}, u32[]{:S(2)}) collective-permute-start(f32[26,1024]{1,0:T(8,128)S(1)} %add.179), channel_id=1, source_target_pairs={{0,24},{4,28},{8,16},{12,20},{16,8},{20,12},{24,0},{28,4},{1,25},{... | collective-permute-start | bytes 319496 | tf_op jit(solution)/shard_map/ppermute | solution.py:1006
  559.6 24.1 %collective-permute-start.53 = (bf16[192,2048]{1,0:T(8,128)(2,1)S(1)}, bf16[192,2048]{1,0:T(8,128)(2,1)S(1)}, u32[]{:S(2)}, u32[]{:S(2)}) collective-permute-start(bf16[192,2048]{1,0:T(8,128)(2,1)S(1)} %collective-permute-done.44.two), channel_id=1, source_target_pairs={{8,0},{16,8},{24,16},{28,24},{20,28},{12,20},{4,12},{0,4},{9,1},{1... | collective-permute-start | bytes 2359304 | tf_op jit(solution)/shard_map/ppermute | solution.py:686
  583.6 20.7 %collective-permute-start.54 = (bf16[192,2048]{1,0:T(8,128)(2,1)S(1)}, bf16[192,2048]{1,0:T(8,128)(2,1)S(1)}, u32[]{:S(2)}, u32[]{:S(2)}) collective-permute-start(bf16[192,2048]{1,0:T(8,128)(2,1)S(1)} %collective-permute-done.52.one), channel_id=1, source_target_pairs={{0,8},{8,16},{16,24},{24,28},{28,20},{20,12},{12,4},{4,0},{1,9},{9... | collective-permute-start | bytes 2359304 | tf_op jit(solution)/shard_map/ppermute | solution.py:686
  (88 other events, 965.1 us)

commit v3 on v2

--- a/solution.py
+++ b/solution.py
@@ -164,12 +164,12 @@
     y_out[...] = y
     gated = y * (gate * jax.nn.sigmoid(gate))
     gated_out[...] = gated.astype(BF16)
-    square_out[...] = mm(jnp.ones((8, channels), BF16), gated * gated, NT)
+    square_out[...] = mm(jnp.ones((8, channels), BF16), gated * gated, NT)[0:1]
 
 
 def coupling_kernel(slots, gated, grad, gain, coupling_out):
-    product = grad[...] * (gated[...].astype(F32) * gain[...])
-    coupling_out[...] = mm(jnp.ones((8, gain.shape[1]), BF16), product, NT)
+    product = grad[...].astype(F32) * (gated[...].astype(F32) * gain[...])
+    coupling_out[...] = mm(jnp.ones((8, gain.shape[1]), BF16), product, NT)[0:1]
 
 
 def norm_kernel(slots, gated, scale_row, gain, low_out):
@@ -230,7 +230,7 @@
     gate_sig = jax.nn.sigmoid(gate)
     silu = gate * gate_sig
     gated = y * silu
-    scaled_grad = scale * grad_in[...]
+    scaled_grad = scale * grad_in[...].astype(F32)
     d_gated = gain[...] * scaled_grad - pull * gated
     low_out[:, :channels] = (d_gated * y * (gate_sig + silu * (1.0 - gate_sig))).astype(BF16)
     channel_grads[6:7] += column_sum(scaled_grad * gated)
@@ -331,7 +331,6 @@
     product, joined, held, sems = rest[-4:]
     rows = own.shape[0]
     tile = product.shape[1]
-    part = min(tile, 256)
     index, step = pl.program_id(0), pl.program_id(1)
     copies = [
         pltpu.make_async_copy(block, joined.at[pl.ds((2 * i + first) * rows, rows)], sems.at[i])
@@ -348,11 +347,7 @@
 
         @pl.when(jnp.logical_and(index >= start, index < start + count))
         def _():
-            @pl.loop(0, tile // part)
-            def _(piece):
-                cols = pl.ds(pl.multiple_of(piece * part, part), part)
-                own_weight = weight[:, cols] if dims == NN else weight[cols, :]
-                product[:, cols] = lax.dot_general(held[step], own_weight, dims, preferred_element_type=F32)
+            product[...] = lax.dot_general(held[step], weight[...], dims, preferred_element_type=F32).astype(product.dtype)
 
     @pl.when(jnp.logical_and(index == pl.num_programs(0) - 1, step == 1))
     def _():
@@ -360,7 +355,7 @@
             copy.wait()
 
 
-def fill_rows(own, other, weights, dims, filled):
+def fill_rows(own, other, weights, dims, filled, kind=F32):
     rows, depth = own.shape
     side = 1 if dims == NN else 0
     widths = [values.shape[side] for values in weights]
@@ -391,10 +386,10 @@
             pl.BlockSpec((rows, tile), lambda j, i: (block(i), j)),
             anywhere,
         ],
-        out_shape=[jax.ShapeDtypeStruct((4 * rows, sum(widths)), F32), jax.ShapeDtypeStruct((4 * rows, depth), BF16)],
+        out_shape=[jax.ShapeDtypeStruct((4 * rows, sum(widths)), kind), jax.ShapeDtypeStruct((4 * rows, depth), BF16)],
         scratch_shapes=[pltpu.VMEM((2, rows, depth), BF16), pltpu.SemaphoreType.DMA((2,))],
         input_output_aliases={2 + count: 0, 3 + count: 1} if second else {},
-        compiler_params=limits(36),
+        compiler_params=pltpu.CompilerParams(dimension_semantics=("arbitrary", "arbitrary")),
         cost_estimate=cost(4 * rows * depth * sum(widths), 4 * rows * (depth + sum(widths))),
     )(own, other, *weights, *(filled if second else ()))
 
@@ -429,7 +424,7 @@
                 pl.BlockSpec((STRETCH, channels), at),
                 pl.BlockSpec((STRETCH, channels), at),
                 pl.BlockSpec((1, 1, width // 2, channels), lambda s, p, *_: (s, p, 0, 0)),
-                pl.BlockSpec((8, STRETCH), row_at),
+                pl.BlockSpec((1, STRETCH), row_at),
             ],
             scratch_shapes=[
                 pltpu.VMEM((24, channels), F32), pltpu.VMEM((24, width), F32), pltpu.VMEM((width // 2, channels), F32),
@@ -439,7 +434,7 @@
             jax.ShapeDtypeStruct((total, channels), F32),
             jax.ShapeDtypeStruct((total, channels), BF16),
             jax.ShapeDtypeStruct((seqs, pieces, width // 2, channels), BF16),
-            jax.ShapeDtypeStruct((8, total), F32),
+            jax.ShapeDtypeStruct((1, total), F32),
         ],
         compiler_params=pltpu.CompilerParams(dimension_semantics=("arbitrary", "arbitrary")),
         cost_estimate=cost(20e9, 40e6),
@@ -457,12 +452,62 @@
             num_scalar_prefetch=1,
             grid=(seqs, pieces),
             in_specs=[pl.BlockSpec((STRETCH, channels), at), pl.BlockSpec((STRETCH, channels), at), whole(gain.shape)],
-            out_specs=pl.BlockSpec((8, STRETCH), lambda s, p, *_: (0, s * pieces + p)),
+            out_specs=pl.BlockSpec((1, STRETCH), lambda s, p, *_: (0, s * pieces + p)),
         ),
-        out_shape=jax.ShapeDtypeStruct((8, total), F32),
+        out_shape=jax.ShapeDtypeStruct((1, total), F32),
         compiler_params=limits(8),
         cost_estimate=cost(2e9, 12e6),
     )(slots, gated, grad, gain)
+
+
+def split_norm_step(owners, numbers, seqs, gated, scale_row, gain, row, give, keep):
+    total, channels = gated.shape
+    count = total // STRETCH
+    pieces = count // seqs
+
+    def kernel(owners, numbers, gated, scale_row, gain, given, kept, near, far, held):
+        eye = iota((STRETCH, STRETCH), 0) == iota((STRETCH, STRETCH), 1)
+        scale = column_of(scale_row[...], eye)
+        low = (gated[...].astype(F32) * gain[...] * scale).astype(BF16)
+        held[...] = low
+        for out, name in ((given, give), (kept, keep)):
+            start = pl.multiple_of(numbers[0, name] * (channels // 2), LANES)
+            out[...] = held[:, pl.ds(start, channels // 2)]
+
+        @pl.when(pl.program_id(0) < count // 2)
+        def _():
+            near[...] = low
+
+        @pl.when(pl.program_id(0) >= count // 2)
+        def _():
+            far[...] = low
+
+    at = lambda i, *_: (i, 0)
+    half_block = pl.BlockSpec((STRETCH, channels // 2), at)
+    return pl.pallas_call(
+        kernel,
+        name="norm_rows",
+        grid_spec=pltpu.PrefetchScalarGridSpec(
+            num_scalar_prefetch=2,
+            grid=(count,),
+            in_specs=[
+                pl.BlockSpec((STRETCH, channels), at),
+                pl.BlockSpec((1, STRETCH), lambda i, own, *_: (0, i % seqs * pieces + own[i // seqs])),
+                whole(gain.shape),
+            ],
+            out_specs=[
+                half_block,
+                half_block,
+                pl.BlockSpec((STRETCH, channels), lambda i, *_: (jnp.minimum(i, count // 2 - 1), 0)),
+                pl.BlockSpec((STRETCH, channels), lambda i, *_: (jnp.maximum(i - count // 2, 0), 0)),
+            ],
+            scratch_shapes=[pltpu.VMEM((STRETCH, channels), BF16)],
+        ),
+        out_shape=[jax.ShapeDtypeStruct((total, channels // 2), BF16)] * 2
+        + [jax.ShapeDtypeStruct((total // 2, channels), BF16)] * 2,
+        compiler_params=limits(12),
+        cost_estimate=cost(1e9, 12e6),
+    )(owners, numbers, gated, scale_row, gain)
 
 
 def norm_step(slots, seqs, gated, scale_row, gain):
@@ -611,23 +656,59 @@
                     return 2 * ((origin & 1) * 4 + (origin >> 1 & 1) * 2 + (origin >> 2 & 1)) + (0 if w > 0 else 1)
 
                 columns["side", step, way] = eighth_of
-        for way in WAYS:
-            columns["first", way] = lambda i, w=way: (0 if w > 0 else n * block) + order.index(i) * block
         for bit in range(3):
-            columns["keep", bit] = lambda i, k=bit: (i >> k & 1) * (halved >> k + 1)
-            columns["give", bit] = lambda i, k=bit: (1 - (i >> k & 1)) * (halved >> k + 1)
+            columns["give", bit] = lambda i, k=bit: 1 - (i >> k & 1)
+            columns["keep", bit] = lambda i, k=bit: i >> k & 1
         self.at = Numbers("dp", n, columns)
 
     def exchange(self, values, bit):
         return lax.ppermute(values, "dp", [(i, i ^ (1 << bit)) for i in range(self.size)])
 
-    def add(self, parts, arrived, step):
-        shape = (self.block, parts.shape[1])
+    def halve(self, kept, arrived, bit):
+        rows, columns = kept.shape
+        first = self.at.names["give", bit]
+
+        def kernel(row, mine, other, given, held):
+            total = (mine[...].astype(F32) + other[...].astype(F32)).astype(BF16)
+
+            @pl.when(pl.program_id(0) == 0)
+            def _():
+                given[...] = total
+
+            @pl.when(pl.program_id(0) == 1)
+            def _():
+                held[...] = total
+
+        half = (rows // 2, columns)
+        at = pl.BlockSpec(half, lambda i, row: (row[0, first + i], 0))
+        return pl.pallas_call(
+            kernel,
+            name="halve",
+            grid_spec=pltpu.PrefetchScalarGridSpec(
+                num_scalar_prefetch=1, grid=(2,), in_specs=[at, at], out_specs=[whole(half), whole(half)]
+            ),
+            out_shape=[jax.ShapeDtypeStruct(half, BF16)] * 2,
+            compiler_params=limits(12),
+            cost_estimate=cost(1e6, 4e6),
+        )(self.at.row, kept, arrived)
+
+    def add(self, parts, arrived, step, extra=None):
+        block, columns = self.block, parts.shape[1]
+        shape = (block, columns)
+        half = 0 if extra is None else extra.shape[0] // 2
+        full = (block + half, columns)
         first = self.at.names["add", step, 1]
 
-        def kernel(row, one, two, came_one, came_two, out_one, out_two):
-            out_one[...] = (came_one[...].astype(F32) + one[...].astype(F32)).astype(BF16)
-            out_two[...] = (came_two[...].astype(F32) + two[...].astype(F32)).astype(BF16)
+        def kernel(row, one, two, *rest):
+            out_one, out_two = rest[-2:]
+            sources = [one[...].astype(F32), two[...].astype(F32)]
+            for i in range(len(arrived)):
+                sources[i] = sources[i] + rest[i][...].astype(F32)
+            out_one[:block] = sources[0].astype(BF16)
+            out_two[:block] = sources[1].astype(BF16)
+            if half:
+                out_one[block:] = rest[2][:half]
+                out_two[block:] = rest[2][half:]
 
         return pl.pallas_call(
             kernel,
@@ -638,15 +719,15 @@
                 in_specs=[
                     pl.BlockSpec(shape, lambda i, row: (row[0, first], 0)),
                     pl.BlockSpec(shape, lambda i, row: (row[0, first + 1], 0)),
-                    whole(shape),
-                    whole(shape),
-                ],
-                out_specs=[whole(shape), whole(shape)],
+                ]
+                + [whole(shape)] * len(arrived)
+                + ([whole(extra.shape)] if half else []),
+                out_specs=[whole(full), whole(full)],
             ),
-            out_shape=[jax.ShapeDtypeStruct(shape, BF16)] * 2,
-            compiler_params=limits(8),
+            out_shape=[jax.ShapeDtypeStruct(full, BF16)] * 2,
+            compiler_params=limits(10),
             cost_estimate=cost(1e6, 4e6),
-        )(self.at.row, parts, parts, *arrived)
+        )(self.at.row, parts, parts, *arrived, *([extra] if half else []))
 
     def store(self, sums, held, step):
         block, height = self.block, self.eighth // 2
@@ -682,24 +763,21 @@
     def all_reduce(self, parts, sums, fillers, finished):
         n, fillers = self.size, list(fillers)
 
-        def send(held):
+        def send(held, earlier=()):
             arrived = [lax.ppermute(values, "dp", self.pairs[way]) for way, values in zip(WAYS, held)]
             made = fillers.pop(0)(lambda values: after(values, *held)) if fillers else []
-            return lax.optimization_barrier((*arrived, *made))[:2]
-
-        held = [rows_at(parts, self.at["first", way], self.block) for way in WAYS]
+            return lax.optimization_barrier((*arrived, *made, *earlier))[:2]
+
+        held = self.add(parts, (), 0)
         for step in range(1, n):
-            held = self.add(parts, send(held), step)
-        extra = finished()
-        half = extra.shape[0] // 2
-        held = [jnp.concatenate([held[0], extra[:half]], axis=0), jnp.concatenate([held[1], extra[half:]], axis=0)]
+            held = self.add(parts, send(held), step, finished() if step == n - 1 else None)
         for step in range(n):
             if step:
-                held = send(held)
+                held = send(held, sums[:1])
             sums = self.store(sums, held, step)
         for filler in fillers:
             filler(lambda values: values)
-        return sums
+        return sums, held
 
 
 class Ranks:
@@ -810,63 +888,7 @@
     offset_row, shared_offset_row = conv_offset[None, :], shared_offset[None, :]
     gain_row = gate_gain[None, :]
 
-    blocked = local and ranks == 4
-    if blocked:
-        own_rows, cot_rows = normed_low.reshape(seqs * rows, model), cot_low.reshape(seqs * rows, model)
-        far_rows = group.shift(own_rows, 1)
-        far_cot = group.shift(after(cot_rows, own_rows), 1)
-        weights = (weight_gate, weight_inner, weight_ss)
-        first = fill_rows(own_rows, group.core(own_rows), weights, NN, None)
-        first_cot = fill_rows(cot_rows, group.core(cot_rows), (weight_out,), NT, None)
-        far_rows = after(far_rows, first[0], first_cot[0])
-        pre, normed_in = fill_rows(far_rows, group.core(far_rows), weights, NN, first)
-    else:
-        normed_in, cot_full = gather(normed_low), gather(cot_low)
-        weights = jnp.concatenate([weight_gate, weight_inner, weight_ss], axis=1)
-        pre = lax.dot_general(normed_in, weights, NN, preferred_element_type=F32)
-        grad = lax.dot_general(cot_full, weight_out, NT, preferred_element_type=F32)
-    y, gated, states, squares = scan_forward(
-        slots, segments, image_span, pre, seg_row, spread, conv_kernel, offset_row, skip, shared_kernel, shared_offset_row,
-        bias, rate,
-    )
-    if blocked:
-        far_cot = after(far_cot, squares)
-        grad, cot_full = fill_rows(far_cot, group.core(far_cot), (weight_out,), NT, first_cot)
-    coupling = coupling_step(slots, seqs, gated, grad, gain_row)
-    sums = total_over(jnp.concatenate([squares[0:1], coupling[0:1]], axis=0), "tensor", ranks)
-    scale_row = lax.rsqrt(sums[0:1] / inner_width + EPSILON)
-    pull_row = scale_row * scale_row * scale_row / inner_width * sums[1:2]
-    normed_out = norm_step(slots, seqs, gated, scale_row, gain_row)
-
-    def backward(start, count, done, pull):
-        return scan_backward(
-            start, count, done, slots, segments, image_span, pre, grad, y, states, seg_row, scale_row, pull, spread,
-            conv_kernel, offset_row, skip, gain_row, shared_kernel, shared_offset_row, bias, rate,
-        )
-
-    out_product = lambda left: lax.dot_general(left, cot_full, TN, preferred_element_type=BF16)
-    made = {}
-    ringed = dps == 8 and seqs > 1 and model == 2 * channels
-    if ringed:
-        ring = Ring(dps, ranks // 2, model, channels)
-        join = lambda mine, arrived: (mine.astype(F32) + arrived.astype(F32)).astype(BF16)
-        part_of = lambda values, kind, bit, axis=0: rows_at(values, ring.at[kind, bit], channels >> bit + 1, axis)
-        given = out_product(part_of(normed_out, "give", 0, 1))
-        arrived = ring.exchange(given, 0)
-        kept = out_product(after(part_of(normed_out, "keep", 0, 1), given))
-        low, shared_part, step_low, channel_grads, head_grads, shared_grads = backward(0, seqs, None, after(pull_row, kept))
-        kept = join(after(kept, low), arrived)
-        given = part_of(kept, "give", 1)
-        arrived = ring.exchange(given, 1)
-        low_part = lax.dot_general(normed_in, after(low, given), TN, preferred_element_type=BF16)
-        made["quarter"] = part_of(kept, "keep", 1), arrived
-    else:
-        out_sum = lax.psum(out_product(normed_out), "dp")
-        low, shared_part, step_low, channel_grads, head_grads, shared_grads = backward(0, seqs, None, pull_row)
-        low_part = lax.dot_general(normed_in, low, TN, preferred_element_type=BF16)
-
-    cut = total // 2 if local else 0
-    half = ranks // 2
+    slab = width // ranks
     weight_low = jnp.concatenate([weight_gate, weight_inner], axis=1)
     weight_side = jnp.concatenate(
         [
@@ -876,14 +898,73 @@
         ],
         axis=1,
     )
+    blocked = local and ranks == 4
+    if blocked:
+        own_rows, cot_rows = normed_low.reshape(seqs * rows, model), cot_low.reshape(seqs * rows, model)
+        far_rows = group.shift(own_rows, 1)
+        far_cot = group.shift(after(cot_rows, own_rows), 1)
+        weights = (weight_gate, weight_inner, weight_ss)
+        first = fill_rows(own_rows, group.core(own_rows), weights, NN, None)
+        first_cot = fill_rows(cot_rows, group.core(cot_rows), (weight_out,), NT, None, BF16)
+        far_rows = after(far_rows, first[0], first_cot[0], weight_low, weight_side)
+        pre, normed_in = fill_rows(far_rows, group.core(far_rows), weights, NN, first)
+    else:
+        normed_in, cot_full = gather(normed_low), gather(cot_low)
+        weights = jnp.concatenate([weight_gate, weight_inner, weight_ss], axis=1)
+        pre = lax.dot_general(normed_in, weights, NN, preferred_element_type=F32)
+        grad = lax.dot_general(cot_full, weight_out, NT, preferred_element_type=BF16)
+    y, gated, states, squares = scan_forward(
+        slots, segments, image_span, pre, seg_row, spread, conv_kernel, offset_row, skip, shared_kernel, shared_offset_row,
+        bias, rate,
+    )
+    if blocked:
+        far_cot = after(far_cot, squares)
+        grad, cot_full = fill_rows(far_cot, group.core(far_cot), (weight_out,), NT, first_cot, BF16)
+    coupling = coupling_step(slots, seqs, gated, grad, gain_row)
+    sums = total_over(jnp.concatenate([squares, coupling], axis=0), "tensor", ranks)
+    scale_row = lax.rsqrt(sums[0:1] / inner_width + EPSILON)
+    pull_row = scale_row * scale_row * scale_row / inner_width * sums[1:2]
+
+    def backward(start, count, done, pull):
+        return scan_backward(
+            start, count, done, slots, segments, image_span, pre, grad, y, states, seg_row, scale_row, pull, spread,
+            conv_kernel, offset_row, skip, gain_row, shared_kernel, shared_offset_row, bias, rate,
+        )
+
+    out_product = lambda left: lax.dot_general(left, cot_full, TN, preferred_element_type=BF16)
+    made = {}
+    ringed = local and dps == 8 and ranks == 4 and seqs > 1 and model == 2 * channels
+    if ringed:
+        ring = Ring(dps, ranks // 2, model, channels)
+        join = lambda mine, arrived: (mine.astype(F32) + arrived.astype(F32)).astype(BF16)
+        first = group.at.names["owner", 0]
+        to_give, to_keep, norm_near, norm_far = split_norm_step(
+            group.at.row[0, first : first + ranks], ring.at.row, seqs, gated, scale_row, gain_row, None,
+            ring.at.names["give", 0], ring.at.names["keep", 0],
+        )
+        given = out_product(to_give)
+        arrived = ring.exchange(given, 0)
+        kept = out_product(after(to_keep, given))
+        done = backward(0, seqs // 2, None, after(pull_row, kept))
+        mixed_far = lax.dot_general(after(norm_far, done[0]), weight_out, NN, preferred_element_type=BF16)
+        given, kept = ring.halve(after(kept, done[0], mixed_far), arrived, 1)
+        arrived = ring.exchange(given, 1)
+        done = backward(seqs // 2, seqs - seqs // 2, done, after(pull_row, given))
+        given, kept = ring.halve(after(kept, done[0]), arrived, 2)
+        low, shared_part, step_low, channel_grads, head_grads, shared_grads = done
+        low_part = lax.dot_general(normed_in, after(low, given), TN, preferred_element_type=BF16)
+        made["eighth"] = kept, ring.exchange(given, 2)
+        low_part = after(low_part, made["eighth"][1])
+    else:
+        normed_out = norm_step(slots, seqs, gated, scale_row, gain_row)
+        norm_near, norm_far = (normed_out[: total // 2], normed_out[total // 2 :]) if local else (normed_out, None)
+        out_sum = lax.psum(out_product(normed_out), "dp")
+        low, shared_part, step_low, channel_grads, head_grads, shared_grads = backward(0, seqs, None, pull_row)
+        low_part = lax.dot_general(normed_in, low, TN, preferred_element_type=BF16)
+
+    cut = total // 2 if local else 0
+    half = ranks // 2
     by_rank = lambda values: values.reshape(-1, seqs, rows, model)
-
-    def quarter_join(hold):
-        mine, other = made["quarter"]
-        kept = join(hold(mine), other)
-        given = part_of(kept, "give", 2)
-        made["eighth"] = part_of(kept, "keep", 2), ring.exchange(given, 2)
-        return [given]
 
     def finished(hold=lambda values: values):
         if "finished" not in made:
@@ -897,7 +978,7 @@
         columns = jnp.moveaxis(hold(shared_part).reshape(total, ranks, slab), 1, 0)
         columns = jnp.concatenate([rows_at(columns, group.at["owner", slot], 1) for slot in range(ranks)], axis=0)
         made["columns"] = columns[:half], group.core(columns[half:])
-        return [columns] + (quarter_join(hold) if ringed else [])
+        return [columns]
 
     def columns_in(hold):
         shared_low = slabs(take_rows("columns", hold).astype(BF16))
@@ -942,11 +1023,12 @@
             made["input"] = [made["input", slot] for slot in range(half)], [made["input", slot] for slot in range(half, ranks)]
         return []
 
-    def mix_of(slots, far):
-        part = slice(slots.start * seqs * rows, slots.stop * seqs * rows) if local else slice(0, total)
-
+    def mix_of(far):
         def run(hold):
-            product = lax.dot_general(hold(normed_out[part]), weight_out, NN, preferred_element_type=BF16)
+            if far and ringed:
+                made["mixed far"] = group.core(by_rank(hold(mixed_far)))
+                return []
+            product = lax.dot_general(hold(norm_far if far else norm_near), weight_out, NN, preferred_element_type=BF16)
             if not local:
                 made["mixed"] = scatter(product), []
             elif far:
@@ -958,11 +1040,13 @@
         return run
 
     def side_product(hold):
-        made["side_part"] = lax.dot_general(normed_in, hold(made["side"]), TN, preferred_element_type=BF16)
+        product = lax.dot_general(hold(made["side"]), normed_in, TN, preferred_element_type=BF16)
+        made["side_part"] = product[: slab + heads]
         return [made["side_part"]]
 
     def input_rows(hold):
         normed_grad = take_rows("input", hold)
+        own = hold(own_low).astype(F32)
         weighted = normed_grad * pre_gain[None, None, :]
         projection = jnp.sum(weighted * own, axis=2, keepdims=True)
         own_grad = row_scale * weighted - row_scale * row_scale * row_scale / model * own * projection
@@ -976,7 +1060,7 @@
         return [made["tokens_grad"]]
 
     def block_rows(hold):
-        made["block_out"] = (own + take_rows("mixed", hold)).astype(BF16)
+        made["block_out"] = (hold(own_low).astype(F32) + take_rows("mixed", hold)).astype(BF16)
         return [made["block_out"]]
 
     def block_order(hold):
@@ -1038,7 +1122,7 @@
     far = [input_rows_of(slot) for slot in (range(half, ranks) if local else range(1))]
     near = [input_rows_of(slot) for slot in (range(half) if local else range(0))]
     def gather_near(hold):
-        slabs_of = hold(made["side_part"])[:, :slab]
+        slabs_of = hold(made["side_part"])[:slab]
         made["gathered"] = [slabs_of]
         for _ in range(1, half):
             made["gathered"].append(group.shift(made["gathered"][-1], 1))
@@ -1048,57 +1132,69 @@
         made["gathered"] = made["gathered"] + [group.core(hold(values)) for values in made["gathered"]]
         return []
 
+    def side_outputs(hold):
+        gathered = jnp.stack([hold(values) for values in made["gathered"]])
+        shared = jnp.concatenate([rows_at(gathered, group.at["slot", owner], 1)[0] for owner in range(ranks)], axis=0)
+        made["shared"] = shared.T.astype(F32)
+        made["step"] = hold(made["side_part"])[slab : slab + heads].T.astype(F32)
+        return [made["shared"], made["step"]]
+
+    def small_outputs(hold):
+        packed = hold(made["small"])
+        shared_sums = packed[16:24, :width]
+        made["outputs"] = [
+            packed[24:].reshape(model), packed[0:4], packed[4], shared_sums[0:4], shared_sums[4], packed[9, :heads],
+            packed[8, :heads], jnp.sum(packed[5].reshape(heads, HEAD), axis=1), packed[6],
+        ]
+        return []
+
     fillers = [
-        columns_out,
-        together(pass_on("columns"), mix_of(range(half, ranks), True) if local else nothing),
+        together(mix_of(True) if local else nothing, columns_out),
+        together(pass_on("columns"), mix_of(False)),
         together(columns_in, side_product),
         together(side_dp[0][0], *far[:1]),
-        *far[1:],
-        together(side_dp[0][1], side_dp[1][0], *near[:1], finish),
-        *near[1:],
-        together(input_pair, pass_on("input"), side_dp[1][1], side_dp[2][0], mix_of(range(half), False)),
-        pass_on("mixed"),
-        together(input_rows, side_dp[2][1]),
+        together(side_dp[0][1], side_dp[1][0], *far[1:2]),
+        *far[2:],
+        together(*near[:1], finish),
+        together(side_dp[1][1], side_dp[2][0], *near[1:2]),
+        *near[2:],
+        together(input_pair, pass_on("input")),
+        together(pass_on("mixed"), side_dp[2][1]),
+        input_rows,
         together(small_start, tensor_send, input_order, gather_near),
         together(tensor_take, pack, small_dp[0][0], block_rows),
         together(small_dp[0][1], small_dp[1][0], block_order, gather_far),
+        together(small_dp[1][1], small_outputs, side_outputs),
     ]
     if ringed:
         sums = [blank((model, channels)), blank((model, channels)), blank((channels, model))]
-        grads = dict(zip(("gate", "inner", "out"), ring.all_reduce(low_part, sums, fillers, finished)))
+        sums, _ = ring.all_reduce(low_part, sums, fillers, finished)
+        grads = dict(zip(("gate", "inner", "out"), sums))
     else:
         low_sum = lax.psum(low_part, "dp").astype(F32)
         grads = {"gate": low_sum[:, :channels], "inner": low_sum[:, channels:], "out": out_sum.astype(F32)}
         for filler in fillers:
             filler(lambda values: values)
-    plain = lambda values: values
-    small_dp[1][1](plain)
-    packed, side_sum = made["small"], made["side_part"]
-    block_out, tokens_grad, grad_out = made["block_out"], made["tokens_grad"], grads["out"]
-    gathered = jnp.stack(made["gathered"])
-    grad_shared = jnp.concatenate(
-        [rows_at(gathered, group.at["slot", owner], 1)[0] for owner in range(ranks)], axis=1
-    ).astype(F32)
-    grad_step = side_sum[:, slab : slab + heads].astype(F32)
-
-    shared_sums = packed[16:24, :width]
+    gain, kernel_grad, offset_grad, shared_kernel_grad, shared_offset_grad, bias_grad, rate_grad, skip_grad, gate_gain_grad = made[
+        "outputs"
+    ]
     return (
-        block_out,
-        tokens_grad,
-        packed[24:].reshape(model),
+        made["block_out"],
+        made["tokens_grad"],
+        gain,
         grads["gate"],
         grads["inner"],
-        grad_step,
-        grad_shared,
-        packed[0:4],
-        packed[4],
-        shared_sums[0:4],
-        shared_sums[4],
-        packed[9, :heads],
-        packed[8, :heads],
-        jnp.sum(packed[5].reshape(heads, HEAD), axis=1),
-        packed[6],
-        grad_out,
+        made["step"],
+        made["shared"],
+        kernel_grad,
+        offset_grad,
+        shared_kernel_grad,
+        shared_offset_grad,
+        bias_grad,
+        rate_grad,
+        skip_grad,
+        gate_gain_grad,
+        grads["out"],
     )
 
 

time: 613 us -> 558 us (0.910)
  waiting for transfers between devices: 128 us -> 90 us
  local copies, waits for them, and re-layouts: 80.5 us -> 52.2 us
  Pallas kernels: 176 us -> 192 us
  starting transfers between devices: 76.3 us -> 65.9 us
    ppermute x28, waiting for transfers between devices: 89 us -> 50.3 us  [send(): lax.ppermute(values, 'dp', self.pairs[way])]
    ppermute x28, starting transfers between devices: 52.9 us -> 34.9 us  [send(): lax.ppermute(values, 'dp', self.pairs[way])]
    dynamic_slice x6 -> x2, local copies, waits for them, and re-layouts: 16.2 us -> 4.08 us  [rows_at(): lax.dynamic_slice(values, starts, sizes, allow_negative_indices=False)]
    slice x8 -> x5, local copies, waits for them, and re-layouts: 11 us -> 2.41 us  [the longest x1 0.63 us: small_outputs(): packed[6]]
    unnamed x131 -> x115, local copies, waits for them, and re-layouts: 32.6 us -> 26.2 us
    pallas_call x1 -> x2, Pallas kernels: 63.6 us -> 68.3 us  [scan_backward(): pl.pallas_call(partial(backward_kernel, channels, start), name='scan_back...]
  transfers between devices with their start and end apart: 59 -> 59, of which waited for: 24 -> 23; matrix products, arithmetic and copies ran while one was open for 29% -> 30% of each run, Pallas kernels for 26% -> 31%
where the time goes in v3:
time: 558 us; the launch traced here: 552 us
  Pallas kernels  192 us (34%)
  matrix products  105 us (19%)
  waiting for transfers between devices  90 us (16%)
  starting transfers between devices  65.9 us (12%)
  local copies, waits for them, and re-layouts  52.2 us (9%)
  other arithmetic  44.8 us (8%)
    pallas_call x2, Pallas kernels, scan_backward(): pl.pallas_call(partial(backward_kernel, channels, start), name='scan_back...  68.3 us
    pallas_call x4, Pallas kernels, fill_rows(): pl.pallas_call(partial(fill_kernel, dims, spans, 1 if second else 0), nam...  62.9 us
    ppermute x28, waiting for transfers between devices, send(): lax.ppermute(values, 'dp', self.pairs[way])  50.3 us
    ppermute x28, starting transfers between devices, send(): lax.ppermute(values, 'dp', self.pairs[way])  34.9 us
    dot_general x4, matrix products, run(): lax.dot_general(low_rows[part], weight_low, NT, preferred_element_type=F32)  30.7 us
    ppermute x10, waiting for transfers between devices, send(): lax.ppermute(values, axis, [(i, i ^ k) for i in range(size)])  29.4 us
    pallas_call x1, Pallas kernels, scan_forward(): pl.pallas_call(partial(forward_kernel, channels), name='scan_forward', gr...  26.9 us
    unnamed x115, local copies, waits for them, and re-layouts  26.2 us
  transfers between devices with their start and end apart: 59, of which 23 were waited for; matrix products, arithmetic and copies ran while one was open for 30% of the time, Pallas kernels for 31%

profile of v3, /device:TPU:0, one launch (start us, length us, event | category | flops | bytes accessed | tf_op | source)
XLA Modules:
  0.0 552.3 jit_solution(2264889013860201112)
XLA Ops:
  24.0 10.7 %fill_rows.5 = (bf16[2048,1024]{1,0:T(8,128)(2,1)}, bf16[2048,2048]{1,0:T(8,128)(2,1)}) custom-call(bf16[512,2048]{1,0:T(8,128)(2,1)} %pad_maximum_fusion.1.own, bf16[512,2048]{1,0:T(8,128)(2,1)} %collective-permute-done.2.other, bf16[1024,2048]{1,0:T(8,128)(2,1)} %rest_0_.7), custom_call_target="tpu_custom_call" | custom-call | flops 4294967296 | bytes 6291456 | tf_op jit(solution)/shard_map/fill_rows/pallas_call | solution.py:378
  34.8 20.9 %fill_rows.4 = (f32[2048,2560]{1,0:T(8,128)}, bf16[2048,2048]{1,0:T(8,128)(2,1)}) custom-call(bf16[512,2048]{1,0:T(8,128)(2,1)} %fusion.3.own, bf16[512,2048]{1,0:T(8,128)(2,1)} %collective-permute-done.1.other, bf16[2048,1024]{1,0:T(8,128)(2,1)} %rest_0_.6, bf16[2048,1024]{1,0:T(8,128)(2,1)} %rest_1_.3, bf16[2048,512]{1,0:T(8,128)(2,1)} %maximum_maximum_fusion.rest_2_), custom_call_target="tpu_custom_call" | custom-call | flops 10737418240 | bytes 9437184 | tf_op jit(solution)/shard_map/fill_rows/pallas_call | solution.py:378
  64.3 20.9 %fill_rows.6 = (f32[2048,2560]{1,0:T(8,128)}, bf16[2048,2048]{1,0:T(8,128)(2,1)}) custom-call(bf16[512,2048]{1,0:T(8,128)(2,1)} %collective-permute-done.own, bf16[512,2048]{1,0:T(8,128)(2,1)} %collective-permute-done.3.other, bf16[2048,1024]{1,0:T(8,128)(2,1)} %rest_0_.6, bf16[2048,1024]{1,0:T(8,128)(2,1)} %rest_1_.3, ...), custom_call_target="tpu_custom_call", output_to_operand_aliasing={{0}: (5, {}), {1}: (6, {})} | custom-call | flops 10737418240 | bytes 9437184 | tf_op jit(solution)/shard_map/fill_rows/pallas_call | solution.py:378
  85.2 26.9 %scan_forward.1 = (f32[2048,1024]{1,0:T(8,128)}, bf16[2048,1024]{1,0:T(8,128)(2,1)}, bf16[2,4,128,1024]{3,2,1,0:T(8,128)(2,1)}, f32[1,2048]{1,0:T(1,128)}) custom-call(s32[4]{0:T(128)} %get-tuple-element.413.slots, s32[2,1024]{1,0:T(2,128)} %seg_sm.5, s32[2,2]{1,0:T(2,128)} %span_sm.5, f32[2048,2560]{1,0:T(8,128)} %get-tuple-element.181.pre.halo, ...), custom_call_target="tpu_custom_call" | custom-call | flops 20000000000 | bytes 40000000 | tf_op jit(solution)/shard_map/scan_forward/pallas_call | solution.py:411
  112.4 3.9 collective-permute-done.5.other
  117.7 10.5 %fill_rows.7 = (bf16[2048,1024]{1,0:T(8,128)(2,1)}, bf16[2048,2048]{1,0:T(8,128)(2,1)}) custom-call(bf16[512,2048]{1,0:T(8,128)(2,1)} %copy-done.23, bf16[512,2048]{1,0:T(8,128)(2,1)} %copy-done.24, bf16[1024,2048]{1,0:T(8,128)(2,1)} %rest_0_.7, bf16[2048,1024]{1,0:T(8,128)(2,1)} %get-tuple-element.177.rest_1_, ...), custom_call_target="tpu_custom_call", output_to_operand_aliasing={{0}: (3, {}), {1}: (4, {})} | custom-call | flops 4294967296 | bytes 6291456 | tf_op jit(solution)/shard_map/fill_rows/pallas_call | solution.py:378
  148.4 9.4 %fusion.81 = bf16[512,2048]{1,0:T(8,128)(2,1)} fusion(bf16[2048,512]{1,0:T(8,128)(2,1)S(1)} %get-tuple-element.191, bf16[2048,2048]{1,0:T(8,128)(2,1)} %get-tuple-element.192), kind=kOutput, calls=%fused_computation.167 | convolution fusion | flops 4294967296 | bytes 12582912 | tf_op jit(solution)/shard_map/dot_general | solution.py:934
  159.3 5.7 %fusion.82.mine = bf16[512,2048]{1,0:T(8,128)(2,1)} fusion(bf16[2048,512]{1,0:T(8,128)(2,1)S(1)} %get-tuple-element.193, bf16[2048,2048]{1,0:T(8,128)(2,1)S(1)} %bitcast.163), kind=kOutput, calls=%fused_computation.168 | convolution fusion | flops 4294967296 | bytes 12582912 | tf_op jit(solution)/shard_map/dot_general | solution.py:934
  165.1 34.3 %scan_backward.2 = (bf16[2048,2048]{1,0:T(8,128)(2,1)}, bf16[2048,256]{1,0:T(8,128)(2,1)}, bf16[2048,128]{1,0:T(8,128)(2,1)}, f32[8,1024]{1,0:T(8,128)}, f32[8,128]{1,0:T(8,128)}, /*index=5*/f32[8,256]{1,0:T(8,128)}) custom-call(s32[4]{0:T(128)} %get-tuple-element.413.slots, s32[2,1024]{1,0:T(2,128)} %seg_sm.5, s32[2,2]{1,0:T(2,128)} %span_sm.5, ...), custom_call_target="tpu_custom_call" | custom-call | flops 22000001024 | bytes 30000000 | tf_op jit(solution)/shard_map/scan_backward/pallas_call | solution.py:552
  199.4 9.4 %fusion.83 = bf16[1024,2048]{1,0:T(8,128)(2,1)} fusion(bf16[1024,1024]{1,0:T(8,128)(2,1)} %copy-done.11, bf16[1024,2048]{1,0:T(8,128)(2,1)} %rest_0_.7), kind=kOutput, calls=%fused_computation.169 | convolution fusion | flops 4294967296 | bytes 10485760 | tf_op jit(solution)/shard_map/dot_general | solution.py:949
  213.1 34.0 %scan_backward.3 = (bf16[2048,2048]{1,0:T(8,128)(2,1)}, bf16[2048,256]{1,0:T(8,128)(2,1)}, bf16[2048,128]{1,0:T(8,128)(2,1)}, f32[8,1024]{1,0:T(8,128)}, f32[8,128]{1,0:T(8,128)}, /*index=5*/f32[8,256]{1,0:T(8,128)}) custom-call(s32[4]{0:T(128)} %get-tuple-element.413.slots, ...), custom_call_target="tpu_custom_call", output_to_operand_aliasing={{0}: (20, {}), {1}: (21, {}), {2}: (22, {})} | custom-call | flops 22000001024 | bytes 30000000 | tf_op jit(solution)/shard_map/scan_backward/pallas_call | solution.py:552
  250.8 22.5 %fusion.84.one.two = bf16[2048,2048]{1,0:T(8,128)(2,1)S(1)} fusion(bf16[2048,2048]{1,0:T(8,128)(2,1)} %get-tuple-element.180, bf16[2048,2048]{1,0:T(8,128)(2,1)} %get-tuple-element.264), kind=kOutput, calls=%fused_computation.170 | convolution fusion | flops 17179869184 | bytes 25165824 | tf_op jit(solution)/shard_map/dot_general | solution.py:955
  281.1 4.8 dynamic-slice_bitcast_fusion.7
  297.8 6.1 %fusion.85 = bf16[1024,2048]{1,0:T(8,128)(2,1)} fusion(bf16[1024,1024]{1,0:T(8,128)(2,1)S(1)} %copy-done.10, bf16[1024,2048]{1,0:T(8,128)(2,1)S(1)} %copy-done.20), kind=kOutput, calls=%fused_computation.171 | convolution fusion | flops 4294967296 | bytes 10485760 | tf_op jit(solution)/shard_map/dot_general | solution.py:1031
  315.5 5.1 fusion.50
  324.6 7.8 %fusion.22 = f32[512,2048]{1,0:T(8,128)S(1)} fusion(bf16[2048,2048]{1,0:T(8,128)(2,1)} %copy-done.25, bf16[2048,2048]{1,0:T(8,128)(2,1)} %get-tuple-element.264), kind=kOutput, calls=%fused_computation.42 | convolution fusion | flops 4294967296 | bytes 14680064 | tf_op jit(solution)/shard_map/dot_general | solution.py:1010
  339.1 7.6 %fusion.20 = f32[512,2048]{1,0:T(8,128)S(1)} fusion(bf16[2048,2048]{1,0:T(8,128)(2,1)} %copy-done.25, bf16[2048,2048]{1,0:T(8,128)(2,1)} %get-tuple-element.264), kind=kOutput, calls=%fused_computation.40 | convolution fusion | flops 4294967296 | bytes 14680064 | tf_op jit(solution)/shard_map/dot_general | solution.py:1010
  355.5 7.6 %fusion.18 = f32[512,2048]{1,0:T(8,128)S(1)} fusion(bf16[2048,2048]{1,0:T(8,128)(2,1)} %copy-done.25, bf16[2048,2048]{1,0:T(8,128)(2,1)} %get-tuple-element.264), kind=kOutput, calls=%fused_computation.38 | convolution fusion | flops 4294967296 | bytes 14680064 | tf_op jit(solution)/shard_map/dot_general | solution.py:1010
  369.4 7.6 %fusion.16 = f32[512,2048]{1,0:T(8,128)S(1)} fusion(bf16[2048,2048]{1,0:T(8,128)(2,1)} %copy-done.25, bf16[2048,2048]{1,0:T(8,128)(2,1)} %get-tuple-element.264), kind=kOutput, calls=%fused_computation.36 | convolution fusion | flops 4294967296 | bytes 14680064 | tf_op jit(solution)/shard_map/dot_general | solution.py:1010
  380.0 4.3 collective-permute-done.26.rest_0_
  384.3 5.0 collective-permute-done.27.rest_1_
  399.8 10.0 %collective-permute-done.29.one = bf16[192,2048]{1,0:T(8,128)(2,1)S(1)} collective-permute-done((bf16[192,2048]{1,0:T(8,128)(2,1)S(1)}, bf16[192,2048]{1,0:T(8,128)(2,1)S(1)}, u32[]{:S(2)}, u32[]{:S(2)}) %collective-permute-start.29) | collective-permute-done | bytes 786464 | tf_op jit(solution)/shard_map/ppermute | solution.py:767
  409.8 5.3 collective-permute-start.35
  423.1 4.0 collective-permute-done.35
  434.6 6.8 %collective-permute-start.36 = (bf16[192,2048]{1,0:T(8,128)(2,1)S(1)}, bf16[192,2048]{1,0:T(8,128)(2,1)S(1)}, u32[]{:S(2)}, u32[]{:S(2)}) collective-permute-start(bf16[192,2048]{1,0:T(8,128)(2,1)S(1)} %collective-permute-done.32.one), channel_id=1, source_target_pairs={{0,8},{8,16},{16,24},{24,28},{28,20},{20,12},{12,4},{4,0},{1,9},{9... | collective-permute-start | bytes 2359304 | tf_op jit(solution)/shard_map/ppermute | solution.py:767
  443.7 4.1 fusion.9
  447.9 8.7 %fusion.7 = bf16[2,256,2048]{2,1,0:T(8,128)(2,1)} fusion(bf16[2,256,2048]{2,1,0:T(8,128)(2,1)S(1)} %bitcast.158, bf16[2,256,2048]{2,1,0:T(8,128)(2,1)} %bitcast.66, f32[2,256]{1,0:T(2,128)S(1)} %fusion.74, f32[2048]{0:T(1024)S(1)} %copy-done.38, f32[2,256]{1,0:T(2,128)S(1)} %rsqrt.20, bf16[2,256,2048]{2,1,0:T(8,128)(2,1)} %collective-permute-done.39, ...), kind=kOutput, calls=%fused_computation.12 | output fusion | flops 23071232 | bytes 12595200 | tf_op jit(solution)/shard_map/mul | solution.py:1052
  465.8 6.9 %collective-permute-done.40.one = bf16[192,2048]{1,0:T(8,128)(2,1)S(1)} collective-permute-done((bf16[192,2048]{1,0:T(8,128)(2,1)S(1)}, bf16[192,2048]{1,0:T(8,128)(2,1)S(1)}, u32[]{:S(2)}, u32[]{:S(2)}) %collective-permute-start.40) | collective-permute-done | bytes 786464 | tf_op jit(solution)/shard_map/ppermute | solution.py:767
  479.7 7.2 %collective-permute-done.46 = f32[10,1024]{1,0:T(8,128)S(1)} collective-permute-done((f32[10,1024]{1,0:T(8,128)S(1)}, f32[10,1024]{1,0:T(8,128)S(1)}, u32[]{:S(2)}, u32[]{:S(2)}) %collective-permute-start.46) | collective-permute-done | bytes 40992 | tf_op jit(solution)/shard_map/ppermute | solution.py:1090
  487.2 4.0 fusion.12
  493.6 4.5 collective-permute-done.43.one
  502.0 18.1 %collective-permute-done.48 = f32[26,1024]{1,0:T(8,128)S(1)} collective-permute-done((f32[26,1024]{1,0:T(8,128)S(1)}, f32[26,1024]{1,0:T(8,128)S(1)}, u32[]{:S(2)}, u32[]{:S(2)}) %collective-permute-start.48) | collective-permute-done | bytes 106528 | tf_op jit(solution)/shard_map/ppermute | solution.py:1090
  (333 shorter events, 205.6 us)
Async XLA Ops:
  5.8 18.2 %collective-permute-start.2 = (bf16[512,2048]{1,0:T(8,128)(2,1)}, bf16[512,2048]{1,0:T(8,128)(2,1)}, u32[]{:S(2)}, u32[]{:S(2)}) collective-permute-start(bf16[512,2048]{1,0:T(8,128)(2,1)} %pad_maximum_fusion.1.own), channel_id=1, source_target_pairs={{0,1},{1,0},{2,3},{3,2},{4,5},{5,4},{6,7},{7,6},{8,9},{9,8},{10,11... | collective-permute-start | bytes 6291464 | tf_op jit(solution)/shard_map/ppermute | solution.py:805
  9.7 25.1 %collective-permute-start.1 = (bf16[512,2048]{1,0:T(8,128)(2,1)}, bf16[512,2048]{1,0:T(8,128)(2,1)}, u32[]{:S(2)}, u32[]{:S(2)}) collective-permute-start(bf16[512,2048]{1,0:T(8,128)(2,1)} %fusion.3.own), channel_id=1, source_target_pairs={{0,1},{1,0},{2,3},{3,2},{4,5},{5,4},{6,7},{7,6},{8,9},{9,8},{10,11... | collective-permute-start | bytes 6291464 | tf_op jit(solution)/shard_map/ppermute | solution.py:805
  9.8 49.1 %collective-permute-start = (bf16[512,2048]{1,0:T(8,128)(2,1)}, bf16[512,2048]{1,0:T(8,128)(2,1)}, u32[]{:S(2)}, u32[]{:S(2)}) collective-permute-start(bf16[512,2048]{1,0:T(8,128)(2,1)} %fusion.3.own), channel_id=1, source_target_pairs={{0,2},{1,3},{2,0},{3,1},{4,6},{5,7},{6,4},{7,5},{8,10},{9,11},{10,... | collective-permute-start | bytes 6291464 | tf_op jit(solution)/shard_map/ppermute | solution.py:808
  58.9 53.2 %collective-permute-start.4 = (bf16[512,2048]{1,0:T(8,128)(2,1)}, bf16[512,2048]{1,0:T(8,128)(2,1)S(1)}, u32[]{:S(2)}, u32[]{:S(2)}) collective-permute-start(bf16[512,2048]{1,0:T(8,128)(2,1)} %pad_maximum_fusion.1.own), channel_id=1, source_target_pairs={{0,2},{1,3},{2,0},{3,1},{4,6},{5,7},{6,4},{7,5},{8,10},{9,11},{10,... | collective-permute-start | bytes 6291464 | tf_op jit(solution)/shard_map/ppermute | solution.py:808
  157.9 51.0 %collective-permute-start.8 = (bf16[512,2048]{1,0:T(8,128)(2,1)}, bf16[512,2048]{1,0:T(8,128)(2,1)S(1)}, u32[]{:S(2)}, u32[]{:S(2)}) collective-permute-start(bf16[512,2048]{1,0:T(8,128)(2,1)} %fusion.81), channel_id=1, source_target_pairs={{0,4},{4,0},{8,12},{12,8},{16,20},{20,16},{24,28},{28,24},{1,5},{5... | collective-permute-start | bytes 6291464 | tf_op jit(solution)/shard_map/ppermute | solution.py:665
  211.5 35.6 %collective-permute-start.9 = (bf16[256,2048]{1,0:T(8,128)(2,1)}, bf16[256,2048]{1,0:T(8,128)(2,1)S(1)}, u32[]{:S(2)}, u32[]{:S(2)}) collective-permute-start(bf16[256,2048]{1,0:T(8,128)(2,1)} %get-tuple-element.199), channel_id=1, source_target_pairs={{0,8},{4,12},{8,0},{12,4},{16,24},{20,28},{24,16},{28,20},{1,9},{5... | collective-permute-start | bytes 3145736 | tf_op jit(solution)/shard_map/ppermute | solution.py:665
  248.2 25.2 %collective-permute-start.10 = (bf16[128,2048]{1,0:T(8,128)(2,1)S(1)}, bf16[128,2048]{1,0:T(8,128)(2,1)}, u32[]{:S(2)}, u32[]{:S(2)}) collective-permute-start(bf16[128,2048]{1,0:T(8,128)(2,1)S(1)} %get-tuple-element.209), channel_id=1, source_target_pairs={{0,16},{4,20},{8,24},{12,28},{16,0},{20,4},{24,8},{28,12},{1,17},{... | collective-permute-start | bytes 1572872 | tf_op jit(solution)/shard_map/ppermute | solution.py:665
  287.9 129.6 %collective-permute-start.34 = (bf16[2,2,256,2048]{3,2,1,0:T(8,128)(2,1)}, bf16[2,2,256,2048]{3,2,1,0:T(8,128)(2,1)}, u32[]{:S(2)}, u32[]{:S(2)}) collective-permute-start(bf16[2,2,256,2048]{3,2,1,0:T(8,128)(2,1)} %bitcast.185), channel_id=1, source_target_pairs={{0,1},{1,0},{2,3},{3,2},{4,5},{5,4},{6,7},{7,6},{8,9},{9,8},{10,11... | collective-permute-start | bytes 12582920 | tf_op jit(solution)/shard_map/ppermute | solution.py:805
  336.2 107.5 %collective-permute-start.38 = (bf16[2,256,2048]{2,1,0:T(8,128)(2,1)}, bf16[2,256,2048]{2,1,0:T(8,128)(2,1)}, u32[]{:S(2)}, u32[]{:S(2)}) collective-permute-start(bf16[2,256,2048]{2,1,0:T(8,128)(2,1)} %bitcast.37), channel_id=1, source_target_pairs={{0,1},{1,0},{2,3},{3,2},{4,5},{5,4},{6,7},{7,6},{8,9},{9,8},{10,11... | collective-permute-start | bytes 6291464 | tf_op jit(solution)/shard_map/ppermute | solution.py:805
  337.0 15.7 %collective-permute-start.21 = (bf16[128,2048]{1,0:T(8,128)(2,1)S(1)}, bf16[128,2048]{1,0:T(8,128)(2,1)S(1)}, u32[]{:S(2)}, u32[]{:S(2)}) collective-permute-start(bf16[128,2048]{1,0:T(8,128)(2,1)S(1)} %get-tuple-element.240), channel_id=1, source_target_pairs={{0,8},{8,16},{16,24},{24,28},{28,20},{20,12},{12,4},{4,0},{1,9},{9... | collective-permute-start | bytes 1572872 | tf_op jit(solution)/shard_map/ppermute | solution.py:767
  349.0 41.2 %collective-permute-start.31 = (bf16[2,256,2048]{2,1,0:T(8,128)(2,1)}, bf16[2,256,2048]{2,1,0:T(8,128)(2,1)S(1)}, u32[]{:S(2)}, u32[]{:S(2)}) collective-permute-start(bf16[2,256,2048]{2,1,0:T(8,128)(2,1)} %bitcast.32), channel_id=1, source_target_pairs={{0,1},{1,0},{2,3},{3,2},{4,5},{5,4},{6,7},{7,6},{8,9},{9,8},{10,11... | collective-permute-start | bytes 6291464 | tf_op jit(solution)/shard_map/ppermute | solution.py:805
  368.0 16.3 %collective-permute-start.26 = (bf16[128,2048]{1,0:T(8,128)(2,1)S(1)}, bf16[128,2048]{1,0:T(8,128)(2,1)S(1)}, u32[]{:S(2)}, u32[]{:S(2)}) collective-permute-start(bf16[128,2048]{1,0:T(8,128)(2,1)S(1)} %get-tuple-element.258), channel_id=1, source_target_pairs={{0,8},{8,16},{16,24},{24,28},{28,20},{20,12},{12,4},{4,0},{1,9},{9... | collective-permute-start | bytes 1572872 | tf_op jit(solution)/shard_map/ppermute | solution.py:767
  392.3 51.4 %collective-permute-start.39 = (bf16[2,256,2048]{2,1,0:T(8,128)(2,1)}, bf16[2,256,2048]{2,1,0:T(8,128)(2,1)}, u32[]{:S(2)}, u32[]{:S(2)}) collective-permute-start(bf16[2,256,2048]{2,1,0:T(8,128)(2,1)} %add_convert_fusion.1), channel_id=1, source_target_pairs={{0,2},{1,3},{2,0},{3,1},{4,6},{5,7},{6,4},{7,5},{8,10},{9,11},{10,... | collective-permute-start | bytes 6291464 | tf_op jit(solution)/shard_map/ppermute | solution.py:808
  393.0 16.8 %collective-permute-start.29 = (bf16[192,2048]{1,0:T(8,128)(2,1)S(1)}, bf16[192,2048]{1,0:T(8,128)(2,1)S(1)}, u32[]{:S(2)}, u32[]{:S(2)}) collective-permute-start(bf16[192,2048]{1,0:T(8,128)(2,1)S(1)} %get-tuple-element.267.one), channel_id=1, source_target_pairs={{0,8},{8,16},{16,24},{24,28},{28,20},{20,12},{12,4},{4,0},{1,9},{9... | collective-permute-start | bytes 2359304 | tf_op jit(solution)/shard_map/ppermute | solution.py:767
  393.3 21.7 %collective-permute-start.30 = (bf16[192,2048]{1,0:T(8,128)(2,1)S(1)}, bf16[192,2048]{1,0:T(8,128)(2,1)S(1)}, u32[]{:S(2)}, u32[]{:S(2)}) collective-permute-start(bf16[192,2048]{1,0:T(8,128)(2,1)S(1)} %get-tuple-element.268.two), channel_id=1, source_target_pairs={{8,0},{16,8},{24,16},{28,24},{20,28},{12,20},{4,12},{0,4},{9,1},{1... | collective-permute-start | bytes 2359304 | tf_op jit(solution)/shard_map/ppermute | solution.py:767
  409.8 17.4 %collective-permute-start.35 = (bf16[80,2048]{1,0:T(8,128)(2,1)S(1)}, bf16[80,2048]{1,0:T(8,128)(2,1)S(1)}, u32[]{:S(2)}, u32[]{:S(2)}) collective-permute-start(bf16[80,2048]{1,0:T(8,128)(2,1)S(1)} %add_convert_fusion.9), channel_id=1, source_target_pairs={{0,16},{4,20},{8,24},{12,28},{16,0},{20,4},{24,8},{28,12},{1,17},{... | collective-permute-start | bytes 983048 | tf_op jit(solution)/shard_map/ppermute | solution.py:1090
  415.0 15.9 %collective-permute-start.32 = (bf16[192,2048]{1,0:T(8,128)(2,1)S(1)}, bf16[192,2048]{1,0:T(8,128)(2,1)S(1)}, u32[]{:S(2)}, u32[]{:S(2)}) collective-permute-start(bf16[192,2048]{1,0:T(8,128)(2,1)S(1)} %collective-permute-done.29.one), channel_id=1, source_target_pairs={{0,8},{8,16},{16,24},{24,28},{28,20},{20,12},{12,4},{4,0},{1,9},{9... | collective-permute-start | bytes 2359304 | tf_op jit(solution)/shard_map/ppermute | solution.py:767
  417.5 17.1 %collective-permute-start.33 = (bf16[192,2048]{1,0:T(8,128)(2,1)S(1)}, bf16[192,2048]{1,0:T(8,128)(2,1)S(1)}, u32[]{:S(2)}, u32[]{:S(2)}) collective-permute-start(bf16[192,2048]{1,0:T(8,128)(2,1)S(1)} %collective-permute-done.30.two), channel_id=1, source_target_pairs={{8,0},{16,8},{24,16},{28,24},{20,28},{12,20},{4,12},{0,4},{9,1},{1... | collective-permute-start | bytes 2359304 | tf_op jit(solution)/shard_map/ppermute | solution.py:767
  427.2 60.0 %collective-permute-start.42 = (bf16[2,256,2048]{2,1,0:T(8,128)(2,1)}, bf16[2,256,2048]{2,1,0:T(8,128)(2,1)}, u32[]{:S(2)}, u32[]{:S(2)}) collective-permute-start(bf16[2,256,2048]{2,1,0:T(8,128)(2,1)} %fusion.14), channel_id=1, source_target_pairs={{0,2},{1,3},{2,0},{3,1},{4,6},{5,7},{6,4},{7,5},{8,10},{9,11},{10,... | collective-permute-start | bytes 6291464 | tf_op jit(solution)/shard_map/ppermute | solution.py:808
  434.6 22.0 %collective-permute-start.36 = (bf16[192,2048]{1,0:T(8,128)(2,1)S(1)}, bf16[192,2048]{1,0:T(8,128)(2,1)S(1)}, u32[]{:S(2)}, u32[]{:S(2)}) collective-permute-start(bf16[192,2048]{1,0:T(8,128)(2,1)S(1)} %collective-permute-done.32.one), channel_id=1, source_target_pairs={{0,8},{8,16},{16,24},{24,28},{28,20},{20,12},{12,4},{4,0},{1,9},{9... | collective-permute-start | bytes 2359304 | tf_op jit(solution)/shard_map/ppermute | solution.py:767
  441.3 16.1 %collective-permute-start.37 = (bf16[192,2048]{1,0:T(8,128)(2,1)S(1)}, bf16[192,2048]{1,0:T(8,128)(2,1)S(1)}, u32[]{:S(2)}, u32[]{:S(2)}) collective-permute-start(bf16[192,2048]{1,0:T(8,128)(2,1)S(1)} %collective-permute-done.33.two), channel_id=1, source_target_pairs={{8,0},{16,8},{24,16},{28,24},{20,28},{12,20},{4,12},{0,4},{9,1},{1... | collective-permute-start | bytes 2359304 | tf_op jit(solution)/shard_map/ppermute | solution.py:767
  457.4 15.4 %collective-permute-start.40 = (bf16[192,2048]{1,0:T(8,128)(2,1)S(1)}, bf16[192,2048]{1,0:T(8,128)(2,1)S(1)}, u32[]{:S(2)}, u32[]{:S(2)}) collective-permute-start(bf16[192,2048]{1,0:T(8,128)(2,1)S(1)} %collective-permute-done.36.one), channel_id=1, source_target_pairs={{0,8},{8,16},{16,24},{24,28},{28,20},{20,12},{12,4},{4,0},{1,9},{9... | collective-permute-start | bytes 2359304 | tf_op jit(solution)/shard_map/ppermute | solution.py:767
  460.2 16.6 %collective-permute-start.41 = (bf16[192,2048]{1,0:T(8,128)(2,1)S(1)}, bf16[192,2048]{1,0:T(8,128)(2,1)S(1)}, u32[]{:S(2)}, u32[]{:S(2)}) collective-permute-start(bf16[192,2048]{1,0:T(8,128)(2,1)S(1)} %collective-permute-done.37.two), channel_id=1, source_target_pairs={{8,0},{16,8},{24,16},{28,24},{20,28},{12,20},{4,12},{0,4},{9,1},{1... | collective-permute-start | bytes 2359304 | tf_op jit(solution)/shard_map/ppermute | solution.py:767
  460.9 17.0 %collective-permute-start.45 = (f32[10,1024]{1,0:T(8,128)S(1)}, f32[10,1024]{1,0:T(8,128)S(1)}, u32[]{:S(2)}, u32[]{:S(2)}) collective-permute-start(f32[10,1024]{1,0:T(8,128)S(1)} %select_maximum_fusion.1), channel_id=1, source_target_pairs={{0,1},{1,0},{2,3},{3,2},{4,5},{5,4},{6,7},{7,6},{8,9},{9,8},{10,11... | collective-permute-start | bytes 122888 | tf_op jit(solution)/shard_map/ppermute | solution.py:1090
  461.0 25.9 %collective-permute-start.46 = (f32[10,1024]{1,0:T(8,128)S(1)}, f32[10,1024]{1,0:T(8,128)S(1)}, u32[]{:S(2)}, u32[]{:S(2)}) collective-permute-start(f32[10,1024]{1,0:T(8,128)S(1)} %select_maximum_fusion.1), channel_id=1, source_target_pairs={{0,2},{1,3},{2,0},{3,1},{4,6},{5,7},{6,4},{7,5},{8,10},{9,11},{10,... | collective-permute-start | bytes 122888 | tf_op jit(solution)/shard_map/ppermute | solution.py:1090
  476.7 46.7 %collective-permute-start.56 = (bf16[64,2048]{1,0:T(8,128)(2,1)S(1)}, bf16[64,2048]{1,0:T(8,128)(2,1)S(1)}, u32[]{:S(2)}, u32[]{:S(2)}) collective-permute-start(bf16[64,2048]{1,0:T(8,128)(2,1)S(1)} %slice.195), channel_id=1, source_target_pairs={{0,2},{1,3},{2,0},{3,1},{4,6},{5,7},{6,4},{7,5},{8,10},{9,11},{10,... | collective-permute-start | bytes 786440 | tf_op jit(solution)/shard_map/ppermute | solution.py:808
  477.9 20.1 %collective-permute-start.43 = (bf16[192,2048]{1,0:T(8,128)(2,1)S(1)}, bf16[192,2048]{1,0:T(8,128)(2,1)S(1)}, u32[]{:S(2)}, u32[]{:S(2)}) collective-permute-start(bf16[192,2048]{1,0:T(8,128)(2,1)S(1)} %collective-permute-done.40.one), channel_id=1, source_target_pairs={{0,8},{8,16},{16,24},{24,28},{28,20},{20,12},{12,4},{4,0},{1,9},{9... | collective-permute-start | bytes 2359304 | tf_op jit(solution)/shard_map/ppermute | solution.py:767
  499.7 26.0 %collective-permute-start.49 = (bf16[192,2048]{1,0:T(8,128)(2,1)S(1)}, bf16[192,2048]{1,0:T(8,128)(2,1)S(1)}, u32[]{:S(2)}, u32[]{:S(2)}) collective-permute-start(bf16[192,2048]{1,0:T(8,128)(2,1)S(1)} %collective-permute-done.43.one), channel_id=1, source_target_pairs={{0,8},{8,16},{16,24},{24,28},{28,20},{20,12},{12,4},{4,0},{1,9},{9... | collective-permute-start | bytes 2359304 | tf_op jit(solution)/shard_map/ppermute | solution.py:767
  500.7 25.1 %collective-permute-start.50 = (bf16[192,2048]{1,0:T(8,128)(2,1)S(1)}, bf16[192,2048]{1,0:T(8,128)(2,1)S(1)}, u32[]{:S(2)}, u32[]{:S(2)}) collective-permute-start(bf16[192,2048]{1,0:T(8,128)(2,1)S(1)} %collective-permute-done.44.two), channel_id=1, source_target_pairs={{8,0},{16,8},{24,16},{28,24},{20,28},{12,20},{4,12},{0,4},{9,1},{1... | collective-permute-start | bytes 2359304 | tf_op jit(solution)/shard_map/ppermute | solution.py:767
  501.7 18.4 %collective-permute-start.48 = (f32[26,1024]{1,0:T(8,128)S(1)}, f32[26,1024]{1,0:T(8,128)S(1)}, u32[]{:S(2)}, u32[]{:S(2)}) collective-permute-start(f32[26,1024]{1,0:T(8,128)S(1)} %fusion.53), channel_id=1, source_target_pairs={{0,4},{4,0},{8,12},{12,8},{16,20},{20,16},{24,28},{28,24},{1,5},{5... | collective-permute-start | bytes 319496 | tf_op jit(solution)/shard_map/ppermute | solution.py:1090
  530.1 19.6 %collective-permute-start.54 = (bf16[192,2048]{1,0:T(8,128)(2,1)S(1)}, bf16[192,2048]{1,0:T(8,128)(2,1)S(1)}, u32[]{:S(2)}, u32[]{:S(2)}) collective-permute-start(bf16[192,2048]{1,0:T(8,128)(2,1)S(1)} %collective-permute-done.49.one), channel_id=1, source_target_pairs={{0,8},{8,16},{16,24},{24,28},{28,20},{20,12},{12,4},{4,0},{1,9},{9... | collective-permute-start | bytes 2359304 | tf_op jit(solution)/shard_map/ppermute | solution.py:767
  530.2 19.6 %collective-permute-start.55 = (bf16[192,2048]{1,0:T(8,128)(2,1)S(1)}, bf16[192,2048]{1,0:T(8,128)(2,1)S(1)}, u32[]{:S(2)}, u32[]{:S(2)}) collective-permute-start(bf16[192,2048]{1,0:T(8,128)(2,1)S(1)} %collective-permute-done.50.two), channel_id=1, source_target_pairs={{8,0},{16,8},{24,16},{28,24},{20,28},{12,20},{4,12},{0,4},{9,1},{1... | collective-permute-start | bytes 2359304 | tf_op jit(solution)/shard_map/ppermute | solution.py:767
  (80 other events, 763.1 us)

commit v4 on v3

--- a/solution.py
+++ b/solution.py
@@ -1091,8 +1091,8 @@
             return [values]
 
         def receive(hold):
-            values, others = made[name]
-            terms = [hold(values).astype(F32)] + [other.astype(F32) for other in others]
+            values, others = hold(made[name])
+            terms = [values.astype(F32)] + [other.astype(F32) for other in others]
             while len(terms) > 1:
                 terms = [terms[i] + terms[i + 1] for i in range(0, len(terms), 2)]
             made[name] = terms[0].astype(kind)
@@ -1108,7 +1108,7 @@
 
     bits_of = lambda size: list(range((size - 1).bit_length()))
     tensor_send, tensor_take = spread_sum("small", "tensor", ranks, bits_of(ranks))
-    small_dp = [spread_sum("small", "dp", dps, bits) for bits in (bits_of(dps)[:1], bits_of(dps)[1:])]
+    small_dp = [spread_sum("small", "dp", dps, bits) for bits in (bits_of(dps)[1:], bits_of(dps)[:1])]
     if ringed:
         side_dp = [spread_sum("side_part", "dp", dps, [bit], BF16) for bit in range(3)]
     else:
@@ -1156,25 +1156,27 @@
         together(side_dp[0][1], side_dp[1][0], *far[1:2]),
         *far[2:],
         together(*near[:1], finish),
-        together(side_dp[1][1], side_dp[2][0], *near[1:2]),
+        together(side_dp[1][1], *near[1:2]),
         *near[2:],
         together(input_pair, pass_on("input")),
-        together(pass_on("mixed"), side_dp[2][1]),
-        input_rows,
+        together(pass_on("mixed"), side_dp[2][0]),
+        together(input_rows, side_dp[2][1]),
         together(small_start, tensor_send, input_order, gather_near),
         together(tensor_take, pack, small_dp[0][0], block_rows),
-        together(small_dp[0][1], small_dp[1][0], block_order, gather_far),
-        together(small_dp[1][1], small_outputs, side_outputs),
+        together(block_order, gather_far),
+        together(small_dp[0][1], small_dp[1][0], side_outputs),
     ]
     if ringed:
         sums = [blank((model, channels)), blank((model, channels)), blank((channels, model))]
-        sums, _ = ring.all_reduce(low_part, sums, fillers, finished)
+        sums, last = ring.all_reduce(low_part, sums, fillers, finished)
         grads = dict(zip(("gate", "inner", "out"), sums))
     else:
         low_sum = lax.psum(low_part, "dp").astype(F32)
         grads = {"gate": low_sum[:, :channels], "inner": low_sum[:, channels:], "out": out_sum.astype(F32)}
         for filler in fillers:
             filler(lambda values: values)
+    finish_small = together(small_dp[1][1], small_outputs)
+    finish_small((lambda values: after(values, *last)) if ringed else (lambda values: values))
     gain, kernel_grad, offset_grad, shared_kernel_grad, shared_offset_grad, bias_grad, rate_grad, skip_grad, gate_gain_grad = made[
         "outputs"
     ]

time: 558 us -> 556 us (level)
    ppermute x10, waiting for transfers between devices: 29.4 us -> 14.4 us  [send(): lax.ppermute(values, axis, [(i, i ^ k) for i in range(size)])]
    ppermute x28, waiting for transfers between devices: 50.3 us -> 60.4 us  [send(): lax.ppermute(values, 'dp', self.pairs[way])]
    unnamed x115 -> x117, local copies, waits for them, and re-layouts: 26.2 us -> 26.4 us
  transfers between devices with their start and end apart: 59 -> 59, of which waited for: 23 -> 26; matrix products, arithmetic and copies ran while one was open for 30% -> 30% of each run, Pallas kernels for 31% -> 31%
where the time goes in v4:
time: 556 us; the launch traced here: 550 us
  Pallas kernels  192 us (35%)
  matrix products  106 us (19%)
  waiting for transfers between devices  85.1 us (15%)
  starting transfers between devices  65.9 us (12%)
  local copies, waits for them, and re-layouts  51.6 us (9%)
  other arithmetic  47.3 us (9%)
    pallas_call x2, Pallas kernels, scan_backward(): pl.pallas_call(partial(backward_kernel, channels, start), name='scan_back...  68 us
    pallas_call x4, Pallas kernels, fill_rows(): pl.pallas_call(partial(fill_kernel, dims, spans, 1 if second else 0), nam...  63.1 us
    ppermute x28, waiting for transfers between devices, send(): lax.ppermute(values, 'dp', self.pairs[way])  60.4 us
    ppermute x28, starting transfers between devices, send(): lax.ppermute(values, 'dp', self.pairs[way])  37.9 us
    dot_general x4, matrix products, run(): lax.dot_general(low_rows[part], weight_low, NT, preferred_element_type=F32)  31.1 us
    pallas_call x1, Pallas kernels, scan_forward(): pl.pallas_call(partial(forward_kernel, channels), name='scan_forward', gr...  26.9 us
    unnamed x117, local copies, waits for them, and re-layouts  26.4 us
    dot_general x1, matrix products, body(): lax.dot_general(normed_in, after(low, given), TN, preferred_element_type=...  22.6 us
  transfers between devices with their start and end apart: 59, of which 26 were waited for; matrix products, arithmetic and copies ran while one was open for 30% of the time, Pallas kernels for 31%

profile of v4, /device:TPU:0, one launch (start us, length us, event | category | flops | bytes accessed | tf_op | source)
XLA Modules:
  0.0 550.1 jit_solution(16835941429970882470)
XLA Ops:
  24.0 10.8 %fill_rows.5 = (bf16[2048,1024]{1,0:T(8,128)(2,1)}, bf16[2048,2048]{1,0:T(8,128)(2,1)}) custom-call(bf16[512,2048]{1,0:T(8,128)(2,1)} %pad_maximum_fusion.1.own, bf16[512,2048]{1,0:T(8,128)(2,1)} %collective-permute-done.2.other, bf16[1024,2048]{1,0:T(8,128)(2,1)} %rest_0_.7), custom_call_target="tpu_custom_call" | custom-call | flops 4294967296 | bytes 6291456 | tf_op jit(solution)/shard_map/fill_rows/pallas_call | solution.py:378
  34.9 20.9 %fill_rows.4 = (f32[2048,2560]{1,0:T(8,128)}, bf16[2048,2048]{1,0:T(8,128)(2,1)}) custom-call(bf16[512,2048]{1,0:T(8,128)(2,1)} %fusion.3.own, bf16[512,2048]{1,0:T(8,128)(2,1)} %collective-permute-done.1.other, bf16[2048,1024]{1,0:T(8,128)(2,1)} %rest_0_.6, bf16[2048,1024]{1,0:T(8,128)(2,1)} %rest_1_.3, bf16[2048,512]{1,0:T(8,128)(2,1)} %maximum_maximum_fusion.rest_2_), custom_call_target="tpu_custom_call" | custom-call | flops 10737418240 | bytes 9437184 | tf_op jit(solution)/shard_map/fill_rows/pallas_call | solution.py:378
  64.3 20.9 %fill_rows.6 = (f32[2048,2560]{1,0:T(8,128)}, bf16[2048,2048]{1,0:T(8,128)(2,1)}) custom-call(bf16[512,2048]{1,0:T(8,128)(2,1)} %collective-permute-done.own, bf16[512,2048]{1,0:T(8,128)(2,1)} %collective-permute-done.3.other, bf16[2048,1024]{1,0:T(8,128)(2,1)} %rest_0_.6, bf16[2048,1024]{1,0:T(8,128)(2,1)} %rest_1_.3, ...), custom_call_target="tpu_custom_call", output_to_operand_aliasing={{0}: (5, {}), {1}: (6, {})} | custom-call | flops 10737418240 | bytes 9437184 | tf_op jit(solution)/shard_map/fill_rows/pallas_call | solution.py:378
  85.2 26.9 %scan_forward.1 = (f32[2048,1024]{1,0:T(8,128)}, bf16[2048,1024]{1,0:T(8,128)(2,1)}, bf16[2,4,128,1024]{3,2,1,0:T(8,128)(2,1)}, f32[1,2048]{1,0:T(1,128)}) custom-call(s32[4]{0:T(128)} %get-tuple-element.433.slots, s32[2,1024]{1,0:T(2,128)} %seg_sm.5, s32[2,2]{1,0:T(2,128)} %span_sm.5, f32[2048,2560]{1,0:T(8,128)} %get-tuple-element.191.pre.halo, ...), custom_call_target="tpu_custom_call" | custom-call | flops 20000000000 | bytes 40000000 | tf_op jit(solution)/shard_map/scan_forward/pallas_call | solution.py:411
  112.4 3.9 collective-permute-done.5.other
  117.7 10.5 %fill_rows.7 = (bf16[2048,1024]{1,0:T(8,128)(2,1)}, bf16[2048,2048]{1,0:T(8,128)(2,1)}) custom-call(bf16[512,2048]{1,0:T(8,128)(2,1)} %copy-done.23, bf16[512,2048]{1,0:T(8,128)(2,1)} %copy-done.24, bf16[1024,2048]{1,0:T(8,128)(2,1)} %rest_0_.7, bf16[2048,1024]{1,0:T(8,128)(2,1)} %get-tuple-element.187.rest_1_, ...), custom_call_target="tpu_custom_call", output_to_operand_aliasing={{0}: (3, {}), {1}: (4, {})} | custom-call | flops 4294967296 | bytes 6291456 | tf_op jit(solution)/shard_map/fill_rows/pallas_call | solution.py:378
  148.4 9.9 %fusion.81 = bf16[512,2048]{1,0:T(8,128)(2,1)} fusion(bf16[2048,512]{1,0:T(8,128)(2,1)S(1)} %get-tuple-element.201, bf16[2048,2048]{1,0:T(8,128)(2,1)} %get-tuple-element.202), kind=kOutput, calls=%fused_computation.167 | convolution fusion | flops 4294967296 | bytes 12582912 | tf_op jit(solution)/shard_map/dot_general | solution.py:934
  159.8 5.8 %fusion.82.mine = bf16[512,2048]{1,0:T(8,128)(2,1)} fusion(bf16[2048,512]{1,0:T(8,128)(2,1)S(1)} %get-tuple-element.203, bf16[2048,2048]{1,0:T(8,128)(2,1)S(1)} %bitcast.163), kind=kOutput, calls=%fused_computation.168 | convolution fusion | flops 4294967296 | bytes 12582912 | tf_op jit(solution)/shard_map/dot_general | solution.py:934
  165.6 34.1 %scan_backward.2 = (bf16[2048,2048]{1,0:T(8,128)(2,1)}, bf16[2048,256]{1,0:T(8,128)(2,1)}, bf16[2048,128]{1,0:T(8,128)(2,1)}, f32[8,1024]{1,0:T(8,128)}, f32[8,128]{1,0:T(8,128)}, /*index=5*/f32[8,256]{1,0:T(8,128)}) custom-call(s32[4]{0:T(128)} %get-tuple-element.433.slots, s32[2,1024]{1,0:T(2,128)} %seg_sm.5, s32[2,2]{1,0:T(2,128)} %span_sm.5, ...), custom_call_target="tpu_custom_call" | custom-call | flops 22000001024 | bytes 30000000 | tf_op jit(solution)/shard_map/scan_backward/pallas_call | solution.py:552
  199.7 9.4 %fusion.83 = bf16[1024,2048]{1,0:T(8,128)(2,1)} fusion(bf16[1024,1024]{1,0:T(8,128)(2,1)} %copy-done.11, bf16[1024,2048]{1,0:T(8,128)(2,1)} %rest_0_.7), kind=kOutput, calls=%fused_computation.169 | convolution fusion | flops 4294967296 | bytes 10485760 | tf_op jit(solution)/shard_map/dot_general | solution.py:949
  213.4 34.0 %scan_backward.3 = (bf16[2048,2048]{1,0:T(8,128)(2,1)}, bf16[2048,256]{1,0:T(8,128)(2,1)}, bf16[2048,128]{1,0:T(8,128)(2,1)}, f32[8,1024]{1,0:T(8,128)}, f32[8,128]{1,0:T(8,128)}, /*index=5*/f32[8,256]{1,0:T(8,128)}) custom-call(s32[4]{0:T(128)} %get-tuple-element.433.slots, ...), custom_call_target="tpu_custom_call", output_to_operand_aliasing={{0}: (20, {}), {1}: (21, {}), {2}: (22, {})} | custom-call | flops 22000001024 | bytes 30000000 | tf_op jit(solution)/shard_map/scan_backward/pallas_call | solution.py:552
  251.1 22.6 %fusion.84.one.two = bf16[2048,2048]{1,0:T(8,128)(2,1)S(1)} fusion(bf16[2048,2048]{1,0:T(8,128)(2,1)} %get-tuple-element.190, bf16[2048,2048]{1,0:T(8,128)(2,1)} %get-tuple-element.275), kind=kOutput, calls=%fused_computation.170 | convolution fusion | flops 17179869184 | bytes 25165824 | tf_op jit(solution)/shard_map/dot_general | solution.py:955
  281.4 4.7 dynamic-slice_bitcast_fusion.7
  298.1 6.1 %fusion.85 = bf16[1024,2048]{1,0:T(8,128)(2,1)} fusion(bf16[1024,1024]{1,0:T(8,128)(2,1)S(1)} %copy-done.10, bf16[1024,2048]{1,0:T(8,128)(2,1)S(1)} %copy-done.20), kind=kOutput, calls=%fused_computation.171 | convolution fusion | flops 4294967296 | bytes 10485760 | tf_op jit(solution)/shard_map/dot_general | solution.py:1031
  315.7 5.1 fusion.50
  324.9 8.0 %fusion.22 = f32[512,2048]{1,0:T(8,128)S(1)} fusion(bf16[2048,2048]{1,0:T(8,128)(2,1)} %copy-done.25, bf16[2048,2048]{1,0:T(8,128)(2,1)} %get-tuple-element.275), kind=kOutput, calls=%fused_computation.42 | convolution fusion | flops 4294967296 | bytes 14680064 | tf_op jit(solution)/shard_map/dot_general | solution.py:1010
  339.5 7.6 %fusion.20 = f32[512,2048]{1,0:T(8,128)S(1)} fusion(bf16[2048,2048]{1,0:T(8,128)(2,1)} %copy-done.25, bf16[2048,2048]{1,0:T(8,128)(2,1)} %get-tuple-element.275), kind=kOutput, calls=%fused_computation.40 | convolution fusion | flops 4294967296 | bytes 14680064 | tf_op jit(solution)/shard_map/dot_general | solution.py:1010
  355.8 7.6 %fusion.18 = f32[512,2048]{1,0:T(8,128)S(1)} fusion(bf16[2048,2048]{1,0:T(8,128)(2,1)} %copy-done.25, bf16[2048,2048]{1,0:T(8,128)(2,1)} %get-tuple-element.275), kind=kOutput, calls=%fused_computation.38 | convolution fusion | flops 4294967296 | bytes 14680064 | tf_op jit(solution)/shard_map/dot_general | solution.py:1010
  370.4 7.8 %fusion.16 = f32[512,2048]{1,0:T(8,128)S(1)} fusion(bf16[2048,2048]{1,0:T(8,128)(2,1)} %copy-done.25, bf16[2048,2048]{1,0:T(8,128)(2,1)} %get-tuple-element.275), kind=kOutput, calls=%fused_computation.36 | convolution fusion | flops 4294967296 | bytes 14680064 | tf_op jit(solution)/shard_map/dot_general | solution.py:1010
  391.8 11.7 %collective-permute-done.29.one = bf16[192,2048]{1,0:T(8,128)(2,1)S(1)} collective-permute-done((bf16[192,2048]{1,0:T(8,128)(2,1)S(1)}, bf16[192,2048]{1,0:T(8,128)(2,1)S(1)}, u32[]{:S(2)}, u32[]{:S(2)}) %collective-permute-start.29) | collective-permute-done | bytes 786464 | tf_op jit(solution)/shard_map/ppermute | solution.py:767
  409.1 3.7 fusion.14
  412.8 9.5 %collective-permute-done.32.one = bf16[192,2048]{1,0:T(8,128)(2,1)S(1)} collective-permute-done((bf16[192,2048]{1,0:T(8,128)(2,1)S(1)}, bf16[192,2048]{1,0:T(8,128)(2,1)S(1)}, u32[]{:S(2)}, u32[]{:S(2)}) %collective-permute-start.32) | collective-permute-done | bytes 786464 | tf_op jit(solution)/shard_map/ppermute | solution.py:767
  423.6 8.6 %collective-permute-start.35 = (bf16[192,2048]{1,0:T(8,128)(2,1)S(1)}, bf16[192,2048]{1,0:T(8,128)(2,1)S(1)}, u32[]{:S(2)}, u32[]{:S(2)}) collective-permute-start(bf16[192,2048]{1,0:T(8,128)(2,1)S(1)} %collective-permute-done.32.one), channel_id=1, source_target_pairs={{0,8},{8,16},{16,24},{24,28},{28,20},{20,12},{12,4},{4,0},{1,9},{9... | collective-permute-start | bytes 2359304 | tf_op jit(solution)/shard_map/ppermute | solution.py:767
  432.2 6.3 %collective-permute-done.39 = bf16[80,2048]{1,0:T(8,128)(2,1)S(1)} collective-permute-done((bf16[80,2048]{1,0:T(8,128)(2,1)S(1)}, bf16[80,2048]{1,0:T(8,128)(2,1)S(1)}, u32[]{:S(2)}, u32[]{:S(2)}) %collective-permute-start.39) | collective-permute-done | bytes 327712 | tf_op jit(solution)/shard_map/ppermute | solution.py:1090
  442.6 4.1 fusion.9
  446.8 8.6 %fusion.7 = bf16[2,256,2048]{2,1,0:T(8,128)(2,1)} fusion(bf16[2,256,2048]{2,1,0:T(8,128)(2,1)S(1)} %bitcast.158, bf16[2,256,2048]{2,1,0:T(8,128)(2,1)} %bitcast.66, f32[2,256]{1,0:T(2,128)S(1)} %fusion.74, f32[2048]{0:T(1024)S(1)} %copy-done.39, f32[2,256]{1,0:T(2,128)S(1)} %rsqrt.20, bf16[2,256,2048]{2,1,0:T(8,128)(2,1)} %collective-permute-done.38, ...), kind=kOutput, calls=%fused_computation.12 | output fusion | flops 23071232 | bytes 12595200 | tf_op jit(solution)/shard_map/mul | solution.py:1052
  473.4 6.0 %collective-permute-done.46 = f32[10,1024]{1,0:T(8,128)S(1)} collective-permute-done((f32[10,1024]{1,0:T(8,128)S(1)}, f32[10,1024]{1,0:T(8,128)S(1)}, u32[]{:S(2)}, u32[]{:S(2)}) %collective-permute-start.46) | collective-permute-done | bytes 40992 | tf_op jit(solution)/shard_map/ppermute | solution.py:1090
  481.1 4.0 fusion.12
  487.5 5.5 collective-permute-done.43.one
  498.3 3.8 collective-permute-start.50
  503.2 10.5 %collective-permute-done.51.one = bf16[192,2048]{1,0:T(8,128)(2,1)S(1)} collective-permute-done((bf16[192,2048]{1,0:T(8,128)(2,1)S(1)}, bf16[192,2048]{1,0:T(8,128)(2,1)S(1)}, u32[]{:S(2)}, u32[]{:S(2)}) %collective-permute-start.51) | collective-permute-done | bytes 786464 | tf_op jit(solution)/shard_map/ppermute | solution.py:767
  535.5 4.0 collective-permute-done.54.one
  (335 shorter events, 205.1 us)
Async XLA Ops:
  5.8 18.2 %collective-permute-start.2 = (bf16[512,2048]{1,0:T(8,128)(2,1)}, bf16[512,2048]{1,0:T(8,128)(2,1)}, u32[]{:S(2)}, u32[]{:S(2)}) collective-permute-start(bf16[512,2048]{1,0:T(8,128)(2,1)} %pad_maximum_fusion.1.own), channel_id=1, source_target_pairs={{0,1},{1,0},{2,3},{3,2},{4,5},{5,4},{6,7},{7,6},{8,9},{9,8},{10,11... | collective-permute-start | bytes 6291464 | tf_op jit(solution)/shard_map/ppermute | solution.py:805
  9.7 25.2 %collective-permute-start.1 = (bf16[512,2048]{1,0:T(8,128)(2,1)}, bf16[512,2048]{1,0:T(8,128)(2,1)}, u32[]{:S(2)}, u32[]{:S(2)}) collective-permute-start(bf16[512,2048]{1,0:T(8,128)(2,1)} %fusion.3.own), channel_id=1, source_target_pairs={{0,1},{1,0},{2,3},{3,2},{4,5},{5,4},{6,7},{7,6},{8,9},{9,8},{10,11... | collective-permute-start | bytes 6291464 | tf_op jit(solution)/shard_map/ppermute | solution.py:805
  9.8 49.1 %collective-permute-start = (bf16[512,2048]{1,0:T(8,128)(2,1)}, bf16[512,2048]{1,0:T(8,128)(2,1)}, u32[]{:S(2)}, u32[]{:S(2)}) collective-permute-start(bf16[512,2048]{1,0:T(8,128)(2,1)} %fusion.3.own), channel_id=1, source_target_pairs={{0,2},{1,3},{2,0},{3,1},{4,6},{5,7},{6,4},{7,5},{8,10},{9,11},{10,... | collective-permute-start | bytes 6291464 | tf_op jit(solution)/shard_map/ppermute | solution.py:808
  58.9 53.3 %collective-permute-start.4 = (bf16[512,2048]{1,0:T(8,128)(2,1)}, bf16[512,2048]{1,0:T(8,128)(2,1)S(1)}, u32[]{:S(2)}, u32[]{:S(2)}) collective-permute-start(bf16[512,2048]{1,0:T(8,128)(2,1)} %pad_maximum_fusion.1.own), channel_id=1, source_target_pairs={{0,2},{1,3},{2,0},{3,1},{4,6},{5,7},{6,4},{7,5},{8,10},{9,11},{10,... | collective-permute-start | bytes 6291464 | tf_op jit(solution)/shard_map/ppermute | solution.py:808
  158.3 50.8 %collective-permute-start.8 = (bf16[512,2048]{1,0:T(8,128)(2,1)}, bf16[512,2048]{1,0:T(8,128)(2,1)S(1)}, u32[]{:S(2)}, u32[]{:S(2)}) collective-permute-start(bf16[512,2048]{1,0:T(8,128)(2,1)} %fusion.81), channel_id=1, source_target_pairs={{0,4},{4,0},{8,12},{12,8},{16,20},{20,16},{24,28},{28,24},{1,5},{5... | collective-permute-start | bytes 6291464 | tf_op jit(solution)/shard_map/ppermute | solution.py:665
  211.8 35.6 %collective-permute-start.9 = (bf16[256,2048]{1,0:T(8,128)(2,1)}, bf16[256,2048]{1,0:T(8,128)(2,1)S(1)}, u32[]{:S(2)}, u32[]{:S(2)}) collective-permute-start(bf16[256,2048]{1,0:T(8,128)(2,1)} %get-tuple-element.209), channel_id=1, source_target_pairs={{0,8},{4,12},{8,0},{12,4},{16,24},{20,28},{24,16},{28,20},{1,9},{5... | collective-permute-start | bytes 3145736 | tf_op jit(solution)/shard_map/ppermute | solution.py:665
  248.5 25.2 %collective-permute-start.10 = (bf16[128,2048]{1,0:T(8,128)(2,1)S(1)}, bf16[128,2048]{1,0:T(8,128)(2,1)}, u32[]{:S(2)}, u32[]{:S(2)}) collective-permute-start(bf16[128,2048]{1,0:T(8,128)(2,1)S(1)} %get-tuple-element.219), channel_id=1, source_target_pairs={{0,16},{4,20},{8,24},{12,28},{16,0},{20,4},{24,8},{28,12},{1,17},{... | collective-permute-start | bytes 1572872 | tf_op jit(solution)/shard_map/ppermute | solution.py:665
  288.2 120.0 %collective-permute-start.34 = (bf16[2,2,256,2048]{3,2,1,0:T(8,128)(2,1)}, bf16[2,2,256,2048]{3,2,1,0:T(8,128)(2,1)}, u32[]{:S(2)}, u32[]{:S(2)}) collective-permute-start(bf16[2,2,256,2048]{3,2,1,0:T(8,128)(2,1)} %bitcast.185), channel_id=1, source_target_pairs={{0,1},{1,0},{2,3},{3,2},{4,5},{5,4},{6,7},{7,6},{8,9},{9,8},{10,11... | collective-permute-start | bytes 12582920 | tf_op jit(solution)/shard_map/ppermute | solution.py:805
  347.3 31.7 %collective-permute-start.28 = (bf16[80,2048]{1,0:T(8,128)(2,1)S(1)}, bf16[80,2048]{1,0:T(8,128)(2,1)}, u32[]{:S(2)}, u32[]{:S(2)}) collective-permute-start(bf16[80,2048]{1,0:T(8,128)(2,1)S(1)} %add_convert_fusion.10), channel_id=1, source_target_pairs={{0,8},{4,12},{8,0},{12,4},{16,24},{20,28},{24,16},{28,20},{1,9},{5... | collective-permute-start | bytes 983048 | tf_op jit(solution)/shard_map/ppermute | solution.py:1090
  350.8 31.3 %collective-permute-start.31 = (bf16[2,256,2048]{2,1,0:T(8,128)(2,1)}, bf16[2,256,2048]{2,1,0:T(8,128)(2,1)S(1)}, u32[]{:S(2)}, u32[]{:S(2)}) collective-permute-start(bf16[2,256,2048]{2,1,0:T(8,128)(2,1)} %bitcast.32), channel_id=1, source_target_pairs={{0,1},{1,0},{2,3},{3,2},{4,5},{5,4},{6,7},{7,6},{8,9},{9,8},{10,11... | collective-permute-start | bytes 6291464 | tf_op jit(solution)/shard_map/ppermute | solution.py:805
  379.0 63.6 %collective-permute-start.37 = (bf16[2,256,2048]{2,1,0:T(8,128)(2,1)}, bf16[2,256,2048]{2,1,0:T(8,128)(2,1)}, u32[]{:S(2)}, u32[]{:S(2)}) collective-permute-start(bf16[2,256,2048]{2,1,0:T(8,128)(2,1)} %bitcast.37), channel_id=1, source_target_pairs={{0,1},{1,0},{2,3},{3,2},{4,5},{5,4},{6,7},{7,6},{8,9},{9,8},{10,11... | collective-permute-start | bytes 6291464 | tf_op jit(solution)/shard_map/ppermute | solution.py:805
  384.3 58.3 %collective-permute-start.38 = (bf16[2,256,2048]{2,1,0:T(8,128)(2,1)}, bf16[2,256,2048]{2,1,0:T(8,128)(2,1)}, u32[]{:S(2)}, u32[]{:S(2)}) collective-permute-start(bf16[2,256,2048]{2,1,0:T(8,128)(2,1)} %add_convert_fusion.1), channel_id=1, source_target_pairs={{0,2},{1,3},{2,0},{3,1},{4,6},{5,7},{6,4},{7,5},{8,10},{9,11},{10,... | collective-permute-start | bytes 6291464 | tf_op jit(solution)/shard_map/ppermute | solution.py:808
  385.0 18.5 %collective-permute-start.29 = (bf16[192,2048]{1,0:T(8,128)(2,1)S(1)}, bf16[192,2048]{1,0:T(8,128)(2,1)S(1)}, u32[]{:S(2)}, u32[]{:S(2)}) collective-permute-start(bf16[192,2048]{1,0:T(8,128)(2,1)S(1)} %get-tuple-element.278.one), channel_id=1, source_target_pairs={{0,8},{8,16},{16,24},{24,28},{28,20},{20,12},{12,4},{4,0},{1,9},{9... | collective-permute-start | bytes 2359304 | tf_op jit(solution)/shard_map/ppermute | solution.py:767
  386.2 17.6 %collective-permute-start.30 = (bf16[192,2048]{1,0:T(8,128)(2,1)S(1)}, bf16[192,2048]{1,0:T(8,128)(2,1)S(1)}, u32[]{:S(2)}, u32[]{:S(2)}) collective-permute-start(bf16[192,2048]{1,0:T(8,128)(2,1)S(1)} %get-tuple-element.279.two), channel_id=1, source_target_pairs={{8,0},{16,8},{24,16},{28,24},{20,28},{12,20},{4,12},{0,4},{9,1},{1... | collective-permute-start | bytes 2359304 | tf_op jit(solution)/shard_map/ppermute | solution.py:767
  403.8 18.6 %collective-permute-start.32 = (bf16[192,2048]{1,0:T(8,128)(2,1)S(1)}, bf16[192,2048]{1,0:T(8,128)(2,1)S(1)}, u32[]{:S(2)}, u32[]{:S(2)}) collective-permute-start(bf16[192,2048]{1,0:T(8,128)(2,1)S(1)} %collective-permute-done.29.one), channel_id=1, source_target_pairs={{0,8},{8,16},{16,24},{24,28},{28,20},{20,12},{12,4},{4,0},{1,9},{9... | collective-permute-start | bytes 2359304 | tf_op jit(solution)/shard_map/ppermute | solution.py:767
  404.4 19.3 %collective-permute-start.33 = (bf16[192,2048]{1,0:T(8,128)(2,1)S(1)}, bf16[192,2048]{1,0:T(8,128)(2,1)S(1)}, u32[]{:S(2)}, u32[]{:S(2)}) collective-permute-start(bf16[192,2048]{1,0:T(8,128)(2,1)S(1)} %collective-permute-done.30.two), channel_id=1, source_target_pairs={{8,0},{16,8},{24,16},{28,24},{20,28},{12,20},{4,12},{0,4},{9,1},{1... | collective-permute-start | bytes 2359304 | tf_op jit(solution)/shard_map/ppermute | solution.py:767
  408.2 30.3 %collective-permute-start.39 = (bf16[80,2048]{1,0:T(8,128)(2,1)S(1)}, bf16[80,2048]{1,0:T(8,128)(2,1)S(1)}, u32[]{:S(2)}, u32[]{:S(2)}) collective-permute-start(bf16[80,2048]{1,0:T(8,128)(2,1)S(1)} %add_convert_fusion.9), channel_id=1, source_target_pairs={{0,16},{4,20},{8,24},{12,28},{16,0},{20,4},{24,8},{28,12},{1,17},{... | collective-permute-start | bytes 983048 | tf_op jit(solution)/shard_map/ppermute | solution.py:1090
  422.4 58.7 %collective-permute-start.42 = (bf16[2,256,2048]{2,1,0:T(8,128)(2,1)}, bf16[2,256,2048]{2,1,0:T(8,128)(2,1)}, u32[]{:S(2)}, u32[]{:S(2)}) collective-permute-start(bf16[2,256,2048]{2,1,0:T(8,128)(2,1)} %fusion.14), channel_id=1, source_target_pairs={{0,2},{1,3},{2,0},{3,1},{4,6},{5,7},{6,4},{7,5},{8,10},{9,11},{10,... | collective-permute-start | bytes 6291464 | tf_op jit(solution)/shard_map/ppermute | solution.py:808
  423.6 31.8 %collective-permute-start.35 = (bf16[192,2048]{1,0:T(8,128)(2,1)S(1)}, bf16[192,2048]{1,0:T(8,128)(2,1)S(1)}, u32[]{:S(2)}, u32[]{:S(2)}) collective-permute-start(bf16[192,2048]{1,0:T(8,128)(2,1)S(1)} %collective-permute-done.32.one), channel_id=1, source_target_pairs={{0,8},{8,16},{16,24},{24,28},{28,20},{20,12},{12,4},{4,0},{1,9},{9... | collective-permute-start | bytes 2359304 | tf_op jit(solution)/shard_map/ppermute | solution.py:767
  438.5 16.9 %collective-permute-start.36 = (bf16[192,2048]{1,0:T(8,128)(2,1)S(1)}, bf16[192,2048]{1,0:T(8,128)(2,1)S(1)}, u32[]{:S(2)}, u32[]{:S(2)}) collective-permute-start(bf16[192,2048]{1,0:T(8,128)(2,1)S(1)} %collective-permute-done.33.two), channel_id=1, source_target_pairs={{8,0},{16,8},{24,16},{28,24},{20,28},{12,20},{4,12},{0,4},{9,1},{1... | collective-permute-start | bytes 2359304 | tf_op jit(solution)/shard_map/ppermute | solution.py:767
  459.3 20.1 %collective-permute-start.46 = (f32[10,1024]{1,0:T(8,128)S(1)}, f32[10,1024]{1,0:T(8,128)S(1)}, u32[]{:S(2)}, u32[]{:S(2)}) collective-permute-start(f32[10,1024]{1,0:T(8,128)S(1)} %select_maximum_fusion.1), channel_id=1, source_target_pairs={{0,2},{1,3},{2,0},{3,1},{4,6},{5,7},{6,4},{7,5},{8,10},{9,11},{10,... | collective-permute-start | bytes 122888 | tf_op jit(solution)/shard_map/ppermute | solution.py:1090
  471.7 26.6 %collective-permute-start.56 = (bf16[64,2048]{1,0:T(8,128)(2,1)S(1)}, bf16[64,2048]{1,0:T(8,128)(2,1)S(1)}, u32[]{:S(2)}, u32[]{:S(2)}) collective-permute-start(bf16[64,2048]{1,0:T(8,128)(2,1)S(1)} %slice.194), channel_id=1, source_target_pairs={{0,2},{1,3},{2,0},{3,1},{4,6},{5,7},{6,4},{7,5},{8,10},{9,11},{10,... | collective-permute-start | bytes 786440 | tf_op jit(solution)/shard_map/ppermute | solution.py:808
  473.0 20.0 %collective-permute-start.43 = (bf16[192,2048]{1,0:T(8,128)(2,1)S(1)}, bf16[192,2048]{1,0:T(8,128)(2,1)S(1)}, u32[]{:S(2)}, u32[]{:S(2)}) collective-permute-start(bf16[192,2048]{1,0:T(8,128)(2,1)S(1)} %collective-permute-done.40.one), channel_id=1, source_target_pairs={{0,8},{8,16},{16,24},{24,28},{28,20},{20,12},{12,4},{4,0},{1,9},{9... | collective-permute-start | bytes 2359304 | tf_op jit(solution)/shard_map/ppermute | solution.py:767
  479.4 16.2 %collective-permute-start.44 = (bf16[192,2048]{1,0:T(8,128)(2,1)S(1)}, bf16[192,2048]{1,0:T(8,128)(2,1)S(1)}, u32[]{:S(2)}, u32[]{:S(2)}) collective-permute-start(bf16[192,2048]{1,0:T(8,128)(2,1)S(1)} %collective-permute-done.41.two), channel_id=1, source_target_pairs={{8,0},{16,8},{24,16},{28,24},{20,28},{12,20},{4,12},{0,4},{9,1},{1... | collective-permute-start | bytes 2359304 | tf_op jit(solution)/shard_map/ppermute | solution.py:767
  495.6 18.0 %collective-permute-start.51 = (bf16[192,2048]{1,0:T(8,128)(2,1)S(1)}, bf16[192,2048]{1,0:T(8,128)(2,1)S(1)}, u32[]{:S(2)}, u32[]{:S(2)}) collective-permute-start(bf16[192,2048]{1,0:T(8,128)(2,1)S(1)} %collective-permute-done.43.one), channel_id=1, source_target_pairs={{0,8},{8,16},{16,24},{24,28},{28,20},{20,12},{12,4},{4,0},{1,9},{9... | collective-permute-start | bytes 2359304 | tf_op jit(solution)/shard_map/ppermute | solution.py:767
  495.6 19.6 %collective-permute-start.52 = (bf16[192,2048]{1,0:T(8,128)(2,1)S(1)}, bf16[192,2048]{1,0:T(8,128)(2,1)S(1)}, u32[]{:S(2)}, u32[]{:S(2)}) collective-permute-start(bf16[192,2048]{1,0:T(8,128)(2,1)S(1)} %collective-permute-done.44.two), channel_id=1, source_target_pairs={{8,0},{16,8},{24,16},{28,24},{20,28},{12,20},{4,12},{0,4},{9,1},{1... | collective-permute-start | bytes 2359304 | tf_op jit(solution)/shard_map/ppermute | solution.py:767
  497.7 24.3 %collective-permute-start.48 = (f32[26,1024]{1,0:T(8,128)S(1)}, f32[26,1024]{1,0:T(8,128)S(1)}, u32[]{:S(2)}, u32[]{:S(2)}) collective-permute-start(f32[26,1024]{1,0:T(8,128)S(1)} %fusion.53), channel_id=1, source_target_pairs={{0,8},{4,12},{8,0},{12,4},{16,24},{20,28},{24,16},{28,20},{1,9},{5... | collective-permute-start | bytes 319496 | tf_op jit(solution)/shard_map/ppermute | solution.py:1090
  497.7 25.6 %collective-permute-start.49 = (f32[26,1024]{1,0:T(8,128)S(1)}, f32[26,1024]{1,0:T(8,128)S(1)}, u32[]{:S(2)}, u32[]{:S(2)}) collective-permute-start(f32[26,1024]{1,0:T(8,128)S(1)} %fusion.53), channel_id=1, source_target_pairs={{0,16},{4,20},{8,24},{12,28},{16,0},{20,4},{24,8},{28,12},{1,17},{... | collective-permute-start | bytes 319496 | tf_op jit(solution)/shard_map/ppermute | solution.py:1090
  498.3 25.0 %collective-permute-start.50 = (f32[26,1024]{1,0:T(8,128)S(1)}, f32[26,1024]{1,0:T(8,128)S(1)}, u32[]{:S(2)}, u32[]{:S(2)}) collective-permute-start(f32[26,1024]{1,0:T(8,128)S(1)} %fusion.53), channel_id=1, source_target_pairs={{0,24},{4,28},{8,16},{12,20},{16,8},{20,12},{24,0},{28,4},{1,25},{... | collective-permute-start | bytes 319496 | tf_op jit(solution)/shard_map/ppermute | solution.py:1090
  519.1 20.3 %collective-permute-start.54 = (bf16[192,2048]{1,0:T(8,128)(2,1)S(1)}, bf16[192,2048]{1,0:T(8,128)(2,1)S(1)}, u32[]{:S(2)}, u32[]{:S(2)}) collective-permute-start(bf16[192,2048]{1,0:T(8,128)(2,1)S(1)} %collective-permute-done.51.one), channel_id=1, source_target_pairs={{0,8},{8,16},{16,24},{24,28},{28,20},{20,12},{12,4},{4,0},{1,9},{9... | collective-permute-start | bytes 2359304 | tf_op jit(solution)/shard_map/ppermute | solution.py:767
  521.9 19.7 %collective-permute-start.55 = (bf16[192,2048]{1,0:T(8,128)(2,1)S(1)}, bf16[192,2048]{1,0:T(8,128)(2,1)S(1)}, u32[]{:S(2)}, u32[]{:S(2)}) collective-permute-start(bf16[192,2048]{1,0:T(8,128)(2,1)S(1)} %collective-permute-done.52.two), channel_id=1, source_target_pairs={{8,0},{16,8},{24,16},{28,24},{20,28},{12,20},{4,12},{0,4},{9,1},{1... | collective-permute-start | bytes 2359304 | tf_op jit(solution)/shard_map/ppermute | solution.py:767
  524.0 18.4 %collective-permute-start.53 = (f32[26,1024]{1,0:T(8,128)}, f32[26,1024]{1,0:T(8,128)}, u32[]{:S(2)}, u32[]{:S(2)}) collective-permute-start(f32[26,1024]{1,0:T(8,128)} %add_add_fusion), channel_id=1, source_target_pairs={{0,4},{4,0},{8,12},{12,8},{16,20},{20,16},{24,28},{28,24},{1,5},{5... | collective-permute-start | bytes 319496 | tf_op jit(solution)/shard_map/ppermute | solution.py:1090
  (81 other events, 772.2 us)

commit v5 on v4

--- a/solution.py
+++ b/solution.py
@@ -1176,7 +1176,7 @@
         for filler in fillers:
             filler(lambda values: values)
     finish_small = together(small_dp[1][1], small_outputs)
-    finish_small((lambda values: after(values, *last)) if ringed else (lambda values: values))
+    finish_small((lambda values: after(values, *last, sums[0])) if ringed else (lambda values: values))
     gain, kernel_grad, offset_grad, shared_kernel_grad, shared_offset_grad, bias_grad, rate_grad, skip_grad, gate_gain_grad = made[
         "outputs"
     ]

time: 556 us -> 555 us (level)
  transfers between devices with their start and end apart: 59 -> 59, of which waited for: 26 -> 25; matrix products, arithmetic and copies ran while one was open for 30% -> 30% of each run, Pallas kernels for 31% -> 31%
where the time goes in v5:
time: 555 us; the launch traced here: 549 us
  Pallas kernels  192 us (35%)
  matrix products  106 us (19%)
  waiting for transfers between devices  84.4 us (15%)
  starting transfers between devices  65.9 us (12%)
  local copies, waits for them, and re-layouts  51.6 us (9%)
  other arithmetic  47.3 us (9%)
    pallas_call x2, Pallas kernels, scan_backward(): pl.pallas_call(partial(backward_kernel, channels, start), name='scan_back...  68 us
    pallas_call x4, Pallas kernels, fill_rows(): pl.pallas_call(partial(fill_kernel, dims, spans, 1 if second else 0), nam...  63.1 us
    ppermute x28, waiting for transfers between devices, send(): lax.ppermute(values, 'dp', self.pairs[way])  60.4 us
    ppermute x28, starting transfers between devices, send(): lax.ppermute(values, 'dp', self.pairs[way])  37.9 us
    dot_general x4, matrix products, run(): lax.dot_general(low_rows[part], weight_low, NT, preferred_element_type=F32)  31.1 us
    pallas_call x1, Pallas kernels, scan_forward(): pl.pallas_call(partial(forward_kernel, channels), name='scan_forward', gr...  26.9 us
    unnamed x117, local copies, waits for them, and re-layouts  26.4 us
    dot_general x1, matrix products, body(): lax.dot_general(normed_in, after(low, given), TN, preferred_element_type=...  22.6 us
  transfers between devices with their start and end apart: 59, of which 25 were waited for; matrix products, arithmetic and copies ran while one was open for 30% of the time, Pallas kernels for 31%

profile of v5, /device:TPU:0, one launch (start us, length us, event | category | flops | bytes accessed | tf_op | source)
XLA Modules:
  0.0 549.4 jit_solution(2924549074137426448)
XLA Ops:
  24.0 10.8 %fill_rows.5 = (bf16[2048,1024]{1,0:T(8,128)(2,1)}, bf16[2048,2048]{1,0:T(8,128)(2,1)}) custom-call(bf16[512,2048]{1,0:T(8,128)(2,1)} %pad_maximum_fusion.1.own, bf16[512,2048]{1,0:T(8,128)(2,1)} %collective-permute-done.2.other, bf16[1024,2048]{1,0:T(8,128)(2,1)} %rest_0_.7), custom_call_target="tpu_custom_call" | custom-call | flops 4294967296 | bytes 6291456 | tf_op jit(solution)/shard_map/fill_rows/pallas_call | solution.py:378
  34.9 20.9 %fill_rows.4 = (f32[2048,2560]{1,0:T(8,128)}, bf16[2048,2048]{1,0:T(8,128)(2,1)}) custom-call(bf16[512,2048]{1,0:T(8,128)(2,1)} %fusion.3.own, bf16[512,2048]{1,0:T(8,128)(2,1)} %collective-permute-done.1.other, bf16[2048,1024]{1,0:T(8,128)(2,1)} %rest_0_.6, bf16[2048,1024]{1,0:T(8,128)(2,1)} %rest_1_.3, bf16[2048,512]{1,0:T(8,128)(2,1)} %maximum_maximum_fusion.rest_2_), custom_call_target="tpu_custom_call" | custom-call | flops 10737418240 | bytes 9437184 | tf_op jit(solution)/shard_map/fill_rows/pallas_call | solution.py:378
  64.3 20.9 %fill_rows.6 = (f32[2048,2560]{1,0:T(8,128)}, bf16[2048,2048]{1,0:T(8,128)(2,1)}) custom-call(bf16[512,2048]{1,0:T(8,128)(2,1)} %collective-permute-done.own, bf16[512,2048]{1,0:T(8,128)(2,1)} %collective-permute-done.3.other, bf16[2048,1024]{1,0:T(8,128)(2,1)} %rest_0_.6, bf16[2048,1024]{1,0:T(8,128)(2,1)} %rest_1_.3, ...), custom_call_target="tpu_custom_call", output_to_operand_aliasing={{0}: (5, {}), {1}: (6, {})} | custom-call | flops 10737418240 | bytes 9437184 | tf_op jit(solution)/shard_map/fill_rows/pallas_call | solution.py:378
  85.2 26.9 %scan_forward.1 = (f32[2048,1024]{1,0:T(8,128)}, bf16[2048,1024]{1,0:T(8,128)(2,1)}, bf16[2,4,128,1024]{3,2,1,0:T(8,128)(2,1)}, f32[1,2048]{1,0:T(1,128)}) custom-call(s32[4]{0:T(128)} %get-tuple-element.433.slots, s32[2,1024]{1,0:T(2,128)} %seg_sm.5, s32[2,2]{1,0:T(2,128)} %span_sm.5, f32[2048,2560]{1,0:T(8,128)} %get-tuple-element.191.pre.halo, ...), custom_call_target="tpu_custom_call" | custom-call | flops 20000000000 | bytes 40000000 | tf_op jit(solution)/shard_map/scan_forward/pallas_call | solution.py:411
  112.4 3.9 collective-permute-done.5.other
  117.7 10.5 %fill_rows.7 = (bf16[2048,1024]{1,0:T(8,128)(2,1)}, bf16[2048,2048]{1,0:T(8,128)(2,1)}) custom-call(bf16[512,2048]{1,0:T(8,128)(2,1)} %copy-done.23, bf16[512,2048]{1,0:T(8,128)(2,1)} %copy-done.24, bf16[1024,2048]{1,0:T(8,128)(2,1)} %rest_0_.7, bf16[2048,1024]{1,0:T(8,128)(2,1)} %get-tuple-element.187.rest_1_, ...), custom_call_target="tpu_custom_call", output_to_operand_aliasing={{0}: (3, {}), {1}: (4, {})} | custom-call | flops 4294967296 | bytes 6291456 | tf_op jit(solution)/shard_map/fill_rows/pallas_call | solution.py:378
  148.4 9.9 %fusion.81 = bf16[512,2048]{1,0:T(8,128)(2,1)} fusion(bf16[2048,512]{1,0:T(8,128)(2,1)S(1)} %get-tuple-element.201, bf16[2048,2048]{1,0:T(8,128)(2,1)} %get-tuple-element.202), kind=kOutput, calls=%fused_computation.167 | convolution fusion | flops 4294967296 | bytes 12582912 | tf_op jit(solution)/shard_map/dot_general | solution.py:934
  159.8 5.8 %fusion.82.mine = bf16[512,2048]{1,0:T(8,128)(2,1)} fusion(bf16[2048,512]{1,0:T(8,128)(2,1)S(1)} %get-tuple-element.203, bf16[2048,2048]{1,0:T(8,128)(2,1)S(1)} %bitcast.163), kind=kOutput, calls=%fused_computation.168 | convolution fusion | flops 4294967296 | bytes 12582912 | tf_op jit(solution)/shard_map/dot_general | solution.py:934
  165.6 34.1 %scan_backward.2 = (bf16[2048,2048]{1,0:T(8,128)(2,1)}, bf16[2048,256]{1,0:T(8,128)(2,1)}, bf16[2048,128]{1,0:T(8,128)(2,1)}, f32[8,1024]{1,0:T(8,128)}, f32[8,128]{1,0:T(8,128)}, /*index=5*/f32[8,256]{1,0:T(8,128)}) custom-call(s32[4]{0:T(128)} %get-tuple-element.433.slots, s32[2,1024]{1,0:T(2,128)} %seg_sm.5, s32[2,2]{1,0:T(2,128)} %span_sm.5, ...), custom_call_target="tpu_custom_call" | custom-call | flops 22000001024 | bytes 30000000 | tf_op jit(solution)/shard_map/scan_backward/pallas_call | solution.py:552
  199.7 9.4 %fusion.83 = bf16[1024,2048]{1,0:T(8,128)(2,1)} fusion(bf16[1024,1024]{1,0:T(8,128)(2,1)} %copy-done.11, bf16[1024,2048]{1,0:T(8,128)(2,1)} %rest_0_.7), kind=kOutput, calls=%fused_computation.169 | convolution fusion | flops 4294967296 | bytes 10485760 | tf_op jit(solution)/shard_map/dot_general | solution.py:949
  213.4 34.0 %scan_backward.3 = (bf16[2048,2048]{1,0:T(8,128)(2,1)}, bf16[2048,256]{1,0:T(8,128)(2,1)}, bf16[2048,128]{1,0:T(8,128)(2,1)}, f32[8,1024]{1,0:T(8,128)}, f32[8,128]{1,0:T(8,128)}, /*index=5*/f32[8,256]{1,0:T(8,128)}) custom-call(s32[4]{0:T(128)} %get-tuple-element.433.slots, ...), custom_call_target="tpu_custom_call", output_to_operand_aliasing={{0}: (20, {}), {1}: (21, {}), {2}: (22, {})} | custom-call | flops 22000001024 | bytes 30000000 | tf_op jit(solution)/shard_map/scan_backward/pallas_call | solution.py:552
  251.1 22.6 %fusion.84.one.two = bf16[2048,2048]{1,0:T(8,128)(2,1)S(1)} fusion(bf16[2048,2048]{1,0:T(8,128)(2,1)} %get-tuple-element.190, bf16[2048,2048]{1,0:T(8,128)(2,1)} %get-tuple-element.275), kind=kOutput, calls=%fused_computation.170 | convolution fusion | flops 17179869184 | bytes 25165824 | tf_op jit(solution)/shard_map/dot_general | solution.py:955
  281.4 4.7 dynamic-slice_bitcast_fusion.7
  298.1 6.1 %fusion.85 = bf16[1024,2048]{1,0:T(8,128)(2,1)} fusion(bf16[1024,1024]{1,0:T(8,128)(2,1)S(1)} %copy-done.10, bf16[1024,2048]{1,0:T(8,128)(2,1)S(1)} %copy-done.20), kind=kOutput, calls=%fused_computation.171 | convolution fusion | flops 4294967296 | bytes 10485760 | tf_op jit(solution)/shard_map/dot_general | solution.py:1031
  315.7 5.1 fusion.50
  324.9 8.0 %fusion.22 = f32[512,2048]{1,0:T(8,128)S(1)} fusion(bf16[2048,2048]{1,0:T(8,128)(2,1)} %copy-done.25, bf16[2048,2048]{1,0:T(8,128)(2,1)} %get-tuple-element.275), kind=kOutput, calls=%fused_computation.42 | convolution fusion | flops 4294967296 | bytes 14680064 | tf_op jit(solution)/shard_map/dot_general | solution.py:1010
  339.5 7.6 %fusion.20 = f32[512,2048]{1,0:T(8,128)S(1)} fusion(bf16[2048,2048]{1,0:T(8,128)(2,1)} %copy-done.25, bf16[2048,2048]{1,0:T(8,128)(2,1)} %get-tuple-element.275), kind=kOutput, calls=%fused_computation.40 | convolution fusion | flops 4294967296 | bytes 14680064 | tf_op jit(solution)/shard_map/dot_general | solution.py:1010
  355.8 7.6 %fusion.18 = f32[512,2048]{1,0:T(8,128)S(1)} fusion(bf16[2048,2048]{1,0:T(8,128)(2,1)} %copy-done.25, bf16[2048,2048]{1,0:T(8,128)(2,1)} %get-tuple-element.275), kind=kOutput, calls=%fused_computation.38 | convolution fusion | flops 4294967296 | bytes 14680064 | tf_op jit(solution)/shard_map/dot_general | solution.py:1010
  370.4 7.8 %fusion.16 = f32[512,2048]{1,0:T(8,128)S(1)} fusion(bf16[2048,2048]{1,0:T(8,128)(2,1)} %copy-done.25, bf16[2048,2048]{1,0:T(8,128)(2,1)} %get-tuple-element.275), kind=kOutput, calls=%fused_computation.36 | convolution fusion | flops 4294967296 | bytes 14680064 | tf_op jit(solution)/shard_map/dot_general | solution.py:1010
  391.8 11.7 %collective-permute-done.29.one = bf16[192,2048]{1,0:T(8,128)(2,1)S(1)} collective-permute-done((bf16[192,2048]{1,0:T(8,128)(2,1)S(1)}, bf16[192,2048]{1,0:T(8,128)(2,1)S(1)}, u32[]{:S(2)}, u32[]{:S(2)}) %collective-permute-start.29) | collective-permute-done | bytes 786464 | tf_op jit(solution)/shard_map/ppermute | solution.py:767
  409.1 3.7 fusion.14
  412.8 9.5 %collective-permute-done.32.one = bf16[192,2048]{1,0:T(8,128)(2,1)S(1)} collective-permute-done((bf16[192,2048]{1,0:T(8,128)(2,1)S(1)}, bf16[192,2048]{1,0:T(8,128)(2,1)S(1)}, u32[]{:S(2)}, u32[]{:S(2)}) %collective-permute-start.32) | collective-permute-done | bytes 786464 | tf_op jit(solution)/shard_map/ppermute | solution.py:767
  423.6 8.6 %collective-permute-start.35 = (bf16[192,2048]{1,0:T(8,128)(2,1)S(1)}, bf16[192,2048]{1,0:T(8,128)(2,1)S(1)}, u32[]{:S(2)}, u32[]{:S(2)}) collective-permute-start(bf16[192,2048]{1,0:T(8,128)(2,1)S(1)} %collective-permute-done.32.one), channel_id=1, source_target_pairs={{0,8},{8,16},{16,24},{24,28},{28,20},{20,12},{12,4},{4,0},{1,9},{9... | collective-permute-start | bytes 2359304 | tf_op jit(solution)/shard_map/ppermute | solution.py:767
  432.2 6.3 %collective-permute-done.39 = bf16[80,2048]{1,0:T(8,128)(2,1)S(1)} collective-permute-done((bf16[80,2048]{1,0:T(8,128)(2,1)S(1)}, bf16[80,2048]{1,0:T(8,128)(2,1)S(1)}, u32[]{:S(2)}, u32[]{:S(2)}) %collective-permute-start.39) | collective-permute-done | bytes 327712 | tf_op jit(solution)/shard_map/ppermute | solution.py:1090
  442.6 4.1 fusion.9
  446.8 8.6 %fusion.7 = bf16[2,256,2048]{2,1,0:T(8,128)(2,1)} fusion(bf16[2,256,2048]{2,1,0:T(8,128)(2,1)S(1)} %bitcast.158, bf16[2,256,2048]{2,1,0:T(8,128)(2,1)} %bitcast.66, f32[2,256]{1,0:T(2,128)S(1)} %fusion.74, f32[2048]{0:T(1024)S(1)} %copy-done.39, f32[2,256]{1,0:T(2,128)S(1)} %rsqrt.20, bf16[2,256,2048]{2,1,0:T(8,128)(2,1)} %collective-permute-done.38, ...), kind=kOutput, calls=%fused_computation.12 | output fusion | flops 23071232 | bytes 12595200 | tf_op jit(solution)/shard_map/mul | solution.py:1052
  473.4 6.0 %collective-permute-done.46 = f32[10,1024]{1,0:T(8,128)S(1)} collective-permute-done((f32[10,1024]{1,0:T(8,128)S(1)}, f32[10,1024]{1,0:T(8,128)S(1)}, u32[]{:S(2)}, u32[]{:S(2)}) %collective-permute-start.46) | collective-permute-done | bytes 40992 | tf_op jit(solution)/shard_map/ppermute | solution.py:1090
  481.1 4.0 fusion.12
  487.5 5.5 collective-permute-done.43.one
  498.3 3.8 collective-permute-start.50
  503.2 10.5 %collective-permute-done.51.one = bf16[192,2048]{1,0:T(8,128)(2,1)S(1)} collective-permute-done((bf16[192,2048]{1,0:T(8,128)(2,1)S(1)}, bf16[192,2048]{1,0:T(8,128)(2,1)S(1)}, u32[]{:S(2)}, u32[]{:S(2)}) %collective-permute-start.51) | collective-permute-done | bytes 786464 | tf_op jit(solution)/shard_map/ppermute | solution.py:767
  535.5 4.0 collective-permute-done.54.one
  (335 shorter events, 204.4 us)
Async XLA Ops:
  5.8 18.2 %collective-permute-start.2 = (bf16[512,2048]{1,0:T(8,128)(2,1)}, bf16[512,2048]{1,0:T(8,128)(2,1)}, u32[]{:S(2)}, u32[]{:S(2)}) collective-permute-start(bf16[512,2048]{1,0:T(8,128)(2,1)} %pad_maximum_fusion.1.own), channel_id=1, source_target_pairs={{0,1},{1,0},{2,3},{3,2},{4,5},{5,4},{6,7},{7,6},{8,9},{9,8},{10,11... | collective-permute-start | bytes 6291464 | tf_op jit(solution)/shard_map/ppermute | solution.py:805
  9.7 25.2 %collective-permute-start.1 = (bf16[512,2048]{1,0:T(8,128)(2,1)}, bf16[512,2048]{1,0:T(8,128)(2,1)}, u32[]{:S(2)}, u32[]{:S(2)}) collective-permute-start(bf16[512,2048]{1,0:T(8,128)(2,1)} %fusion.3.own), channel_id=1, source_target_pairs={{0,1},{1,0},{2,3},{3,2},{4,5},{5,4},{6,7},{7,6},{8,9},{9,8},{10,11... | collective-permute-start | bytes 6291464 | tf_op jit(solution)/shard_map/ppermute | solution.py:805
  9.8 49.1 %collective-permute-start = (bf16[512,2048]{1,0:T(8,128)(2,1)}, bf16[512,2048]{1,0:T(8,128)(2,1)}, u32[]{:S(2)}, u32[]{:S(2)}) collective-permute-start(bf16[512,2048]{1,0:T(8,128)(2,1)} %fusion.3.own), channel_id=1, source_target_pairs={{0,2},{1,3},{2,0},{3,1},{4,6},{5,7},{6,4},{7,5},{8,10},{9,11},{10,... | collective-permute-start | bytes 6291464 | tf_op jit(solution)/shard_map/ppermute | solution.py:808
  58.9 53.3 %collective-permute-start.4 = (bf16[512,2048]{1,0:T(8,128)(2,1)}, bf16[512,2048]{1,0:T(8,128)(2,1)S(1)}, u32[]{:S(2)}, u32[]{:S(2)}) collective-permute-start(bf16[512,2048]{1,0:T(8,128)(2,1)} %pad_maximum_fusion.1.own), channel_id=1, source_target_pairs={{0,2},{1,3},{2,0},{3,1},{4,6},{5,7},{6,4},{7,5},{8,10},{9,11},{10,... | collective-permute-start | bytes 6291464 | tf_op jit(solution)/shard_map/ppermute | solution.py:808
  158.3 50.8 %collective-permute-start.8 = (bf16[512,2048]{1,0:T(8,128)(2,1)}, bf16[512,2048]{1,0:T(8,128)(2,1)S(1)}, u32[]{:S(2)}, u32[]{:S(2)}) collective-permute-start(bf16[512,2048]{1,0:T(8,128)(2,1)} %fusion.81), channel_id=1, source_target_pairs={{0,4},{4,0},{8,12},{12,8},{16,20},{20,16},{24,28},{28,24},{1,5},{5... | collective-permute-start | bytes 6291464 | tf_op jit(solution)/shard_map/ppermute | solution.py:665
  211.8 35.6 %collective-permute-start.9 = (bf16[256,2048]{1,0:T(8,128)(2,1)}, bf16[256,2048]{1,0:T(8,128)(2,1)S(1)}, u32[]{:S(2)}, u32[]{:S(2)}) collective-permute-start(bf16[256,2048]{1,0:T(8,128)(2,1)} %get-tuple-element.209), channel_id=1, source_target_pairs={{0,8},{4,12},{8,0},{12,4},{16,24},{20,28},{24,16},{28,20},{1,9},{5... | collective-permute-start | bytes 3145736 | tf_op jit(solution)/shard_map/ppermute | solution.py:665
  248.5 25.2 %collective-permute-start.10 = (bf16[128,2048]{1,0:T(8,128)(2,1)S(1)}, bf16[128,2048]{1,0:T(8,128)(2,1)}, u32[]{:S(2)}, u32[]{:S(2)}) collective-permute-start(bf16[128,2048]{1,0:T(8,128)(2,1)S(1)} %get-tuple-element.219), channel_id=1, source_target_pairs={{0,16},{4,20},{8,24},{12,28},{16,0},{20,4},{24,8},{28,12},{1,17},{... | collective-permute-start | bytes 1572872 | tf_op jit(solution)/shard_map/ppermute | solution.py:665
  288.2 120.0 %collective-permute-start.34 = (bf16[2,2,256,2048]{3,2,1,0:T(8,128)(2,1)}, bf16[2,2,256,2048]{3,2,1,0:T(8,128)(2,1)}, u32[]{:S(2)}, u32[]{:S(2)}) collective-permute-start(bf16[2,2,256,2048]{3,2,1,0:T(8,128)(2,1)} %bitcast.185), channel_id=1, source_target_pairs={{0,1},{1,0},{2,3},{3,2},{4,5},{5,4},{6,7},{7,6},{8,9},{9,8},{10,11... | collective-permute-start | bytes 12582920 | tf_op jit(solution)/shard_map/ppermute | solution.py:805
  347.3 31.7 %collective-permute-start.28 = (bf16[80,2048]{1,0:T(8,128)(2,1)S(1)}, bf16[80,2048]{1,0:T(8,128)(2,1)}, u32[]{:S(2)}, u32[]{:S(2)}) collective-permute-start(bf16[80,2048]{1,0:T(8,128)(2,1)S(1)} %add_convert_fusion.10), channel_id=1, source_target_pairs={{0,8},{4,12},{8,0},{12,4},{16,24},{20,28},{24,16},{28,20},{1,9},{5... | collective-permute-start | bytes 983048 | tf_op jit(solution)/shard_map/ppermute | solution.py:1090
  350.8 31.3 %collective-permute-start.31 = (bf16[2,256,2048]{2,1,0:T(8,128)(2,1)}, bf16[2,256,2048]{2,1,0:T(8,128)(2,1)S(1)}, u32[]{:S(2)}, u32[]{:S(2)}) collective-permute-start(bf16[2,256,2048]{2,1,0:T(8,128)(2,1)} %bitcast.32), channel_id=1, source_target_pairs={{0,1},{1,0},{2,3},{3,2},{4,5},{5,4},{6,7},{7,6},{8,9},{9,8},{10,11... | collective-permute-start | bytes 6291464 | tf_op jit(solution)/shard_map/ppermute | solution.py:805
  379.0 63.6 %collective-permute-start.37 = (bf16[2,256,2048]{2,1,0:T(8,128)(2,1)}, bf16[2,256,2048]{2,1,0:T(8,128)(2,1)}, u32[]{:S(2)}, u32[]{:S(2)}) collective-permute-start(bf16[2,256,2048]{2,1,0:T(8,128)(2,1)} %bitcast.37), channel_id=1, source_target_pairs={{0,1},{1,0},{2,3},{3,2},{4,5},{5,4},{6,7},{7,6},{8,9},{9,8},{10,11... | collective-permute-start | bytes 6291464 | tf_op jit(solution)/shard_map/ppermute | solution.py:805
  384.3 58.3 %collective-permute-start.38 = (bf16[2,256,2048]{2,1,0:T(8,128)(2,1)}, bf16[2,256,2048]{2,1,0:T(8,128)(2,1)}, u32[]{:S(2)}, u32[]{:S(2)}) collective-permute-start(bf16[2,256,2048]{2,1,0:T(8,128)(2,1)} %add_convert_fusion.1), channel_id=1, source_target_pairs={{0,2},{1,3},{2,0},{3,1},{4,6},{5,7},{6,4},{7,5},{8,10},{9,11},{10,... | collective-permute-start | bytes 6291464 | tf_op jit(solution)/shard_map/ppermute | solution.py:808
  385.0 18.5 %collective-permute-start.29 = (bf16[192,2048]{1,0:T(8,128)(2,1)S(1)}, bf16[192,2048]{1,0:T(8,128)(2,1)S(1)}, u32[]{:S(2)}, u32[]{:S(2)}) collective-permute-start(bf16[192,2048]{1,0:T(8,128)(2,1)S(1)} %get-tuple-element.278.one), channel_id=1, source_target_pairs={{0,8},{8,16},{16,24},{24,28},{28,20},{20,12},{12,4},{4,0},{1,9},{9... | collective-permute-start | bytes 2359304 | tf_op jit(solution)/shard_map/ppermute | solution.py:767
  386.2 17.6 %collective-permute-start.30 = (bf16[192,2048]{1,0:T(8,128)(2,1)S(1)}, bf16[192,2048]{1,0:T(8,128)(2,1)S(1)}, u32[]{:S(2)}, u32[]{:S(2)}) collective-permute-start(bf16[192,2048]{1,0:T(8,128)(2,1)S(1)} %get-tuple-element.279.two), channel_id=1, source_target_pairs={{8,0},{16,8},{24,16},{28,24},{20,28},{12,20},{4,12},{0,4},{9,1},{1... | collective-permute-start | bytes 2359304 | tf_op jit(solution)/shard_map/ppermute | solution.py:767
  403.8 18.6 %collective-permute-start.32 = (bf16[192,2048]{1,0:T(8,128)(2,1)S(1)}, bf16[192,2048]{1,0:T(8,128)(2,1)S(1)}, u32[]{:S(2)}, u32[]{:S(2)}) collective-permute-start(bf16[192,2048]{1,0:T(8,128)(2,1)S(1)} %collective-permute-done.29.one), channel_id=1, source_target_pairs={{0,8},{8,16},{16,24},{24,28},{28,20},{20,12},{12,4},{4,0},{1,9},{9... | collective-permute-start | bytes 2359304 | tf_op jit(solution)/shard_map/ppermute | solution.py:767
  404.4 19.3 %collective-permute-start.33 = (bf16[192,2048]{1,0:T(8,128)(2,1)S(1)}, bf16[192,2048]{1,0:T(8,128)(2,1)S(1)}, u32[]{:S(2)}, u32[]{:S(2)}) collective-permute-start(bf16[192,2048]{1,0:T(8,128)(2,1)S(1)} %collective-permute-done.30.two), channel_id=1, source_target_pairs={{8,0},{16,8},{24,16},{28,24},{20,28},{12,20},{4,12},{0,4},{9,1},{1... | collective-permute-start | bytes 2359304 | tf_op jit(solution)/shard_map/ppermute | solution.py:767
  408.2 30.3 %collective-permute-start.39 = (bf16[80,2048]{1,0:T(8,128)(2,1)S(1)}, bf16[80,2048]{1,0:T(8,128)(2,1)S(1)}, u32[]{:S(2)}, u32[]{:S(2)}) collective-permute-start(bf16[80,2048]{1,0:T(8,128)(2,1)S(1)} %add_convert_fusion.9), channel_id=1, source_target_pairs={{0,16},{4,20},{8,24},{12,28},{16,0},{20,4},{24,8},{28,12},{1,17},{... | collective-permute-start | bytes 983048 | tf_op jit(solution)/shard_map/ppermute | solution.py:1090
  422.4 58.7 %collective-permute-start.42 = (bf16[2,256,2048]{2,1,0:T(8,128)(2,1)}, bf16[2,256,2048]{2,1,0:T(8,128)(2,1)}, u32[]{:S(2)}, u32[]{:S(2)}) collective-permute-start(bf16[2,256,2048]{2,1,0:T(8,128)(2,1)} %fusion.14), channel_id=1, source_target_pairs={{0,2},{1,3},{2,0},{3,1},{4,6},{5,7},{6,4},{7,5},{8,10},{9,11},{10,... | collective-permute-start | bytes 6291464 | tf_op jit(solution)/shard_map/ppermute | solution.py:808
  423.6 31.8 %collective-permute-start.35 = (bf16[192,2048]{1,0:T(8,128)(2,1)S(1)}, bf16[192,2048]{1,0:T(8,128)(2,1)S(1)}, u32[]{:S(2)}, u32[]{:S(2)}) collective-permute-start(bf16[192,2048]{1,0:T(8,128)(2,1)S(1)} %collective-permute-done.32.one), channel_id=1, source_target_pairs={{0,8},{8,16},{16,24},{24,28},{28,20},{20,12},{12,4},{4,0},{1,9},{9... | collective-permute-start | bytes 2359304 | tf_op jit(solution)/shard_map/ppermute | solution.py:767
  438.5 16.9 %collective-permute-start.36 = (bf16[192,2048]{1,0:T(8,128)(2,1)S(1)}, bf16[192,2048]{1,0:T(8,128)(2,1)S(1)}, u32[]{:S(2)}, u32[]{:S(2)}) collective-permute-start(bf16[192,2048]{1,0:T(8,128)(2,1)S(1)} %collective-permute-done.33.two), channel_id=1, source_target_pairs={{8,0},{16,8},{24,16},{28,24},{20,28},{12,20},{4,12},{0,4},{9,1},{1... | collective-permute-start | bytes 2359304 | tf_op jit(solution)/shard_map/ppermute | solution.py:767
  459.3 20.1 %collective-permute-start.46 = (f32[10,1024]{1,0:T(8,128)S(1)}, f32[10,1024]{1,0:T(8,128)S(1)}, u32[]{:S(2)}, u32[]{:S(2)}) collective-permute-start(f32[10,1024]{1,0:T(8,128)S(1)} %select_maximum_fusion.1), channel_id=1, source_target_pairs={{0,2},{1,3},{2,0},{3,1},{4,6},{5,7},{6,4},{7,5},{8,10},{9,11},{10,... | collective-permute-start | bytes 122888 | tf_op jit(solution)/shard_map/ppermute | solution.py:1090
  471.7 26.6 %collective-permute-start.56 = (bf16[64,2048]{1,0:T(8,128)(2,1)S(1)}, bf16[64,2048]{1,0:T(8,128)(2,1)S(1)}, u32[]{:S(2)}, u32[]{:S(2)}) collective-permute-start(bf16[64,2048]{1,0:T(8,128)(2,1)S(1)} %slice.194), channel_id=1, source_target_pairs={{0,2},{1,3},{2,0},{3,1},{4,6},{5,7},{6,4},{7,5},{8,10},{9,11},{10,... | collective-permute-start | bytes 786440 | tf_op jit(solution)/shard_map/ppermute | solution.py:808
  473.0 20.0 %collective-permute-start.43 = (bf16[192,2048]{1,0:T(8,128)(2,1)S(1)}, bf16[192,2048]{1,0:T(8,128)(2,1)S(1)}, u32[]{:S(2)}, u32[]{:S(2)}) collective-permute-start(bf16[192,2048]{1,0:T(8,128)(2,1)S(1)} %collective-permute-done.40.one), channel_id=1, source_target_pairs={{0,8},{8,16},{16,24},{24,28},{28,20},{20,12},{12,4},{4,0},{1,9},{9... | collective-permute-start | bytes 2359304 | tf_op jit(solution)/shard_map/ppermute | solution.py:767
  479.4 16.2 %collective-permute-start.44 = (bf16[192,2048]{1,0:T(8,128)(2,1)S(1)}, bf16[192,2048]{1,0:T(8,128)(2,1)S(1)}, u32[]{:S(2)}, u32[]{:S(2)}) collective-permute-start(bf16[192,2048]{1,0:T(8,128)(2,1)S(1)} %collective-permute-done.41.two), channel_id=1, source_target_pairs={{8,0},{16,8},{24,16},{28,24},{20,28},{12,20},{4,12},{0,4},{9,1},{1... | collective-permute-start | bytes 2359304 | tf_op jit(solution)/shard_map/ppermute | solution.py:767
  495.6 18.0 %collective-permute-start.51 = (bf16[192,2048]{1,0:T(8,128)(2,1)S(1)}, bf16[192,2048]{1,0:T(8,128)(2,1)S(1)}, u32[]{:S(2)}, u32[]{:S(2)}) collective-permute-start(bf16[192,2048]{1,0:T(8,128)(2,1)S(1)} %collective-permute-done.43.one), channel_id=1, source_target_pairs={{0,8},{8,16},{16,24},{24,28},{28,20},{20,12},{12,4},{4,0},{1,9},{9... | collective-permute-start | bytes 2359304 | tf_op jit(solution)/shard_map/ppermute | solution.py:767
  495.6 19.6 %collective-permute-start.52 = (bf16[192,2048]{1,0:T(8,128)(2,1)S(1)}, bf16[192,2048]{1,0:T(8,128)(2,1)S(1)}, u32[]{:S(2)}, u32[]{:S(2)}) collective-permute-start(bf16[192,2048]{1,0:T(8,128)(2,1)S(1)} %collective-permute-done.44.two), channel_id=1, source_target_pairs={{8,0},{16,8},{24,16},{28,24},{20,28},{12,20},{4,12},{0,4},{9,1},{1... | collective-permute-start | bytes 2359304 | tf_op jit(solution)/shard_map/ppermute | solution.py:767
  497.7 24.3 %collective-permute-start.48 = (f32[26,1024]{1,0:T(8,128)S(1)}, f32[26,1024]{1,0:T(8,128)S(1)}, u32[]{:S(2)}, u32[]{:S(2)}) collective-permute-start(f32[26,1024]{1,0:T(8,128)S(1)} %fusion.53), channel_id=1, source_target_pairs={{0,8},{4,12},{8,0},{12,4},{16,24},{20,28},{24,16},{28,20},{1,9},{5... | collective-permute-start | bytes 319496 | tf_op jit(solution)/shard_map/ppermute | solution.py:1090
  497.7 25.6 %collective-permute-start.49 = (f32[26,1024]{1,0:T(8,128)S(1)}, f32[26,1024]{1,0:T(8,128)S(1)}, u32[]{:S(2)}, u32[]{:S(2)}) collective-permute-start(f32[26,1024]{1,0:T(8,128)S(1)} %fusion.53), channel_id=1, source_target_pairs={{0,16},{4,20},{8,24},{12,28},{16,0},{20,4},{24,8},{28,12},{1,17},{... | collective-permute-start | bytes 319496 | tf_op jit(solution)/shard_map/ppermute | solution.py:1090
  498.3 25.0 %collective-permute-start.50 = (f32[26,1024]{1,0:T(8,128)S(1)}, f32[26,1024]{1,0:T(8,128)S(1)}, u32[]{:S(2)}, u32[]{:S(2)}) collective-permute-start(f32[26,1024]{1,0:T(8,128)S(1)} %fusion.53), channel_id=1, source_target_pairs={{0,24},{4,28},{8,16},{12,20},{16,8},{20,12},{24,0},{28,4},{1,25},{... | collective-permute-start | bytes 319496 | tf_op jit(solution)/shard_map/ppermute | solution.py:1090
  519.1 20.3 %collective-permute-start.54 = (bf16[192,2048]{1,0:T(8,128)(2,1)S(1)}, bf16[192,2048]{1,0:T(8,128)(2,1)S(1)}, u32[]{:S(2)}, u32[]{:S(2)}) collective-permute-start(bf16[192,2048]{1,0:T(8,128)(2,1)S(1)} %collective-permute-done.51.one), channel_id=1, source_target_pairs={{0,8},{8,16},{16,24},{24,28},{28,20},{20,12},{12,4},{4,0},{1,9},{9... | collective-permute-start | bytes 2359304 | tf_op jit(solution)/shard_map/ppermute | solution.py:767
  521.9 19.7 %collective-permute-start.55 = (bf16[192,2048]{1,0:T(8,128)(2,1)S(1)}, bf16[192,2048]{1,0:T(8,128)(2,1)S(1)}, u32[]{:S(2)}, u32[]{:S(2)}) collective-permute-start(bf16[192,2048]{1,0:T(8,128)(2,1)S(1)} %collective-permute-done.52.two), channel_id=1, source_target_pairs={{8,0},{16,8},{24,16},{28,24},{20,28},{12,20},{4,12},{0,4},{9,1},{1... | collective-permute-start | bytes 2359304 | tf_op jit(solution)/shard_map/ppermute | solution.py:767
  524.0 20.0 %collective-permute-start.53 = (f32[26,1024]{1,0:T(8,128)}, f32[26,1024]{1,0:T(8,128)}, u32[]{:S(2)}, u32[]{:S(2)}) collective-permute-start(f32[26,1024]{1,0:T(8,128)} %add_add_fusion), channel_id=1, source_target_pairs={{0,4},{4,0},{8,12},{12,8},{16,20},{20,16},{24,28},{28,24},{1,5},{5... | collective-permute-start | bytes 319496 | tf_op jit(solution)/shard_map/ppermute | solution.py:1090
  (81 other events, 772.2 us)
